TPU v7x, 32 devices: a whole 2x2x4 slice. The times are simulated.
32 devices in a mesh: row: 4 (over z), col: 8 (over y, x, core).
Axes of the slice: x: 2, y: 2, z: 4, core: 2. Of those that a mesh axis runs over, the one named last changes fastest.
Arguments:
- tokens: bfloat16 [128, 8192], P('col', 'row'), may hold values from -6 to 6
- cotangent: bfloat16 [128, 8192], P('col', 'row'), may hold values from -6 to 6
- up_weight: bfloat16 [8192, 32768], P('row', 'col'), may hold values from -0.125 to 0.125
- down_weight: bfloat16 [32768, 8192], P('col', 'row'), may hold values from -0.0625 to 0.0625
- block_index: int32 [64, 96], replicated, may hold values from 0 to 256, as said below
Outputs:
- input_grad: bfloat16 [128, 8192], P('col', 'row')
- up_grad: bfloat16 [8192, 32768], P('row', 'col')
- down_grad: bfloat16 [32768, 8192], P('col', 'row')
Inputs may be any that keep to these rules, and one draw needn't show every extreme that they name: `block_index`: row i lists distinct block columns in rising order, then the value 256 as padding up to 96 entries; each row keeps 32 to 96 blocks, and some row keeps exactly 96.
All inputs are finite; a program needn't handle non-finite values.
Results may differ from a plain program's by a relative error of at most 0.005.
Values may be sent and summed in bfloat16 or wider, within the bound.
No kernel may reach another device: no remote copies, remote signals or barrier semaphores. Data moves between devices by JAX's collectives and lax.ppermute only.
A program may use at most 256 MiB of HBM per device.

v0:
```python
import jax
import jax.numpy as jnp
from jax import lax
from jax.sharding import PartitionSpec as P

BLOCK = 128


def tile_mask(block_index, row_blocks, col_blocks):
    row_place = lax.axis_index("row")
    col_place = lax.axis_index("col")
    own_rows = lax.dynamic_slice_in_dim(block_index, row_place * row_blocks, row_blocks, 0)
    own_cols = col_place * col_blocks + jnp.arange(col_blocks, dtype=jnp.int32)
    return jnp.any(own_rows[:, :, None] == own_cols[None, None, :], axis=1)


def finish_hidden(hidden, act_grad):
    activated = jax.nn.gelu(hidden).astype(jnp.bfloat16)
    _, pullback = jax.vjp(jax.nn.gelu, hidden)
    hidden_grad = pullback(act_grad)[0].astype(jnp.bfloat16)
    return (activated, hidden_grad)


def local(tokens, cotangent, up_weight, down_weight, block_index):
    feat_rows, unit_cols = up_weight.shape
    row_blocks = feat_rows // BLOCK
    col_blocks = unit_cols // BLOCK
    block_hits = tile_mask(block_index, row_blocks, col_blocks)
    mask_half = block_hits.astype(jnp.bfloat16)
    mask_full = block_hits.astype(jnp.float32)
    masked_up = (
        up_weight.reshape(row_blocks, BLOCK, col_blocks, BLOCK) * mask_half[:, None, :, None]
    ).reshape(feat_rows, unit_cols)
    masked_down = (
        down_weight.reshape(col_blocks, BLOCK, row_blocks, BLOCK) * mask_half.T[:, None, :, None]
    ).reshape(unit_cols, feat_rows)
    token_all, cotan_all = (
        lax.all_gather(tokens, "col", axis=0, tiled=True),
        lax.all_gather(cotangent, "col", axis=0, tiled=True),
    )
    hidden_part = jnp.dot(token_all, masked_up, preferred_element_type=jnp.float32)
    grad_part = lax.dot_general(
        cotan_all, masked_down, (((1,), (1,)), ((), ())), preferred_element_type=jnp.float32
    )
    hidden, act_grad = (
        lax.psum_scatter(hidden_part, "row", scatter_dimension=0, tiled=True),
        lax.psum_scatter(grad_part, "row", scatter_dimension=0, tiled=True),
    )
    activated, hidden_grad = finish_hidden(hidden, act_grad)
    act_all, hgrad_all = (
        lax.all_gather(activated, "row", axis=0, tiled=True),
        lax.all_gather(hidden_grad, "row", axis=0, tiled=True),
    )
    down_sum = lax.dot_general(
        act_all, cotan_all, (((0,), (0,)), ((), ())), preferred_element_type=jnp.float32
    )
    down_grad = (
        (down_sum.reshape(col_blocks, BLOCK, row_blocks, BLOCK) * mask_full.T[:, None, :, None])
        .reshape(unit_cols, feat_rows)
        .astype(jnp.bfloat16)
    )
    up_sum = lax.dot_general(
        token_all, hgrad_all, (((0,), (0,)), ((), ())), preferred_element_type=jnp.float32
    )
    up_grad = (
        (up_sum.reshape(row_blocks, BLOCK, col_blocks, BLOCK) * mask_full[:, None, :, None])
        .reshape(feat_rows, unit_cols)
        .astype(jnp.bfloat16)
    )
    input_grad = lax.psum_scatter(
        lax.dot_general(
            hgrad_all, masked_up, (((1,), (1,)), ((), ())), preferred_element_type=jnp.float32
        ),
        "col",
        scatter_dimension=0,
        tiled=True,
    )
    return (input_grad.astype(jnp.bfloat16), up_grad, down_grad)


def solution(mesh):
    return jax.shard_map(
        local,
        mesh=mesh,
        in_specs=(P("col", "row"), P("col", "row"), P("row", "col"), P("col", "row"), P()),
        out_specs=(P("col", "row"), P("row", "col"), P("col", "row")),
        check_vma=False,
    )
```

profile of v0, /device:TPU:0, one launch (start us, length us, event | category | flops | bytes accessed | tf_op | source)
XLA Modules:
  0.0 275.2 jit_solution(9096781239344507857)
XLA Ops:
  7.2 0.0 reduce-scatter.10.cloned.1.call-start
  7.2 0.7 copy-done
  7.9 0.4 compare_reduce_fusion
  8.4 0.1 copy.20
  8.5 11.6 %all_gather.12 = bf16[128,2048]{1,0:T(8,128)(2,1)S(1)} all-gather(bf16[16,2048]{1,0:T(8,128)(2,1)} %param.6), channel_id=1, replica_groups=mesh['row'=4,'col'=8] {'col'}, dimensions={0}, use_global_device_ids=true | all-gather | bytes 589824 | tf_op jit(solution)/shard_map/all_gather | solution.py:39
  20.1 6.2 %mul.99 = bf16[32,128,16,128]{3,2,1,0:T(8,128)(2,1)} broadcast(bf16[32,16]{1,0:T(8,128)(2,1)S(1)} %copy.20), dimensions={0,2} | broadcast | bytes 16778240 | tf_op jit(solution)/shard_map/mul | solution.py:35
  26.3 14.0 %fusion.4 = f32[128,4096]{0,1:T(8,128)S(1)} fusion(bf16[128,2048]{1,0:T(8,128)(2,1)S(1)} %all_gather.12, bf16[4096,2048]{1,0:T(8,128)(2,1)} %param.8, bf16[512,8,16,128]{3,2,1,0:T(8,128)(2,1)} %bitcast.50), kind=kOutput, calls=%fused_computation.9 | convolution fusion | flops 2155872256 | bytes 36175872 | tf_op jit(solution)/shard_map/dot_general | solution.py:42
  40.3 1.8 copy.32
  42.1 0.0 reduce-scatter.12.cloned.1.call-start
  42.2 9.5 %all_gather.13 = bf16[128,2048]{1,0:T(8,128)(2,1)S(1)} all-gather(bf16[16,2048]{1,0:T(8,128)(2,1)S(1)} %copy-done.4), channel_id=1, replica_groups=mesh['row'=4,'col'=8] {'col'}, dimensions={0}, use_global_device_ids=true | all-gather | bytes 589824 | tf_op jit(solution)/shard_map/all_gather | solution.py:38
  51.7 6.2 %mul.102 = bf16[16,128,32,128]{3,2,1,0:T(8,128)(2,1)} broadcast(bf16[16,32]{1,0:T(8,128)(2,1)S(1)} %get-tuple-element.19), dimensions={0,2} | broadcast | bytes 16778240 | tf_op jit(solution)/shard_map/mul | solution.py:32
  57.9 14.8 %convolution_bitcast_fusion = f32[128,4096]{0,1:T(8,128)S(1)} fusion(bf16[128,2048]{1,0:T(8,128)(2,1)S(1)} %all_gather.13, bf16[2048,4096]{1,0:T(8,128)(2,1)} %param.7, bf16[256,8,32,128]{3,2,1,0:T(8,128)(2,1)} %bitcast.48), kind=kOutput, calls=%fused_computation.8 | convolution fusion | flops 2155872256 | bytes 36175872 | tf_op jit(solution)/shard_map/dot_general | solution.py:41
  72.7 1.8 copy.34
  74.6 0.0 all-gather.3.cloned.1.call-start
  74.6 11.6 %reduce-scatter.10.cloned.1.call-done = f32[32,4096]{1,0:T(8,128)} async-done(((f32[128,4096]{1,0:T(8,128)}), f32[32,4096]{1,0:T(8,128)}) %reduce-scatter.10.cloned.1.call-update) | async-done | bytes 524304 | tf_op jit(solution)/shard_map/reduce_scatter | solution.py:47
  86.2 45.7 %reduce-scatter.12.cloned.1.call-done = f32[32,4096]{1,0:T(8,128)} async-done(((f32[128,4096]{1,0:T(8,128)}), f32[32,4096]{1,0:T(8,128)}) %reduce-scatter.12.cloned.1.call-update) | async-done | bytes 524304 | tf_op jit(solution)/shard_map/reduce_scatter | solution.py:46
  131.9 2.4 multiply_convert_fusion
  134.3 0.0 all-gather.5.cloned.1.call-start
  134.4 0.1 copy.30
  134.4 0.1 copy.28
  134.5 0.4 all-gather.5.cloned.1.call-update
  134.9 0.2 reduce-scatter.8.cloned.1.call-start
  135.1 26.5 %all-gather.3.cloned.1.call-done = bf16[128,4096]{1,0:T(8,128)(2,1)} async-done(((bf16[32,4096]{1,0:T(8,128)(2,1)}), bf16[128,4096]{1,0:T(8,128)(2,1)}) %all-gather.3.cloned.1.call-update) | async-done | bytes 1048592 | tf_op jit(solution)/shard_map/all_gather | solution.py:52
  161.7 11.2 %mul.119 = f32[16,128,32,128]{1,0,3,2:T(8,128)} broadcast(f32[16,32]{0,1:T(8,128)S(1)} %copy.28), dimensions={0,2} | broadcast | bytes 33556480 | tf_op jit(solution)/shard_map/mul | solution.py:66
  172.9 21.8 %fusion.1 = bf16[2048,4096]{0,1:T(8,128)(2,1)} fusion(f32[512,8,16,128]{3,2,1,0:T(8,128)} %bitcast.47, bf16[128,4096]{1,0:T(8,128)(2,1)S(1)} %copy-done.3, bf16[128,2048]{1,0:T(8,128)(2,1)S(1)} %all_gather.13), kind=kOutput, calls=%fused_computation.3 | convolution fusion | flops 2164260864 | bytes 51904512 | tf_op jit(solution)/shard_map/dot_general | solution.py:62
  194.7 21.2 %copy.31 = bf16[2048,4096]{1,0:T(8,128)(2,1)} copy(bf16[2048,4096]{0,1:T(8,128)(2,1)} %fusion.1) | data formatting | bytes 33554432
  215.9 15.6 %fusion.5 = f32[128,2048]{1,0:T(8,128)} fusion(bf16[128,4096]{1,0:T(8,128)(2,1)S(1)} %copy-done.3, bf16[2048,4096]{1,0:T(8,128)(2,1)} %param.7, bf16[256,8,32,128]{3,2,1,0:T(8,128)(2,1)} %bitcast.49), kind=kOutput, calls=%fused_computation.10 | convolution fusion | flops 2155872256 | bytes 35651584 | tf_op jit(solution)/shard_map/dot_general | solution.py:71
  231.5 0.0 all-gather.5.cloned.1.call-done
  231.6 11.4 %mul.123 = f32[32,128,16,128]{3,2,1,0:T(8,128)} broadcast(f32[32,16]{1,0:T(8,128)S(1)} %copy.30), dimensions={0,2} | broadcast | bytes 33556480 | tf_op jit(solution)/shard_map/mul | solution.py:58
  242.9 21.9 %fusion = bf16[4096,2048]{1,0:T(8,128)(2,1)} fusion(f32[512,8,16,128]{3,2,1,0:T(8,128)} %bitcast.46, bf16[128,4096]{1,0:T(8,128)(2,1)S(1)} %copy-done.2, bf16[128,2048]{1,0:T(8,128)(2,1)S(1)} %all_gather.12), kind=kOutput, calls=%fused_computation.1 | convolution fusion | flops 2164260864 | bytes 51904512 | tf_op jit(solution)/shard_map/dot_general | solution.py:54
  264.8 2.3 reduce-scatter.8.cloned.1.call-done
  267.1 1.5 convert_element_type.43
  (16 shorter events, 0.1 us)
Async XLA Ops:
  7.2 0.8 copy-start
  7.2 79.0 %reduce-scatter.10.cloned.1.call-start = ((), (), s32[]{:S(2)}) async-start(), calls=%async_computation.6 | async-start | bytes 2621440 | tf_op jit(solution)/shard_map/reduce_scatter | solution.py:47
  26.3 15.9 %copy-start.4 = (bf16[16,2048]{1,0:T(8,128)(2,1)S(1)}, bf16[16,2048]{1,0:T(8,128)(2,1)}, u32[]{:S(2)}) copy-start(bf16[16,2048]{1,0:T(8,128)(2,1)} %param.5) | copy-start | bytes 196612
  42.1 89.8 %reduce-scatter.12.cloned.1.call-start = ((), (), s32[]{:S(2)}) async-start(), calls=%async_computation.7 | async-start | bytes 2621440 | tf_op jit(solution)/shard_map/reduce_scatter | solution.py:46
  74.6 87.1 %all-gather.3.cloned.1.call-start = ((), (), s32[]{:S(2)}) async-start(), calls=%async_computation.3 | async-start | bytes 1310720 | tf_op jit(solution)/shard_map/all_gather | solution.py:52
  134.3 97.2 %all-gather.5.cloned.1.call-start = ((), (), s32[]{:S(2)}) async-start(), calls=%async_computation.5 | async-start | bytes 1310720 | tf_op jit(solution)/shard_map/all_gather | solution.py:51
  134.9 132.2 %reduce-scatter.8.cloned.1.call-start = ((), (), s32[]{:S(2)}) async-start(), calls=%async_computation.4 | async-start | bytes 1179648 | tf_op jit(solution)/shard_map/reduce_scatter | solution.py:70
  161.7 11.2 %copy-start.3 = (bf16[128,4096]{1,0:T(8,128)(2,1)S(1)}, bf16[128,4096]{1,0:T(8,128)(2,1)}, u32[]{:S(2)}) copy-start(bf16[128,4096]{1,0:T(8,128)(2,1)} %all-gather.3.cloned.1.call-done) | copy-start | bytes 3145732
  231.5 11.4 %copy-start.2 = (bf16[128,4096]{1,0:T(8,128)(2,1)S(1)}, bf16[128,4096]{1,0:T(8,128)(2,1)}, u32[]{:S(2)}) copy-start(bf16[128,4096]{1,0:T(8,128)(2,1)} %all-gather.5.cloned.1.call-done) | copy-start | bytes 3145732
  242.9 25.7 %copy-start.1 = (s32[64,96]{1,0:T(8,128)S(1)}, s32[64,96]{1,0:T(8,128)}, u32[]{:S(2)}) copy-start(s32[64,96]{1,0:T(8,128)} %param.9) | copy-start | bytes 73732
Sparse Core Ops, SparseCore 0:
  42.3 43.9 reduce-scatter.9
  89.1 42.8 reduce-scatter.11
  134.4 27.1 all-gather.2
  163.1 27.3 all-gather.4
  231.6 35.4 reduce-scatter.7
where the time goes:
time: 276 us; the launch traced here: 275 us
  matrix products  88 us (32%)
  waiting for transfers between devices  86.7 us (31%)
  local copies, waits for them, and re-layouts  60.8 us (22%)
  blocking collectives  21.2 us (8%)
  between operations  13.9 us (5%)
  other arithmetic  4.33 us (2%)
    reduce_scatter x1, waiting for transfers between devices, local(): lax.psum_scatter(hidden_part, 'row', scatter_dimension=0, tiled=True)  45.7 us
    all_gather x1, waiting for transfers between devices, local(): lax.all_gather(hidden_grad, 'row', axis=0, tiled=True)  26.5 us
    unnamed x13, local copies, waits for them, and re-layouts  25.5 us
    dot_general x1, matrix products, local(): lax.dot_general(act_all, cotan_all, (((0,), (0,)), ((), ())), preferred_e...  21.9 us
    dot_general x1, matrix products, local(): lax.dot_general(token_all, hgrad_all, (((0,), (0,)), ((), ())), preferred...  21.8 us
    dot_general x1, matrix products, local(): lax.dot_general(hgrad_all, masked_up, (((1,), (1,)), ((), ())), preferred...  15.6 us
    dot_general x1, matrix products, local(): jnp.dot(token_all, masked_up, preferred_element_type=jnp.float32)  14.8 us
    dot_general x1, matrix products, local(): lax.dot_general(cotan_all, masked_down, (((1,), (1,)), ((), ())), preferr...  14 us
  transfers between devices with their start and end apart: 5, of which 4 were waited for; matrix products, arithmetic and copies ran while one was open for 46% of the time, Pallas kernels for 0%

commit v1 on v0

v1 whole, which is shorter than its diff:
```python
import functools

import jax
import jax.numpy as jnp
from jax import lax
from jax.experimental import pallas as pl
from jax.experimental.pallas import tpu as pltpu
from jax.sharding import PartitionSpec as P


BLOCK = 128
SUB = 16
PAIR = 2
VMEM_LIMIT = 56 * 1024 * 1024
SHARES = (3, 4, 4, 3, 2)
ROOT = 0.7978845608028654
CUBE = 0.044715


def chunk_steps(steps):
    total = sum(SHARES)
    edges = [0]
    run = 0
    for share in SHARES:
        run += share
        edge = (run * steps) // total
        if edge > edges[-1]:
            edges.append(edge)
    return [(a, b - a) for a, b in zip(edges[:-1], edges[1:])]


def tile_mask(block_index, row_blocks, col_blocks):
    row_place = lax.axis_index("row")
    col_place = lax.axis_index("col")
    own_rows = lax.dynamic_slice_in_dim(block_index, row_place * row_blocks, row_blocks, 0)
    own_cols = col_place * col_blocks + jnp.arange(col_blocks, dtype=jnp.int32)
    return jnp.any(own_rows[:, :, None] == own_cols[None, None, :], axis=1)


def masked(block, mask):
    groups = mask.shape[0]
    width = block.shape[1]
    tiled = block.reshape(groups, BLOCK // SUB, SUB, width) * mask[:, None]
    return tiled.reshape(groups * BLOCK, width)


def dot(a, b, dims=((1,), (0,))):
    return lax.dot_general(a, b, (dims, ((), ())), preferred_element_type=jnp.float32)


def forward_kernel(pair_ref, up_ref, down_ref, mu_ref, md_ref, own_ref, send_ref):
    up = masked(up_ref[...], mu_ref[...])
    hidden = dot(pair_ref[0], up)
    own_ref[0] = hidden
    send_ref[0] = hidden.astype(send_ref.dtype)
    down = masked(down_ref[...], md_ref[...])
    grad = dot(pair_ref[1], down, ((1,), (1,)))
    own_ref[1] = grad
    send_ref[1] = grad.astype(send_ref.dtype)


def forward(pair, up, down, mu, md, first, count, width):
    _, tokens, feats = pair.shape
    blocks = width // BLOCK
    part = pl.BlockSpec((2, tokens, width), lambda j: (0, 0, j))
    return pl.pallas_call(
        forward_kernel,
        grid=(count,),
        in_specs=[
            pl.BlockSpec((2, tokens, feats), lambda j: (0, 0, 0)),
            pl.BlockSpec((feats, width), lambda j: (0, first + j)),
            pl.BlockSpec((width, feats), lambda j: (first + j, 0)),
            pl.BlockSpec((feats // BLOCK, SUB, width), lambda j: (0, 0, first + j)),
            pl.BlockSpec((blocks, SUB, feats), lambda j: (first + j, 0, 0)),
        ],
        out_specs=[part, part],
        out_shape=[
            jax.ShapeDtypeStruct((2, tokens, count * width), jnp.float32),
            jax.ShapeDtypeStruct((2, tokens, count * width), jnp.bfloat16),
        ],
        compiler_params=pltpu.CompilerParams(vmem_limit_bytes=VMEM_LIMIT),
        cost_estimate=pl.CostEstimate(
            flops=4 * tokens * feats * width * count,
            bytes_accessed=4 * feats * width * count + 4 * tokens * feats,
            transcendentals=0,
        ),
        name="forward",
    )(pair, up, down, mu, md)


def finish(v, g):
    square = v * v
    t = jnp.tanh(v * (ROOT + (ROOT * CUBE) * square))
    half = 0.5 + 0.5 * t
    slope = half + (0.5 * v) * ((1.0 - t) * (1.0 + t)) * (ROOT + (3.0 * ROOT * CUBE) * square)
    return v * half, g * slope


def inner(own, came, up, mu, state, first, count, width):
    _, tokens, chunk = own.shape
    feats = up.shape[0]
    have = state is not None
    n_came = len(came)
    rows = tokens // 2

    def body(*refs):
        own_ref, came_refs, up_ref, mu_ref = refs[0], refs[1:1 + n_came], refs[1 + n_came], refs[2 + n_came]
        act_ref, hgrad_ref, lo_ref, hi_ref = refs[-4:]

        @pl.when(pl.program_id(0) == 0)
        def _():
            lo_ref[...] = refs[3 + n_came][...] if have else jnp.zeros_like(lo_ref)
            hi_ref[...] = refs[4 + n_came][...] if have else jnp.zeros_like(hi_ref)

        def total(k):
            value = own_ref[k]
            for ref in came_refs:
                value += ref[k].astype(jnp.float32)
            return value

        act, grad = finish(total(0), total(1))
        hgrad = grad.astype(jnp.bfloat16)
        act_ref[...] = act.astype(jnp.bfloat16)
        hgrad_ref[...] = hgrad
        band = min(feats, 4 * BLOCK)
        for b in range(feats // band):
            cut = slice(b * band, (b + 1) * band)
            part = dot(hgrad, masked(up_ref[cut, :], mu_ref[b * (band // BLOCK):(b + 1) * (band // BLOCK)]), ((1,), (1,)))
            lo_ref[:, cut] += part[:rows]
            hi_ref[:, cut] += part[rows:]

    part = pl.BlockSpec((2, tokens, width), lambda j: (0, 0, j))
    half_spec = pl.BlockSpec((rows, feats), lambda j: (0, 0))
    out = pl.BlockSpec((tokens, width), lambda j: (0, j))
    return pl.pallas_call(
        body,
        grid=(count,),
        in_specs=[
            *([part] * (1 + n_came)),
            pl.BlockSpec((feats, width), lambda j: (0, first + j)),
            pl.BlockSpec((feats // BLOCK, SUB, width), lambda j: (0, 0, first + j)),
            *([half_spec] * (2 if have else 0)),
        ],
        out_specs=[out, out, half_spec, half_spec],
        out_shape=[
            jax.ShapeDtypeStruct((tokens, chunk), jnp.bfloat16),
            jax.ShapeDtypeStruct((tokens, chunk), jnp.bfloat16),
            jax.ShapeDtypeStruct((rows, feats), jnp.float32),
            jax.ShapeDtypeStruct((rows, feats), jnp.float32),
        ],
        compiler_params=pltpu.CompilerParams(vmem_limit_bytes=VMEM_LIMIT),
        cost_estimate=pl.CostEstimate(
            flops=2 * tokens * feats * chunk,
            bytes_accessed=2 * feats * chunk + 8 * tokens * feats,
            transcendentals=tokens * chunk,
        ),
        name="inner",
    )(own, *came, up, mu, *(state or ()))


def weight_grads(tokt, pair, act, hgrad, mu, md, grads, units, first, count, width):
    _, tokens, feats = pair.shape
    blocks = width // BLOCK
    have = grads is not None

    def body(*refs):
        tokt_ref, cot_ref, act_ref, hgrad_ref, mu_ref, md_ref = refs[:6]
        upg_ref, dng_ref = refs[-2:]
        hgrad = hgrad_ref[...]
        act_t = act_ref[...].astype(jnp.float32).T.astype(jnp.bfloat16)
        band = min(feats, 4 * BLOCK)
        for b in range(feats // band):
            cut = slice(b * band, (b + 1) * band)
            mask = mu_ref[b * (band // BLOCK):(b + 1) * (band // BLOCK)]
            upg_ref[cut, :] = masked(dot(tokt_ref[cut, :], hgrad).astype(jnp.bfloat16), mask)
            dng_ref[:, cut] = masked(dot(act_t, cot_ref[0, :, cut]).astype(jnp.bfloat16), md_ref[:, :, cut])

    part = pl.BlockSpec((tokens, width), lambda j: (0, j))
    any_spec = pl.BlockSpec(memory_space=pl.ANY)
    return pl.pallas_call(
        body,
        grid=(count,),
        in_specs=[
            pl.BlockSpec((feats, tokens), lambda j: (0, 0)),
            pl.BlockSpec((1, tokens, feats), lambda j: (1, 0, 0)),
            part,
            part,
            pl.BlockSpec((feats // BLOCK, SUB, width), lambda j: (0, 0, first + j)),
            pl.BlockSpec((blocks, SUB, feats), lambda j: (first + j, 0, 0)),
            *([any_spec] * (2 if have else 0)),
        ],
        out_specs=[
            pl.BlockSpec((feats, width), lambda j: (0, first + j)),
            pl.BlockSpec((width, feats), lambda j: (first + j, 0)),
        ],
        out_shape=[
            jax.ShapeDtypeStruct((feats, units), jnp.bfloat16),
            jax.ShapeDtypeStruct((units, feats), jnp.bfloat16),
        ],
        input_output_aliases={6: 0, 7: 1} if have else {},
        compiler_params=pltpu.CompilerParams(vmem_limit_bytes=VMEM_LIMIT),
        cost_estimate=pl.CostEstimate(
            flops=4 * tokens * feats * width * count,
            bytes_accessed=4 * feats * width * count + 4 * tokens * feats,
            transcendentals=0,
        ),
        name="weight_grads",
    )(tokt, pair, act, hgrad, mu, md, *(grads or ()))


def xor_pairs(n, bits):
    return [(i, i ^ bits) for i in range(n)]


def gather_tokens(x, n, masks):
    if n == 1:
        return x, masks
    parts = [x] + [lax.ppermute(x, "col", xor_pairs(n, s)) for s in range(2, n, 2)]
    half = jnp.concatenate(parts, axis=1)
    half, masks = lax.optimization_barrier((half, masks))
    return jnp.concatenate([half, lax.ppermute(half, "col", xor_pairs(n, 1))], axis=1), masks


def scatter_tokens(lo, hi, n):
    mine = lo + lax.ppermute(hi, "col", xor_pairs(n, 1))
    rows = 2 * mine.shape[0] // n
    send = mine[rows:].astype(jnp.bfloat16)
    out = mine[:rows]
    for k, s in enumerate(range(2, n, 2)):
        came = lax.ppermute(send[k * rows:(k + 1) * rows], "col", xor_pairs(n, s))
        out = out + came.astype(jnp.float32)
    return out


def shift(x, pairs):
    return lax.ppermute(x, "row", pairs)


def local(rows, cols, tokens, cotangent, up_weight, down_weight, block_index):
    feats, units = up_weight.shape
    row_blocks = feats // BLOCK
    col_blocks = units // BLOCK
    hits = tile_mask(block_index, row_blocks, col_blocks).astype(jnp.bfloat16)
    mu = jnp.broadcast_to(hits[:, None, :, None], (row_blocks, SUB, col_blocks, BLOCK)).reshape(row_blocks, SUB, units)
    md = jnp.broadcast_to(hits.T[:, None, :, None], (col_blocks, SUB, row_blocks, BLOCK)).reshape(col_blocks, SUB, feats)
    pair, (mu, md) = gather_tokens(jnp.stack([tokens, cotangent]), cols, (mu, md))
    tokt = pair[0].T
    width = PAIR * BLOCK
    plan = chunk_steps(units // width)
    right = rows // 2
    sums = []
    for first, count in plan:
        own, near = forward(pair, up_weight, down_weight, mu, md, first, count, width)
        came = []
        for k in range(right - 1):
            came.append(shift(near, [(k, k + 1), (rows - 1 - k, rows - 2 - k)]))
            near = (own + sum(x.astype(jnp.float32) for x in came)).astype(jnp.bfloat16)
        came.append(shift(near, [(right - 1, right), (right, right - 1)]))
        out = own + came[-1].astype(jnp.float32)
        for k in reversed(range(right - 1)):
            far = shift(out.astype(jnp.bfloat16), [(k + 1, k), (rows - 2 - k, rows - 1 - k)])
            came.append(far)
            out = out + far.astype(jnp.float32)
        sums.append((own, came))
    state = grads = None
    for c, (first, count) in enumerate(plan):
        act, hgrad, *state = inner(*sums[c], up_weight, mu, state, first, count, width)
        grads = weight_grads(tokt, pair, act, hgrad, mu, md, grads, units, first, count, width)
    input_grad = scatter_tokens(*state, cols)
    return (input_grad.astype(jnp.bfloat16), *grads)


def whole(rows, cols, *arrays):
    return local(rows, cols, *arrays)


def solution(mesh):
    return jax.shard_map(
        functools.partial(whole, mesh.shape["row"], mesh.shape["col"]),
        mesh=mesh,
        in_specs=(P("col", "row"), P("col", "row"), P("row", "col"), P("col", "row"), P()),
        out_specs=(P("col", "row"), P("row", "col"), P("col", "row")),
        check_vma=False,
    )
```

time: 276 us -> 187 us (0.68)
  Pallas kernels: 0 us -> 89 us
  matrix products: 88 us -> 0 us
  local copies, waits for them, and re-layouts: 60.8 us -> 8.17 us
  waiting for transfers between devices: 86.7 us -> 53.3 us
  starting transfers between devices: 0.39 us -> 27.3 us
  blocking collectives: 21.2 us -> 0 us
  between operations: 13.9 us -> 1.26 us
    pallas_call x0 -> x15, Pallas kernels: none -> 89 us  [the longest x5 32.1 us: forward(): pl.pallas_call(forward_kernel, grid=(count,), in_specs=[pl.BlockSpec((2,...]
    dot_general x5 -> x0, matrix products: 88 us -> none  [the longest x1 21.9 us: local(): lax.dot_general(act_all, cotan_all, (((0,), (0,)), ((), ())), preferred_e...]
    reduce_scatter x3 -> x0, waiting for transfers between devices: 59.7 us -> none  [the longest x1 45.7 us: local(): lax.psum_scatter(hidden_part, 'row', scatter_dimension=0, tiled=True)]
    ppermute x0 -> x23, waiting for transfers between devices: none -> 53.3 us  [the longest x15 46.1 us: shift(): return lax.ppermute(x, 'row', pairs)]
    mul x4 -> x0, local copies, waits for them, and re-layouts: 35 us -> none  [the longest x1 11.4 us: local(): down_sum.reshape(col_blocks, BLOCK, row_blocks, BLOCK)]
    ppermute x0 -> x23, starting transfers between devices: none -> 27.3 us  [the longest x15 19.1 us: shift(): return lax.ppermute(x, 'row', pairs)]
    all_gather x2 -> x0, waiting for transfers between devices: 26.6 us -> none  [the longest x1 26.5 us: local(): lax.all_gather(hidden_grad, 'row', axis=0, tiled=True)]
    unnamed x13 -> x49, local copies, waits for them, and re-layouts: 25.5 us -> 3.49 us
  transfers between devices with their start and end apart: 5 -> 23, of which waited for: 4 -> 8; matrix products, arithmetic and copies ran while one was open for 46% -> 3% of each run, Pallas kernels for 0% -> 40%
where the time goes in v1:
time: 187 us; the launch traced here: 186 us
  Pallas kernels  89 us (48%)
  waiting for transfers between devices  53.3 us (29%)
  starting transfers between devices  27.3 us (15%)
  local copies, waits for them, and re-layouts  8.17 us (4%)
  other arithmetic  6.51 us (3%)
    ppermute x15, waiting for transfers between devices, shift(): return lax.ppermute(x, 'row', pairs)  46.1 us
    pallas_call x5, Pallas kernels, forward(): pl.pallas_call(forward_kernel, grid=(count,), in_specs=[pl.BlockSpec((2,...  32.1 us
    pallas_call x5, Pallas kernels, weight_grads(): pl.pallas_call(body, grid=(count,), in_specs=[pl.BlockSpec((feats, tokens...  29.5 us
    pallas_call x5, Pallas kernels, inner(): pl.pallas_call(body, grid=(count,), in_specs=[*[part] * (1 + n_came), pl....  27.4 us
    ppermute x15, starting transfers between devices, shift(): return lax.ppermute(x, 'row', pairs)  19.1 us
    ppermute x3, waiting for transfers between devices, gather_tokens(): lax.ppermute(x, 'col', xor_pairs(n, s))  5.31 us
    ppermute x3, starting transfers between devices, gather_tokens(): lax.ppermute(x, 'col', xor_pairs(n, s))  4.57 us
  transfers between devices with their start and end apart: 23, of which 8 were waited for; matrix products, arithmetic and copies ran while one was open for 3% of the time, Pallas kernels for 40%

profile of v1, /device:TPU:0, one launch (start us, length us, event | category | flops | bytes accessed | tf_op | source)
XLA Modules:
  0.0 185.6 jit_solution(17901497247530350782)
XLA Ops:
  1.5 3.0 %collective-permute-start = (bf16[2,16,2048]{2,1,0:T(8,128)(2,1)S(1)}, bf16[2,16,2048]{2,1,0:T(8,128)(2,1)S(1)}, u32[]{:S(2)}, u32[]{:S(2)}) collective-permute-start(bf16[2,16,2048]{2,1,0:T(8,128)(2,1)S(1)} %pad_maximum_fusion.1), channel_id=1, source_target_pairs={{0,2},{1,3},{2,0},{3,1},{4,6},{5,7},{6,4},{7,5},{8,10},{9,11},{10,... | collective-permute-start | bytes 393224 | tf_op jit(solution)/shard_map/ppermute | solution.py:218
  4.6 1.5 collective-permute-start.1
  7.0 1.4 collective-permute-done
  8.5 3.9 %collective-permute-done.1 = bf16[2,16,2048]{2,1,0:T(8,128)(2,1)S(1)} collective-permute-done((bf16[2,16,2048]{2,1,0:T(8,128)(2,1)S(1)}, bf16[2,16,2048]{2,1,0:T(8,128)(2,1)S(1)}, u32[]{:S(2)}, u32[]{:S(2)}) %collective-permute-start.1) | collective-permute-done | bytes 131104 | tf_op jit(solution)/shard_map/ppermute | solution.py:218
  13.3 1.6 broadcast_in_dim.27.md_ref.refs_5_
  14.9 1.6 broadcast_in_dim.24.mu_ref.refs_5_.refs_4_
  16.5 1.9 %collective-permute-done.3 = bf16[2,64,2048]{2,1,0:T(8,128)(2,1)S(1)} collective-permute-done((bf16[2,64,2048]{2,1,0:T(8,128)(2,1)S(1)}, bf16[2,64,2048]{2,1,0:T(8,128)(2,1)S(1)}, u32[]{:S(2)}, u32[]{:S(2)}) %collective-permute-start.3) | collective-permute-done | bytes 524320 | tf_op jit(solution)/shard_map/ppermute | solution.py:221
  19.5 6.5 %forward.9 = (f32[2,128,768]{2,1,0:T(8,128)}, bf16[2,128,768]{2,1,0:T(8,128)(2,1)}) custom-call(bf16[2,128,2048]{2,1,0:T(8,128)(2,1)} %copy-done.2, bf16[2048,4096]{1,0:T(8,128)(2,1)} %refs_4_.9, bf16[4096,2048]{1,0:T(8,128)(2,1)} %down_ref.9, bf16[16,16,4096]{2,1,0:T(8,128)(2,1)} %broadcast_in_dim.24.mu_ref.refs_5_.refs_4_, ...), custom_call_target="tpu_custom_call" | custom-call | flops 805306368 | bytes 7340032 | tf_op jit(solution)/shard_map/forward/pallas_call | solution.py:66
  25.9 4.4 %forward.5 = (f32[2,128,512]{2,1,0:T(8,128)}, bf16[2,128,512]{2,1,0:T(8,128)(2,1)}) custom-call(bf16[2,128,2048]{2,1,0:T(8,128)(2,1)} %copy-done.2, bf16[2048,4096]{1,0:T(8,128)(2,1)} %refs_4_.9, bf16[4096,2048]{1,0:T(8,128)(2,1)} %down_ref.9, bf16[16,16,4096]{2,1,0:T(8,128)(2,1)} %broadcast_in_dim.24.mu_ref.refs_5_.refs_4_, ...), custom_call_target="tpu_custom_call" | custom-call | flops 536870912 | bytes 5242880 | tf_op jit(solution)/shard_map/forward/pallas_call | solution.py:66
  30.3 3.5 %collective-permute-start.16 = (bf16[2,128,768]{2,1,0:T(8,128)(2,1)S(1)}, bf16[2,128,768]{2,1,0:T(8,128)(2,1)S(1)}, u32[]{:S(2)}, u32[]{:S(2)}) collective-permute-start(bf16[2,128,768]{2,1,0:T(8,128)(2,1)S(1)} %copy-done.22), channel_id=1, source_target_pairs={{0,8},{24,16},{1,9},{25,17},{2,10},{26,18},{3,11},{27,19},{4,12},{... | collective-permute-start | bytes 1179656 | tf_op jit(solution)/shard_map/ppermute | solution.py:236
  35.1 7.3 %forward.8 = (f32[2,128,1024]{2,1,0:T(8,128)}, bf16[2,128,1024]{2,1,0:T(8,128)(2,1)}) custom-call(bf16[2,128,2048]{2,1,0:T(8,128)(2,1)} %copy-done.2, bf16[2048,4096]{1,0:T(8,128)(2,1)} %refs_4_.9, bf16[4096,2048]{1,0:T(8,128)(2,1)} %down_ref.9, bf16[16,16,4096]{2,1,0:T(8,128)(2,1)} %broadcast_in_dim.24.mu_ref.refs_5_.refs_4_, ...), custom_call_target="tpu_custom_call" | custom-call | flops 1073741824 | bytes 9437184 | tf_op jit(solution)/shard_map/forward/pallas_call | solution.py:66
  43.8 7.3 %forward.7 = (f32[2,128,1024]{2,1,0:T(8,128)}, bf16[2,128,1024]{2,1,0:T(8,128)(2,1)}) custom-call(bf16[2,128,2048]{2,1,0:T(8,128)(2,1)} %copy-done.2, bf16[2048,4096]{1,0:T(8,128)(2,1)} %refs_4_.9, bf16[4096,2048]{1,0:T(8,128)(2,1)} %down_ref.9, bf16[16,16,4096]{2,1,0:T(8,128)(2,1)} %broadcast_in_dim.24.mu_ref.refs_5_.refs_4_, ...), custom_call_target="tpu_custom_call" | custom-call | flops 1073741824 | bytes 9437184 | tf_op jit(solution)/shard_map/forward/pallas_call | solution.py:66
  51.2 1.7 collective-permute-start.10
  52.8 6.6 %forward.6 = (f32[2,128,768]{2,1,0:T(8,128)}, bf16[2,128,768]{2,1,0:T(8,128)(2,1)}) custom-call(bf16[2,128,2048]{2,1,0:T(8,128)(2,1)} %copy-done.2, bf16[2048,4096]{1,0:T(8,128)(2,1)} %refs_4_.9, bf16[4096,2048]{1,0:T(8,128)(2,1)} %down_ref.9, bf16[16,16,4096]{2,1,0:T(8,128)(2,1)} %broadcast_in_dim.24.mu_ref.refs_5_.refs_4_, ...), custom_call_target="tpu_custom_call" | custom-call | flops 805306368 | bytes 7340032 | tf_op jit(solution)/shard_map/forward/pallas_call | solution.py:66
  62.3 16.8 %collective-permute-done.7.refs_1_ = bf16[2,128,768]{2,1,0:T(8,128)(2,1)S(1)} collective-permute-done((bf16[2,128,768]{2,1,0:T(8,128)(2,1)}, bf16[2,128,768]{2,1,0:T(8,128)(2,1)S(1)}, u32[]{:S(2)}, u32[]{:S(2)}) %collective-permute-start.7) | collective-permute-done | bytes 393248 | tf_op jit(solution)/shard_map/ppermute | solution.py:236
  87.2 1.3 add_convert_fusion.6
  90.0 1.5 collective-permute-start.6
  91.5 10.2 %collective-permute-done.18.refs_3_ = bf16[2,128,768]{2,1,0:T(8,128)(2,1)} collective-permute-done((bf16[2,128,768]{2,1,0:T(8,128)(2,1)S(1)}, bf16[2,128,768]{2,1,0:T(8,128)(2,1)}, u32[]{:S(2)}, u32[]{:S(2)}) %collective-permute-start.18) | collective-permute-done | bytes 393248 | tf_op jit(solution)/shard_map/ppermute | solution.py:236
  101.7 5.2 %inner.5 = (bf16[128,768]{1,0:T(8,128)(2,1)}, bf16[128,768]{1,0:T(8,128)(2,1)}, f32[64,2048]{1,0:T(8,128)}, f32[64,2048]{1,0:T(8,128)}) custom-call(f32[2,128,768]{2,1,0:T(8,128)} %get-tuple-element.57.refs_0_, bf16[2,128,768]{2,1,0:T(8,128)(2,1)} %copy-done.13, bf16[2,128,768]{2,1,0:T(8,128)(2,1)} %copy-done.15, ...), custom_call_target="tpu_custom_call" | custom-call | flops 402653184 | bytes 5242880 | tf_op jit(solution)/shard_map/inner/pallas_call | solution.py:135
  106.9 11.3 %collective-permute-done.15.refs_3_ = bf16[2,128,1024]{2,1,0:T(8,128)(2,1)S(1)} collective-permute-done((bf16[2,128,1024]{2,1,0:T(8,128)(2,1)S(1)}, bf16[2,128,1024]{2,1,0:T(8,128)(2,1)S(1)}, u32[]{:S(2)}, u32[]{:S(2)}) %collective-permute-start.15) | collective-permute-done | bytes 524320 | tf_op jit(solution)/shard_map/ppermute | solution.py:236
  119.0 6.3 %inner.6 = (bf16[128,1024]{1,0:T(8,128)(2,1)}, bf16[128,1024]{1,0:T(8,128)(2,1)}, f32[64,2048]{1,0:T(8,128)}, f32[64,2048]{1,0:T(8,128)}) custom-call(f32[2,128,1024]{2,1,0:T(8,128)} %get-tuple-element.55.refs_0_, bf16[2,128,1024]{2,1,0:T(8,128)(2,1)} %copy-done.9, bf16[2,128,1024]{2,1,0:T(8,128)(2,1)} %copy-done.11, bf16[2,128,1024]{2,1,0:T(8,128)(2,1)} %copy-done.19, ...), custom_call_target="tpu_custom_call" | custom-call | flops 536870912 | bytes 6291456 | tf_op jit(solution)/shard_map/inner/pallas_call | solution.py:135
  125.3 6.4 %collective-permute-done.12.refs_3_ = bf16[2,128,1024]{2,1,0:T(8,128)(2,1)S(1)} collective-permute-done((bf16[2,128,1024]{2,1,0:T(8,128)(2,1)S(1)}, bf16[2,128,1024]{2,1,0:T(8,128)(2,1)S(1)}, u32[]{:S(2)}, u32[]{:S(2)}) %collective-permute-start.12) | collective-permute-done | bytes 524320 | tf_op jit(solution)/shard_map/ppermute | solution.py:236
  132.4 6.3 %inner.7 = (bf16[128,1024]{1,0:T(8,128)(2,1)}, bf16[128,1024]{1,0:T(8,128)(2,1)}, f32[64,2048]{1,0:T(8,128)}, f32[64,2048]{1,0:T(8,128)}) custom-call(f32[2,128,1024]{2,1,0:T(8,128)} %get-tuple-element.53.refs_0_, bf16[2,128,1024]{2,1,0:T(8,128)(2,1)} %copy-done.8, bf16[2,128,1024]{2,1,0:T(8,128)(2,1)} %copy-done.10, bf16[2,128,1024]{2,1,0:T(8,128)(2,1)} %copy-done.18, ...), custom_call_target="tpu_custom_call" | custom-call | flops 536870912 | bytes 6291456 | tf_op jit(solution)/shard_map/inner/pallas_call | solution.py:135
  138.7 1.5 collective-permute-done.9.refs_3_
  140.2 5.6 %inner.8 = (bf16[128,768]{1,0:T(8,128)(2,1)}, bf16[128,768]{1,0:T(8,128)(2,1)}, f32[64,2048]{1,0:T(8,128)}, f32[64,2048]{1,0:T(8,128)}) custom-call(f32[2,128,768]{2,1,0:T(8,128)} %get-tuple-element.51.refs_0_, bf16[2,128,768]{2,1,0:T(8,128)(2,1)} %copy-done.12, bf16[2,128,768]{2,1,0:T(8,128)(2,1)} %copy-done.14, ...), custom_call_target="tpu_custom_call" | custom-call | flops 402653184 | bytes 5242880 | tf_op jit(solution)/shard_map/inner/pallas_call | solution.py:135
  146.5 4.1 %inner.9 = (bf16[128,512]{1,0:T(8,128)(2,1)}, bf16[128,512]{1,0:T(8,128)(2,1)}, f32[64,2048]{1,0:T(8,128)}, f32[64,2048]{1,0:T(8,128)}) custom-call(f32[2,128,512]{2,1,0:T(8,128)} %get-tuple-element.49.refs_0_, bf16[2,128,512]{2,1,0:T(8,128)(2,1)} %copy-done.16, bf16[2,128,512]{2,1,0:T(8,128)(2,1)} %copy-done.17, bf16[2,128,512]{2,1,0:T(8,128)(2,1)} %copy-done.21, ...), custom_call_target="tpu_custom_call" | custom-call | flops 268435456 | bytes 4194304 | tf_op jit(solution)/shard_map/inner/pallas_call | solution.py:135
  151.8 5.7 %weight_grads.5 = (bf16[2048,4096]{1,0:T(8,128)(2,1)}, bf16[4096,2048]{1,0:T(8,128)(2,1)}) custom-call(bf16[2048,128]{1,0:T(8,128)(2,1)} %copy.27.refs_0_, bf16[2,128,2048]{2,1,0:T(8,128)(2,1)} %copy-done.2, bf16[128,768]{1,0:T(8,128)(2,1)} %get-tuple-element.77.refs_2_, bf16[128,768]{1,0:T(8,128)(2,1)} %get-tuple-element.78.refs_3_, ...), custom_call_target="tpu_custom_call" | custom-call | flops 805306368 | bytes 7340032 | tf_op jit(solution)/shard_map/weight_grads/pallas_call | solution.py:180
  157.5 6.9 %weight_grads.6 = (bf16[2048,4096]{1,0:T(8,128)(2,1)}, bf16[4096,2048]{1,0:T(8,128)(2,1)}) custom-call(bf16[2048,128]{1,0:T(8,128)(2,1)} %copy.27.refs_0_, bf16[2,128,2048]{2,1,0:T(8,128)(2,1)} %copy-done.2, bf16[128,1024]{1,0:T(8,128)(2,1)} %get-tuple-element.75.refs_2_, ...), custom_call_target="tpu_custom_call", output_to_operand_aliasing={{0}: (6, {}), {1}: (7, {})} | custom-call | flops 1073741824 | bytes 9437184 | tf_op jit(solution)/shard_map/weight_grads/pallas_call | solution.py:180
  164.4 6.9 %weight_grads.7 = (bf16[2048,4096]{1,0:T(8,128)(2,1)}, bf16[4096,2048]{1,0:T(8,128)(2,1)}) custom-call(bf16[2048,128]{1,0:T(8,128)(2,1)} %copy.27.refs_0_, bf16[2,128,2048]{2,1,0:T(8,128)(2,1)} %copy-done.2, bf16[128,1024]{1,0:T(8,128)(2,1)} %get-tuple-element.73.refs_2_, ...), custom_call_target="tpu_custom_call", output_to_operand_aliasing={{0}: (6, {}), {1}: (7, {})} | custom-call | flops 1073741824 | bytes 9437184 | tf_op jit(solution)/shard_map/weight_grads/pallas_call | solution.py:180
  173.5 1.4 collective-permute-start.22
  175.0 5.7 %weight_grads.8 = (bf16[2048,4096]{1,0:T(8,128)(2,1)}, bf16[4096,2048]{1,0:T(8,128)(2,1)}) custom-call(bf16[2048,128]{1,0:T(8,128)(2,1)} %copy.27.refs_0_, bf16[2,128,2048]{2,1,0:T(8,128)(2,1)} %copy-done.2, bf16[128,768]{1,0:T(8,128)(2,1)} %get-tuple-element.71.refs_2_, ...), custom_call_target="tpu_custom_call", output_to_operand_aliasing={{0}: (6, {}), {1}: (7, {})} | custom-call | flops 805306368 | bytes 7340032 | tf_op jit(solution)/shard_map/weight_grads/pallas_call | solution.py:180
  180.7 4.3 %weight_grads.9 = (bf16[2048,4096]{1,0:T(8,128)(2,1)}, bf16[4096,2048]{1,0:T(8,128)(2,1)}) custom-call(bf16[2048,128]{1,0:T(8,128)(2,1)} %copy.27.refs_0_, bf16[2,128,2048]{2,1,0:T(8,128)(2,1)} %copy-done.2, bf16[128,512]{1,0:T(8,128)(2,1)} %get-tuple-element.69.refs_2_, ...), custom_call_target="tpu_custom_call", output_to_operand_aliasing={{0}: (6, {}), {1}: (7, {})} | custom-call | flops 536870912 | bytes 5242880 | tf_op jit(solution)/shard_map/weight_grads/pallas_call | solution.py:180
  (105 shorter events, 24.9 us)
Async XLA Ops:
  1.5 6.9 %collective-permute-start = (bf16[2,16,2048]{2,1,0:T(8,128)(2,1)S(1)}, bf16[2,16,2048]{2,1,0:T(8,128)(2,1)S(1)}, u32[]{:S(2)}, u32[]{:S(2)}) collective-permute-start(bf16[2,16,2048]{2,1,0:T(8,128)(2,1)S(1)} %pad_maximum_fusion.1), channel_id=1, source_target_pairs={{0,2},{1,3},{2,0},{3,1},{4,6},{5,7},{6,4},{7,5},{8,10},{9,11},{10,... | collective-permute-start | bytes 393224 | tf_op jit(solution)/shard_map/ppermute | solution.py:218
  4.6 7.8 %collective-permute-start.1 = (bf16[2,16,2048]{2,1,0:T(8,128)(2,1)S(1)}, bf16[2,16,2048]{2,1,0:T(8,128)(2,1)S(1)}, u32[]{:S(2)}, u32[]{:S(2)}) collective-permute-start(bf16[2,16,2048]{2,1,0:T(8,128)(2,1)S(1)} %pad_maximum_fusion.1), channel_id=1, source_target_pairs={{0,4},{1,5},{2,6},{3,7},{4,0},{5,1},{6,2},{7,3},{8,12},{9,13},{10,... | collective-permute-start | bytes 393224 | tf_op jit(solution)/shard_map/ppermute | solution.py:218
  6.1 6.3 %collective-permute-start.2 = (bf16[2,16,2048]{2,1,0:T(8,128)(2,1)S(1)}, bf16[2,16,2048]{2,1,0:T(8,128)(2,1)S(1)}, u32[]{:S(2)}, u32[]{:S(2)}) collective-permute-start(bf16[2,16,2048]{2,1,0:T(8,128)(2,1)S(1)} %pad_maximum_fusion.1), channel_id=1, source_target_pairs={{0,6},{1,7},{2,4},{3,5},{4,2},{5,3},{6,0},{7,1},{8,14},{9,15},{10,... | collective-permute-start | bytes 393224 | tf_op jit(solution)/shard_map/ppermute | solution.py:218
  16.5 1.9 %collective-permute-start.3 = (bf16[2,64,2048]{2,1,0:T(8,128)(2,1)S(1)}, bf16[2,64,2048]{2,1,0:T(8,128)(2,1)S(1)}, u32[]{:S(2)}, u32[]{:S(2)}) collective-permute-start(bf16[2,64,2048]{2,1,0:T(8,128)(2,1)S(1)} %pad_maximum_fusion), channel_id=1, source_target_pairs={{0,1},{1,0},{2,3},{3,2},{4,5},{5,4},{6,7},{7,6},{8,9},{9,8},{10,11... | collective-permute-start | bytes 1572872 | tf_op jit(solution)/shard_map/ppermute | solution.py:221
  30.3 31.2 %collective-permute-start.16 = (bf16[2,128,768]{2,1,0:T(8,128)(2,1)S(1)}, bf16[2,128,768]{2,1,0:T(8,128)(2,1)S(1)}, u32[]{:S(2)}, u32[]{:S(2)}) collective-permute-start(bf16[2,128,768]{2,1,0:T(8,128)(2,1)S(1)} %copy-done.22), channel_id=1, source_target_pairs={{0,8},{24,16},{1,9},{25,17},{2,10},{26,18},{3,11},{27,19},{4,12},{... | collective-permute-start | bytes 1179656 | tf_op jit(solution)/shard_map/ppermute | solution.py:236
  33.8 26.9 %collective-permute-start.4 = (bf16[2,128,512]{2,1,0:T(8,128)(2,1)}, bf16[2,128,512]{2,1,0:T(8,128)(2,1)S(1)}, u32[]{:S(2)}, u32[]{:S(2)}) collective-permute-start(bf16[2,128,512]{2,1,0:T(8,128)(2,1)} %get-tuple-element.50), channel_id=1, source_target_pairs={{0,8},{24,16},{1,9},{25,17},{2,10},{26,18},{3,11},{27,19},{4,12},{... | collective-permute-start | bytes 786440 | tf_op jit(solution)/shard_map/ppermute | solution.py:236
  42.5 38.6 %collective-permute-start.13 = (bf16[2,128,1024]{2,1,0:T(8,128)(2,1)}, bf16[2,128,1024]{2,1,0:T(8,128)(2,1)S(1)}, u32[]{:S(2)}, u32[]{:S(2)}) collective-permute-start(bf16[2,128,1024]{2,1,0:T(8,128)(2,1)} %get-tuple-element.56), channel_id=1, source_target_pairs={{0,8},{24,16},{1,9},{25,17},{2,10},{26,18},{3,11},{27,19},{4,12},{... | collective-permute-start | bytes 1572872 | tf_op jit(solution)/shard_map/ppermute | solution.py:236
  51.1 30.9 %copy-start.4 = (f32[2,128,1024]{2,1,0:T(8,128)S(1)}, f32[2,128,1024]{2,1,0:T(8,128)}, u32[]{:S(2)}) copy-start(f32[2,128,1024]{2,1,0:T(8,128)} %get-tuple-element.53.refs_0_) | copy-start | bytes 3145732
  51.2 30.8 %collective-permute-start.10 = (bf16[2,128,1024]{2,1,0:T(8,128)(2,1)}, bf16[2,128,1024]{2,1,0:T(8,128)(2,1)S(1)}, u32[]{:S(2)}, u32[]{:S(2)}) collective-permute-start(bf16[2,128,1024]{2,1,0:T(8,128)(2,1)} %get-tuple-element.54), channel_id=1, source_target_pairs={{0,8},{24,16},{1,9},{25,17},{2,10},{26,18},{3,11},{27,19},{4,12},{... | collective-permute-start | bytes 1572872 | tf_op jit(solution)/shard_map/ppermute | solution.py:236
  59.4 19.7 %collective-permute-start.7 = (bf16[2,128,768]{2,1,0:T(8,128)(2,1)}, bf16[2,128,768]{2,1,0:T(8,128)(2,1)S(1)}, u32[]{:S(2)}, u32[]{:S(2)}) collective-permute-start(bf16[2,128,768]{2,1,0:T(8,128)(2,1)} %get-tuple-element.52), channel_id=1, source_target_pairs={{0,8},{24,16},{1,9},{25,17},{2,10},{26,18},{3,11},{27,19},{4,12},{... | collective-permute-start | bytes 1179656 | tf_op jit(solution)/shard_map/ppermute | solution.py:236
  60.7 46.2 %copy-start.16 = (bf16[2,128,512]{2,1,0:T(8,128)(2,1)}, bf16[2,128,512]{2,1,0:T(8,128)(2,1)S(1)}, u32[]{:S(2)}) copy-start(bf16[2,128,512]{2,1,0:T(8,128)(2,1)S(1)} %collective-permute-done.4.refs_1_) | copy-start | bytes 786436
  60.8 29.1 %collective-permute-start.5 = (bf16[2,128,512]{2,1,0:T(8,128)(2,1)S(1)}, bf16[2,128,512]{2,1,0:T(8,128)(2,1)S(1)}, u32[]{:S(2)}, u32[]{:S(2)}) collective-permute-start(bf16[2,128,512]{2,1,0:T(8,128)(2,1)S(1)} %add_convert_fusion.9), channel_id=1, source_target_pairs={{8,16},{16,8},{9,17},{17,9},{10,18},{18,10},{11,19},{19,11},{12,20... | collective-permute-start | bytes 786440 | tf_op jit(solution)/shard_map/ppermute | solution.py:236
  61.5 40.2 %copy-start.13 = (bf16[2,128,768]{2,1,0:T(8,128)(2,1)}, bf16[2,128,768]{2,1,0:T(8,128)(2,1)S(1)}, u32[]{:S(2)}) copy-start(bf16[2,128,768]{2,1,0:T(8,128)(2,1)S(1)} %collective-permute-done.16.refs_1_) | copy-start | bytes 1179652
  61.6 21.3 %collective-permute-start.17 = (bf16[2,128,768]{2,1,0:T(8,128)(2,1)S(1)}, bf16[2,128,768]{2,1,0:T(8,128)(2,1)S(1)}, u32[]{:S(2)}, u32[]{:S(2)}) collective-permute-start(bf16[2,128,768]{2,1,0:T(8,128)(2,1)S(1)} %add_convert_fusion.5), channel_id=1, source_target_pairs={{8,16},{16,8},{9,17},{17,9},{10,18},{18,10},{11,19},{19,11},{12,20... | collective-permute-start | bytes 1179656 | tf_op jit(solution)/shard_map/ppermute | solution.py:236
  80.4 6.8 %collective-permute-start.8 = (bf16[2,128,768]{2,1,0:T(8,128)(2,1)S(1)}, bf16[2,128,768]{2,1,0:T(8,128)(2,1)S(1)}, u32[]{:S(2)}, u32[]{:S(2)}) collective-permute-start(bf16[2,128,768]{2,1,0:T(8,128)(2,1)S(1)} %add_convert_fusion.7), channel_id=1, source_target_pairs={{8,16},{16,8},{9,17},{17,9},{10,18},{18,10},{11,19},{19,11},{12,20... | collective-permute-start | bytes 1179656 | tf_op jit(solution)/shard_map/ppermute | solution.py:236
  81.1 37.0 %copy-start.9 = (bf16[2,128,1024]{2,1,0:T(8,128)(2,1)}, bf16[2,128,1024]{2,1,0:T(8,128)(2,1)S(1)}, u32[]{:S(2)}) copy-start(bf16[2,128,1024]{2,1,0:T(8,128)(2,1)S(1)} %collective-permute-done.13.refs_1_) | copy-start | bytes 1572868
  81.3 3.0 %collective-permute-start.14 = (bf16[2,128,1024]{2,1,0:T(8,128)(2,1)S(1)}, bf16[2,128,1024]{2,1,0:T(8,128)(2,1)S(1)}, u32[]{:S(2)}, u32[]{:S(2)}) collective-permute-start(bf16[2,128,1024]{2,1,0:T(8,128)(2,1)S(1)} %add_convert_fusion.1), channel_id=1, source_target_pairs={{8,16},{16,8},{9,17},{17,9},{10,18},{18,10},{11,19},{19,11},{12,20... | collective-permute-start | bytes 1572872 | tf_op jit(solution)/shard_map/ppermute | solution.py:236
  82.0 43.2 %copy-start.8 = (bf16[2,128,1024]{2,1,0:T(8,128)(2,1)}, bf16[2,128,1024]{2,1,0:T(8,128)(2,1)S(1)}, u32[]{:S(2)}) copy-start(bf16[2,128,1024]{2,1,0:T(8,128)(2,1)S(1)} %collective-permute-done.10.refs_1_) | copy-start | bytes 1572868
  82.2 3.6 %collective-permute-start.11 = (bf16[2,128,1024]{2,1,0:T(8,128)(2,1)S(1)}, bf16[2,128,1024]{2,1,0:T(8,128)(2,1)S(1)}, u32[]{:S(2)}, u32[]{:S(2)}) collective-permute-start(bf16[2,128,1024]{2,1,0:T(8,128)(2,1)S(1)} %add_convert_fusion.3), channel_id=1, source_target_pairs={{8,16},{16,8},{9,17},{17,9},{10,18},{18,10},{11,19},{19,11},{12,20... | collective-permute-start | bytes 1572872 | tf_op jit(solution)/shard_map/ppermute | solution.py:236
  83.0 18.7 %collective-permute-start.18 = (bf16[2,128,768]{2,1,0:T(8,128)(2,1)S(1)}, bf16[2,128,768]{2,1,0:T(8,128)(2,1)}, u32[]{:S(2)}, u32[]{:S(2)}) collective-permute-start(bf16[2,128,768]{2,1,0:T(8,128)(2,1)S(1)} %add_convert_fusion.4), channel_id=1, source_target_pairs={{8,0},{16,24},{9,1},{17,25},{10,2},{18,26},{11,3},{19,27},{12,4},{... | collective-permute-start | bytes 1179656 | tf_op jit(solution)/shard_map/ppermute | solution.py:236
  84.3 33.9 %copy-start.11 = (bf16[2,128,1024]{2,1,0:T(8,128)(2,1)}, bf16[2,128,1024]{2,1,0:T(8,128)(2,1)S(1)}, u32[]{:S(2)}) copy-start(bf16[2,128,1024]{2,1,0:T(8,128)(2,1)S(1)} %collective-permute-done.14.refs_2_) | copy-start | bytes 1572868
  84.4 33.7 %collective-permute-start.15 = (bf16[2,128,1024]{2,1,0:T(8,128)(2,1)S(1)}, bf16[2,128,1024]{2,1,0:T(8,128)(2,1)S(1)}, u32[]{:S(2)}, u32[]{:S(2)}) collective-permute-start(bf16[2,128,1024]{2,1,0:T(8,128)(2,1)S(1)} %add_convert_fusion), channel_id=1, source_target_pairs={{8,0},{16,24},{9,1},{17,25},{10,2},{18,26},{11,3},{19,27},{12,4},{... | collective-permute-start | bytes 1572872 | tf_op jit(solution)/shard_map/ppermute | solution.py:236
  85.8 39.5 %copy-start.10 = (bf16[2,128,1024]{2,1,0:T(8,128)(2,1)}, bf16[2,128,1024]{2,1,0:T(8,128)(2,1)S(1)}, u32[]{:S(2)}) copy-start(bf16[2,128,1024]{2,1,0:T(8,128)(2,1)S(1)} %collective-permute-done.11.refs_2_) | copy-start | bytes 1572868
  85.9 45.7 %collective-permute-start.12 = (bf16[2,128,1024]{2,1,0:T(8,128)(2,1)S(1)}, bf16[2,128,1024]{2,1,0:T(8,128)(2,1)S(1)}, u32[]{:S(2)}, u32[]{:S(2)}) collective-permute-start(bf16[2,128,1024]{2,1,0:T(8,128)(2,1)S(1)} %add_convert_fusion.2), channel_id=1, source_target_pairs={{8,0},{16,24},{9,1},{17,25},{10,2},{18,26},{11,3},{19,27},{12,4},{... | collective-permute-start | bytes 1572872 | tf_op jit(solution)/shard_map/ppermute | solution.py:236
  87.2 38.0 %copy-start.14 = (bf16[2,128,768]{2,1,0:T(8,128)(2,1)}, bf16[2,128,768]{2,1,0:T(8,128)(2,1)S(1)}, u32[]{:S(2)}) copy-start(bf16[2,128,768]{2,1,0:T(8,128)(2,1)S(1)} %collective-permute-done.8.refs_2_) | copy-start | bytes 1179652
  88.6 51.6 %collective-permute-start.9 = (bf16[2,128,768]{2,1,0:T(8,128)(2,1)S(1)}, bf16[2,128,768]{2,1,0:T(8,128)(2,1)}, u32[]{:S(2)}, u32[]{:S(2)}) collective-permute-start(bf16[2,128,768]{2,1,0:T(8,128)(2,1)S(1)} %add_convert_fusion.6), channel_id=1, source_target_pairs={{8,0},{16,24},{9,1},{17,25},{10,2},{18,26},{11,3},{19,27},{12,4},{... | collective-permute-start | bytes 1179656 | tf_op jit(solution)/shard_map/ppermute | solution.py:236
  89.9 35.4 %copy-start.17 = (bf16[2,128,512]{2,1,0:T(8,128)(2,1)}, bf16[2,128,512]{2,1,0:T(8,128)(2,1)S(1)}, u32[]{:S(2)}) copy-start(bf16[2,128,512]{2,1,0:T(8,128)(2,1)S(1)} %collective-permute-done.5.refs_2_) | copy-start | bytes 786436
  90.0 55.8 %collective-permute-start.6 = (bf16[2,128,512]{2,1,0:T(8,128)(2,1)S(1)}, bf16[2,128,512]{2,1,0:T(8,128)(2,1)S(1)}, u32[]{:S(2)}, u32[]{:S(2)}) collective-permute-start(bf16[2,128,512]{2,1,0:T(8,128)(2,1)S(1)} %add_convert_fusion.8), channel_id=1, source_target_pairs={{8,0},{16,24},{9,1},{17,25},{10,2},{18,26},{11,3},{19,27},{12,4},{... | collective-permute-start | bytes 786440 | tf_op jit(solution)/shard_map/ppermute | solution.py:236
  150.6 20.7 %collective-permute-start.19 = (f32[64,2048]{1,0:T(8,128)}, f32[64,2048]{1,0:T(8,128)S(1)}, u32[]{:S(2)}, u32[]{:S(2)}) collective-permute-start(f32[64,2048]{1,0:T(8,128)} %get-tuple-element.68), channel_id=1, source_target_pairs={{0,1},{1,0},{2,3},{3,2},{4,5},{5,4},{6,7},{7,6},{8,9},{9,8},{10,11... | collective-permute-start | bytes 1572872 | tf_op jit(solution)/shard_map/ppermute | solution.py:225
  171.4 13.6 %collective-permute-start.20 = (bf16[16,2048]{1,0:T(8,128)(2,1)S(1)}, bf16[16,2048]{1,0:T(8,128)(2,1)S(1)}, u32[]{:S(2)}, u32[]{:S(2)}) collective-permute-start(bf16[16,2048]{1,0:T(8,128)(2,1)S(1)} %get-tuple-element.91), channel_id=1, source_target_pairs={{0,2},{1,3},{2,0},{3,1},{4,6},{5,7},{6,4},{7,5},{8,10},{9,11},{10,... | collective-permute-start | bytes 196616 | tf_op jit(solution)/shard_map/ppermute | solution.py:230
  172.7 12.3 %collective-permute-start.21 = (bf16[16,2048]{1,0:T(8,128)(2,1)S(1)}, bf16[16,2048]{1,0:T(8,128)(2,1)S(1)}, u32[]{:S(2)}, u32[]{:S(2)}) collective-permute-start(bf16[16,2048]{1,0:T(8,128)(2,1)S(1)} %get-tuple-element.93), channel_id=1, source_target_pairs={{0,4},{1,5},{2,6},{3,7},{4,0},{5,1},{6,2},{7,3},{8,12},{9,13},{10,... | collective-permute-start | bytes 196616 | tf_op jit(solution)/shard_map/ppermute | solution.py:230
  173.5 11.5 %collective-permute-start.22 = (bf16[16,2048]{1,0:T(8,128)(2,1)S(1)}, bf16[16,2048]{1,0:T(8,128)(2,1)S(1)}, u32[]{:S(2)}, u32[]{:S(2)}) collective-permute-start(bf16[16,2048]{1,0:T(8,128)(2,1)S(1)} %get-tuple-element.92), channel_id=1, source_target_pairs={{0,6},{1,7},{2,4},{3,5},{4,2},{5,3},{6,0},{7,1},{8,14},{9,15},{10,... | collective-permute-start | bytes 196616 | tf_op jit(solution)/shard_map/ppermute | solution.py:230
  (14 other events, 132.2 us)

commit v2 on v1

v2 whole, which is shorter than its diff:
```python
import functools

import jax
import jax.numpy as jnp
from jax import lax
from jax.experimental import pallas as pl
from jax.experimental.pallas import tpu as pltpu
from jax.sharding import PartitionSpec as P


BLOCK = 128
SUB = 16
PAIR = 2
VMEM_LIMIT = 24 * 1024 * 1024
PARAMS = pltpu.CompilerParams(vmem_limit_bytes=VMEM_LIMIT)
SHARES = (3, 5, 5, 3)
GROUPS = (1, 1, 1, 1)
LATE = 1
BAND = 4
ROOT = 0.7978845608028654
CUBE = 0.044715


def chunk_steps(steps):
    total = sum(SHARES)
    edges = [0]
    run = 0
    for share in SHARES:
        run += share
        edge = (run * steps) // total
        if edge > edges[-1]:
            edges.append(edge)
    return [(a, b - a) for a, b in zip(edges[:-1], edges[1:])]


def tile_mask(block_index, row_blocks, col_blocks):
    row_place = lax.axis_index("row")
    col_place = lax.axis_index("col")
    own_rows = lax.dynamic_slice_in_dim(block_index, row_place * row_blocks, row_blocks, 0)
    own_cols = col_place * col_blocks + jnp.arange(col_blocks, dtype=jnp.int32)
    return jnp.any(own_rows[:, :, None] == own_cols[None, None, :], axis=1)


def masked(block, mask_ref, first, cut=slice(None)):
    rows, width = block.shape
    parts = []
    for g in range(rows // BLOCK):
        row = jnp.broadcast_to(mask_ref[first + g:first + g + 1, cut], (SUB, width)).astype(block.dtype)
        part = block[g * BLOCK:(g + 1) * BLOCK].reshape(BLOCK // SUB, SUB, width) * row[None]
        parts.append(part.reshape(BLOCK, width))
    return jnp.concatenate(parts, axis=0) if len(parts) > 1 else parts[0]


def dot(a, b, dims=((1,), (0,))):
    return lax.dot_general(a, b, (dims, ((), ())), preferred_element_type=jnp.float32)


def forward(pair, up, down, mu, md, first, counts, width):
    _, tokens, feats = pair.shape
    blocks = width // BLOCK
    steps = sum(counts)
    edges = [sum(counts[:k]) for k in range(len(counts))]

    def body(pair_ref, up_ref, down_ref, mu_ref, md_ref, *out_refs):
        step = pl.program_id(0)
        hidden = dot(pair_ref[0], masked(up_ref[...], mu_ref, 0))
        grad = dot(pair_ref[1], masked(down_ref[...], md_ref.at[0], 0), ((1,), (1,)))
        for k, (edge, count) in enumerate(zip(edges, counts)):
            def put(k=k):
                own_ref, send_ref = out_refs[2 * k:2 * k + 2]
                own_ref[0] = hidden
                own_ref[1] = grad
                send_ref[0] = hidden.astype(send_ref.dtype)
                send_ref[1] = grad.astype(send_ref.dtype)

            if len(counts) == 1:
                put()
            else:
                pl.when((step >= edge) & (step < edge + count))(put)

    def part(edge, count):
        return pl.BlockSpec((2, tokens, width), lambda j: (0, 0, jnp.clip(j - edge, 0, count - 1)))

    out_specs, out_shape = [], []
    for edge, count in zip(edges, counts):
        for kind in (jnp.float32, jnp.bfloat16):
            out_specs.append(part(edge, count))
            out_shape.append(jax.ShapeDtypeStruct((2, tokens, count * width), kind))
    return pl.pallas_call(
        body,
        grid=(steps,),
        in_specs=[
            pl.BlockSpec((2, tokens, feats), lambda j: (0, 0, 0)),
            pl.BlockSpec((feats, width), lambda j: (0, first + j)),
            pl.BlockSpec((width, feats), lambda j: (first + j, 0)),
            pl.BlockSpec((feats // BLOCK, width), lambda j: (0, first + j)),
            pl.BlockSpec((1, blocks, feats), lambda j: (first + j, 0, 0)),
        ],
        out_specs=out_specs,
        out_shape=out_shape,
        compiler_params=PARAMS,
        cost_estimate=pl.CostEstimate(
            flops=4 * tokens * feats * width * steps,
            bytes_accessed=4 * feats * width * steps + 4 * tokens * feats,
            transcendentals=0,
        ),
        name="forward",
    )(pair, up, down, mu, md)


def finish(v, g):
    square = v * v
    t = jnp.tanh(v * (ROOT + (ROOT * CUBE) * square))
    half = 0.5 + 0.5 * t
    slope = half + (0.5 * v) * ((1.0 - t) * (1.0 + t)) * (ROOT + (3.0 * ROOT * CUBE) * square)
    return v * half, g * slope


def chunk_kernel(own, came, up, mu, state, grads, weights, first, count, width):
    _, tokens, chunk = own.shape
    feats, units = up.shape
    blocks = width // BLOCK
    rows = tokens // 2
    n_came = len(came)

    def body(*refs):
        refs = list(refs)
        own_ref = refs.pop(0)
        came_refs = [refs.pop(0) for _ in range(n_came)]
        up_ref, mu_ref = refs.pop(0), refs.pop(0)
        lo_in, hi_in = (refs.pop(0), refs.pop(0)) if state else (None, None)
        if weights:
            tokt_ref, cot_ref, md_ref = refs[:3]
        lo_ref, hi_ref, one_ref, two_ref = refs[-4:]

        @pl.when(pl.program_id(0) == 0)
        def _():
            lo_ref[...] = lo_in[...] if state else jnp.zeros_like(lo_ref)
            hi_ref[...] = hi_in[...] if state else jnp.zeros_like(hi_ref)

        def total(k):
            value = own_ref[k]
            for ref in came_refs:
                value += ref[k].astype(jnp.float32)
            return value

        act, grad = finish(total(0), total(1))
        hgrad = grad.astype(jnp.bfloat16)
        if weights:
            act_t = act.T.astype(jnp.bfloat16)
        else:
            one_ref[...] = act.astype(jnp.bfloat16)
            two_ref[...] = hgrad
        band = min(feats, BAND * BLOCK)
        for b in range(feats // band):
            cut = slice(b * band, (b + 1) * band)
            at = b * (band // BLOCK)
            part = dot(hgrad, masked(up_ref[cut, :], mu_ref, at), ((1,), (1,)))
            lo_ref[:, cut] += part[:rows]
            hi_ref[:, cut] += part[rows:]
            if weights:
                one_ref[cut, :] = masked(dot(tokt_ref[cut, :], hgrad).astype(jnp.bfloat16), mu_ref, at)
                two_ref[:, cut] = masked(dot(act_t, cot_ref[0, :, cut]).astype(jnp.bfloat16), md_ref.at[0], 0, cut)

    part = pl.BlockSpec((2, tokens, width), lambda j: (0, 0, j))
    half_spec = pl.BlockSpec((rows, feats), lambda j: (0, 0))
    half_shape = jax.ShapeDtypeStruct((rows, feats), jnp.float32)
    in_specs = [
        *([part] * (1 + n_came)),
        pl.BlockSpec((feats, width), lambda j: (0, first + j)),
        pl.BlockSpec((feats // BLOCK, width), lambda j: (0, first + j)),
        *([half_spec] * (2 if state else 0)),
    ]
    operands = [own, *came, up, mu, *(state or ())]
    aliases = {}
    if weights:
        in_specs += weight_in_specs(tokens, feats, blocks, first)
        operands += weights
        if grads:
            aliases = {len(operands): 2, len(operands) + 1: 3}
            in_specs += [pl.BlockSpec(memory_space=pl.ANY)] * 2
            operands += grads
        out_specs, out_shape = weight_outs(feats, units, first, width)
    else:
        out_specs = [pl.BlockSpec((tokens, width), lambda j: (0, j))] * 2
        out_shape = [jax.ShapeDtypeStruct((tokens, chunk), jnp.bfloat16)] * 2
    times = 3 if weights else 1
    return pl.pallas_call(
        body,
        grid=(count,),
        in_specs=in_specs,
        out_specs=[half_spec, half_spec, *out_specs],
        out_shape=[half_shape, half_shape, *out_shape],
        input_output_aliases=aliases,
        compiler_params=PARAMS,
        cost_estimate=pl.CostEstimate(
            flops=2 * times * tokens * feats * chunk,
            bytes_accessed=2 * times * feats * chunk + 8 * tokens * feats,
            transcendentals=tokens * chunk,
        ),
        name="chunk",
    )(*operands)


def weight_in_specs(tokens, feats, blocks, first):
    return [
        pl.BlockSpec((feats, tokens), lambda j: (0, 0)),
        pl.BlockSpec((1, tokens, feats), lambda j: (1, 0, 0)),
        pl.BlockSpec((1, blocks, feats), lambda j: (first + j, 0, 0)),
    ]


def weight_outs(feats, units, first, width):
    specs = [
        pl.BlockSpec((feats, width), lambda j: (0, first + j)),
        pl.BlockSpec((width, feats), lambda j: (first + j, 0)),
    ]
    return specs, [pltpu.HBM((feats, units), jnp.bfloat16), pltpu.HBM((units, feats), jnp.bfloat16)]


def weight_grads(act, hgrad, mu, weights, grads, units, first, count, width):
    tokens, feats = weights[1].shape[1:]

    def body(tokt_ref, cot_ref, md_ref, act_ref, hgrad_ref, mu_ref, *refs):
        upg_ref, dng_ref = refs[-2:]
        hgrad = hgrad_ref[...]
        act_t = act_ref[...].astype(jnp.float32).T.astype(jnp.bfloat16)
        band = min(feats, BAND * BLOCK)
        for b in range(feats // band):
            cut = slice(b * band, (b + 1) * band)
            upg_ref[cut, :] = masked(dot(tokt_ref[cut, :], hgrad).astype(jnp.bfloat16), mu_ref, b * (band // BLOCK))
            dng_ref[:, cut] = masked(dot(act_t, cot_ref[0, :, cut]).astype(jnp.bfloat16), md_ref.at[0], 0, cut)

    part = pl.BlockSpec((tokens, width), lambda j: (0, j))
    any_spec = pl.BlockSpec(memory_space=pl.ANY)
    out_specs, out_shape = weight_outs(feats, units, first, width)
    return pl.pallas_call(
        body,
        grid=(count,),
        in_specs=[
            *weight_in_specs(tokens, feats, width // BLOCK, first),
            part,
            part,
            pl.BlockSpec((feats // BLOCK, width), lambda j: (0, first + j)),
            *([any_spec] * (2 if grads else 0)),
        ],
        out_specs=out_specs,
        out_shape=out_shape,
        input_output_aliases={6: 0, 7: 1} if grads else {},
        compiler_params=PARAMS,
        cost_estimate=pl.CostEstimate(
            flops=4 * tokens * feats * width * count,
            bytes_accessed=4 * feats * width * count + 4 * tokens * feats,
            transcendentals=0,
        ),
        name="weight_grads",
    )(*weights, act, hgrad, mu, *(grads or ()))


def xor_pairs(n, bits):
    return [(i, i ^ bits) for i in range(n)]


def gather_tokens(x, n, masks):
    if n == 1:
        return x, masks
    parts = [x] + [lax.ppermute(x, "col", xor_pairs(n, s)) for s in range(2, n, 2)]
    half = jnp.concatenate(parts, axis=1)
    half, masks = lax.optimization_barrier((half, masks))
    return jnp.concatenate([half, lax.ppermute(half, "col", xor_pairs(n, 1))], axis=1), masks


def scatter_tokens(lo, hi, n):
    mine = lo + lax.ppermute(hi, "col", xor_pairs(n, 1))
    rows = 2 * mine.shape[0] // n
    send = mine[rows:].astype(jnp.bfloat16)
    out = mine[:rows]
    for k, s in enumerate(range(2, n, 2)):
        came = lax.ppermute(send[k * rows:(k + 1) * rows], "col", xor_pairs(n, s))
        out = out + came.astype(jnp.float32)
    return out


def shift(x, pairs):
    return lax.ppermute(x, "row", pairs)


def local(rows, cols, tokens, cotangent, up_weight, down_weight, block_index):
    feats, units = up_weight.shape
    row_blocks = feats // BLOCK
    col_blocks = units // BLOCK
    hits = tile_mask(block_index, row_blocks, col_blocks).astype(jnp.float32)
    width = PAIR * BLOCK
    mu = jnp.repeat(hits, BLOCK, axis=1)
    md = jnp.repeat(hits.T, BLOCK, axis=1).reshape(units // width, PAIR, feats)
    pair, (mu, md) = gather_tokens(jnp.stack([tokens, cotangent]), cols, (mu, md))
    up_weight, down_weight = (pltpu.with_memory_space_constraint(w, pltpu.HBM) for w in (up_weight, down_weight))
    weights = [pair[0].T, pair, md]
    plan = chunk_steps(units // width)
    owns = []
    while len(owns) < len(plan):
        group = plan[len(owns):len(owns) + GROUPS[min(len(owns), len(GROUPS) - 1)]]
        outs = forward(pair, up_weight, down_weight, mu, md, group[0][0], [n for _, n in group], width)
        owns += list(zip(outs[::2], outs[1::2]))
    right = rows // 2
    sums = []
    for own, near in owns:
        came = []
        for k in range(right - 1):
            came.append(shift(near, [(k, k + 1), (rows - 1 - k, rows - 2 - k)]))
            near = (own + sum(x.astype(jnp.float32) for x in came)).astype(jnp.bfloat16)
        came.append(shift(near, [(right - 1, right), (right, right - 1)]))
        out = own + came[-1].astype(jnp.float32)
        for k in reversed(range(right - 1)):
            far = shift(out.astype(jnp.bfloat16), [(k + 1, k), (rows - 2 - k, rows - 1 - k)])
            came.append(far)
            out = out + far.astype(jnp.float32)
        sums.append((own, came))
    state = grads = None
    late = []
    for c, (first, count) in enumerate(plan):
        whole_chunk = c + LATE < len(plan)
        *state, one, two = chunk_kernel(
            *sums[c], up_weight, mu, state, grads, weights if whole_chunk else None, first, count, width
        )
        if whole_chunk:
            grads = [one, two]
        else:
            late.append((c, first, count, one, two))
    for c, first, count, act, hgrad in late:
        grads = weight_grads(act, hgrad, mu, weights, grads, units, first, count, width)
    input_grad = scatter_tokens(*state, cols)
    return (input_grad.astype(jnp.bfloat16), *grads)


def whole(rows, cols, *arrays):
    return local(rows, cols, *arrays)


def solution(mesh):
    return jax.shard_map(
        functools.partial(whole, mesh.shape["row"], mesh.shape["col"]),
        mesh=mesh,
        in_specs=(P("col", "row"), P("col", "row"), P("row", "col"), P("col", "row"), P()),
        out_specs=(P("col", "row"), P("row", "col"), P("col", "row")),
        check_vma=False,
    )
```

time: 187 us -> 142 us (0.76)
  Pallas kernels: 89 us -> 58.1 us
  waiting for transfers between devices: 53.3 us -> 43.8 us
  local copies, waits for them, and re-layouts: 8.17 us -> 4.38 us
  starting transfers between devices: 27.3 us -> 24.5 us
    pallas_call x15 -> x9, Pallas kernels: 89 us -> 58.1 us  [the longest x4 31.6 us: chunk_kernel(): pl.pallas_call(body, grid=(count,), in_specs=in_specs, out_specs=[half_sp...]
    ppermute x15 -> x12, waiting for transfers between devices: 46.1 us -> 34.9 us  [shift(): return lax.ppermute(x, 'row', pairs)]
    broadcast_in_dim x4 -> x2, local copies, waits for them, and re-layouts: 3.5 us -> 0.25 us  [the longest x1 0.13 us: local(): md = jnp.repeat(hits.T, BLOCK, axis=1).reshape(units // width, PAIR, feats)]
    ppermute x15 -> x12, starting transfers between devices: 19.1 us -> 16.2 us  [shift(): return lax.ppermute(x, 'row', pairs)]
    convert_element_type x5 -> x4, other arithmetic: 1.78 us -> 4.44 us  [local(): out.astype(jnp.bfloat16)]
    ppermute x1, waiting for transfers between devices: 0.01 us -> 1.9 us  [scatter_tokens(): mine = lo + lax.ppermute(hi, 'col', xor_pairs(n, 1))]
  transfers between devices with their start and end apart: 23 -> 20, of which waited for: 8 -> 9; matrix products, arithmetic and copies ran while one was open for 3% -> 6% of each run, Pallas kernels for 40% -> 36%
where the time goes in v2:
time: 142 us; the launch traced here: 140 us
  Pallas kernels  58.1 us (41%)
  waiting for transfers between devices  43.8 us (31%)
  starting transfers between devices  24.5 us (17%)
  other arithmetic  7.77 us (5%)
  local copies, waits for them, and re-layouts  4.38 us (3%)
    ppermute x12, waiting for transfers between devices, shift(): return lax.ppermute(x, 'row', pairs)  34.9 us
    pallas_call x4, Pallas kernels, chunk_kernel(): pl.pallas_call(body, grid=(count,), in_specs=in_specs, out_specs=[half_sp...  31.6 us
    pallas_call x4, Pallas kernels, forward(): pl.pallas_call(body, grid=(steps,), in_specs=[pl.BlockSpec((2, tokens, fe...  22.5 us
    ppermute x12, starting transfers between devices, shift(): return lax.ppermute(x, 'row', pairs)  16.2 us
    ppermute x3, waiting for transfers between devices, gather_tokens(): lax.ppermute(x, 'col', xor_pairs(n, s))  5.14 us
    ppermute x3, starting transfers between devices, gather_tokens(): lax.ppermute(x, 'col', xor_pairs(n, s))  4.57 us
    convert_element_type x4, other arithmetic, local(): out.astype(jnp.bfloat16)  4.44 us
    pallas_call x1, Pallas kernels, weight_grads(): pl.pallas_call(body, grid=(count,), in_specs=[*weight_in_specs(tokens, fe...  4.03 us
  transfers between devices with their start and end apart: 20, of which 9 were waited for; matrix products, arithmetic and copies ran while one was open for 6% of the time, Pallas kernels for 36%

profile of v2, /device:TPU:0, one launch (start us, length us, event | category | flops | bytes accessed | tf_op | source)
XLA Modules:
  0.0 139.6 jit_solution(5506049844734621482)
XLA Ops:
  1.6 3.0 %collective-permute-start = (bf16[2,16,2048]{2,1,0:T(8,128)(2,1)S(1)}, bf16[2,16,2048]{2,1,0:T(8,128)(2,1)S(1)}, u32[]{:S(2)}, u32[]{:S(2)}) collective-permute-start(bf16[2,16,2048]{2,1,0:T(8,128)(2,1)S(1)} %pad_maximum_fusion.1), channel_id=1, source_target_pairs={{0,2},{1,3},{2,0},{3,1},{4,6},{5,7},{6,4},{7,5},{8,10},{9,11},{10,... | collective-permute-start | bytes 393224 | tf_op jit(solution)/shard_map/ppermute | solution.py:267
  4.6 1.5 %collective-permute-start.1 = (bf16[2,16,2048]{2,1,0:T(8,128)(2,1)S(1)}, bf16[2,16,2048]{2,1,0:T(8,128)(2,1)S(1)}, u32[]{:S(2)}, u32[]{:S(2)}) collective-permute-start(bf16[2,16,2048]{2,1,0:T(8,128)(2,1)S(1)} %pad_maximum_fusion.1), channel_id=1, source_target_pairs={{0,4},{1,5},{2,6},{3,7},{4,0},{5,1},{6,2},{7,3},{8,12},{9,13},{10,... | collective-permute-start | bytes 393224 | tf_op jit(solution)/shard_map/ppermute | solution.py:267
  8.5 3.9 %collective-permute-done.1 = bf16[2,16,2048]{2,1,0:T(8,128)(2,1)S(1)} collective-permute-done((bf16[2,16,2048]{2,1,0:T(8,128)(2,1)S(1)}, bf16[2,16,2048]{2,1,0:T(8,128)(2,1)S(1)}, u32[]{:S(2)}, u32[]{:S(2)}) %collective-permute-start.1) | collective-permute-done | bytes 131104 | tf_op jit(solution)/shard_map/ppermute | solution.py:267
  12.6 1.8 %collective-permute-done.3 = bf16[2,64,2048]{2,1,0:T(8,128)(2,1)S(1)} collective-permute-done((bf16[2,64,2048]{2,1,0:T(8,128)(2,1)S(1)}, bf16[2,64,2048]{2,1,0:T(8,128)(2,1)S(1)}, u32[]{:S(2)}, u32[]{:S(2)}) %collective-permute-start.3) | collective-permute-done | bytes 524320 | tf_op jit(solution)/shard_map/ppermute | solution.py:270
  14.5 4.5 %forward.7 = (f32[2,128,768]{2,1,0:T(8,128)S(1)}, bf16[2,128,768]{2,1,0:T(8,128)(2,1)S(1)}) custom-call(bf16[2,128,2048]{2,1,0:T(8,128)(2,1)S(1)} %constant_dynamic-update-slice_fusion.pair_ref.refs_7_.refs_9_.cot_ref, bf16[2048,4096]{1,0:T(8,128)(2,1)} %refs_4_.7, bf16[4096,2048]{1,0:T(8,128)(2,1)} %down_ref.7, f32[16,4096]{1,0:T(8,128)S(1)} %bitcast.12, ...), custom_call_target="tpu_custom_call" | custom-call | flops 805306368 | bytes 7340032 | tf_op jit(solution)/shard_map/forward/pallas_call | solution.py:89
  19.0 3.5 %collective-permute-start.13 = (bf16[2,128,768]{2,1,0:T(8,128)(2,1)S(1)}, bf16[2,128,768]{2,1,0:T(8,128)(2,1)S(1)}, u32[]{:S(2)}, u32[]{:S(2)}) collective-permute-start(bf16[2,128,768]{2,1,0:T(8,128)(2,1)S(1)} %get-tuple-element.42), channel_id=1, source_target_pairs={{0,8},{24,16},{1,9},{25,17},{2,10},{26,18},{3,11},{27,19},{4,12},{... | collective-permute-start | bytes 1179656 | tf_op jit(solution)/shard_map/ppermute | solution.py:285
  22.5 4.5 %forward.4 = (f32[2,128,768]{2,1,0:T(8,128)S(1)}, bf16[2,128,768]{2,1,0:T(8,128)(2,1)S(1)}) custom-call(bf16[2,128,2048]{2,1,0:T(8,128)(2,1)S(1)} %constant_dynamic-update-slice_fusion.pair_ref.refs_7_.refs_9_.cot_ref, bf16[2048,4096]{1,0:T(8,128)(2,1)} %refs_4_.7, bf16[4096,2048]{1,0:T(8,128)(2,1)} %down_ref.7, f32[16,4096]{1,0:T(8,128)S(1)} %bitcast.13, ...), custom_call_target="tpu_custom_call" | custom-call | flops 805306368 | bytes 7340032 | tf_op jit(solution)/shard_map/forward/pallas_call | solution.py:89
  27.0 1.3 collective-permute-start.4
  28.3 6.8 %forward.6 = (f32[2,128,1280]{2,1,0:T(8,128)S(1)}, bf16[2,128,1280]{2,1,0:T(8,128)(2,1)S(1)}) custom-call(bf16[2,128,2048]{2,1,0:T(8,128)(2,1)S(1)} %constant_dynamic-update-slice_fusion.pair_ref.refs_7_.refs_9_.cot_ref, bf16[2048,4096]{1,0:T(8,128)(2,1)} %refs_4_.7, bf16[4096,2048]{1,0:T(8,128)(2,1)} %down_ref.7, f32[16,4096]{1,0:T(8,128)S(1)} %bitcast.14, ...), custom_call_target="tpu_custom_call" | custom-call | flops 1342177280 | bytes 11534336 | tf_op jit(solution)/shard_map/forward/pallas_call | solution.py:89
  35.1 1.3 collective-permute-start.10
  36.4 6.8 %forward.5 = (f32[2,128,1280]{2,1,0:T(8,128)S(1)}, bf16[2,128,1280]{2,1,0:T(8,128)(2,1)S(1)}) custom-call(bf16[2,128,2048]{2,1,0:T(8,128)(2,1)S(1)} %constant_dynamic-update-slice_fusion.pair_ref.refs_7_.refs_9_.cot_ref, bf16[2048,4096]{1,0:T(8,128)(2,1)} %refs_4_.7, bf16[4096,2048]{1,0:T(8,128)(2,1)} %down_ref.7, f32[16,4096]{1,0:T(8,128)S(1)} %bitcast.15, ...), custom_call_target="tpu_custom_call" | custom-call | flops 1342177280 | bytes 11534336 | tf_op jit(solution)/shard_map/forward/pallas_call | solution.py:89
  43.2 1.3 collective-permute-start.7
  46.2 1.4 %collective-permute-start.5 = (bf16[2,128,768]{2,1,0:T(8,128)(2,1)}, bf16[2,128,768]{2,1,0:T(8,128)(2,1)}, u32[]{:S(2)}, u32[]{:S(2)}) collective-permute-start(bf16[2,128,768]{2,1,0:T(8,128)(2,1)} %add_convert_fusion.7), channel_id=1, source_target_pairs={{8,16},{16,8},{9,17},{17,9},{10,18},{18,10},{11,19},{19,11},{12,20... | collective-permute-start | bytes 1179656 | tf_op jit(solution)/shard_map/ppermute | solution.py:285
  47.7 6.8 %collective-permute-done.10.refs_1_ = bf16[2,128,1280]{2,1,0:T(8,128)(2,1)S(1)} collective-permute-done((bf16[2,128,1280]{2,1,0:T(8,128)(2,1)S(1)}, bf16[2,128,1280]{2,1,0:T(8,128)(2,1)S(1)}, u32[]{:S(2)}, u32[]{:S(2)}) %collective-permute-start.10) | collective-permute-done | bytes 655392 | tf_op jit(solution)/shard_map/ppermute | solution.py:285
  56.0 11.7 %collective-permute-done.7.refs_1_ = bf16[2,128,1280]{2,1,0:T(8,128)(2,1)S(1)} collective-permute-done((bf16[2,128,1280]{2,1,0:T(8,128)(2,1)S(1)}, bf16[2,128,1280]{2,1,0:T(8,128)(2,1)S(1)}, u32[]{:S(2)}, u32[]{:S(2)}) %collective-permute-start.7) | collective-permute-done | bytes 655392 | tf_op jit(solution)/shard_map/ppermute | solution.py:285
  70.1 1.3 collective-permute-start.15
  72.5 1.3 collective-permute-start.12
  74.9 1.3 collective-permute-start.9
  77.0 1.3 copy.20.refs_6_.refs_8_.tokt_ref
  78.4 1.4 %add_convert_fusion.6 = bf16[2,128,768]{2,1,0:T(8,128)(2,1)S(1)} fusion(f32[2,128,768]{2,1,0:T(8,128)} %copy-done.4, bf16[2,128,768]{2,1,0:T(8,128)(2,1)} %collective-permute-done.5.refs_2_), kind=kLoop, calls=%fused_computation.6 | loop fusion | flops 589824 | bytes 1572864 | tf_op jit(solution)/shard_map/convert_element_type | solution.py:315
  79.8 1.4 %collective-permute-start.6 = (bf16[2,128,768]{2,1,0:T(8,128)(2,1)S(1)}, bf16[2,128,768]{2,1,0:T(8,128)(2,1)S(1)}, u32[]{:S(2)}, u32[]{:S(2)}) collective-permute-start(bf16[2,128,768]{2,1,0:T(8,128)(2,1)S(1)} %add_convert_fusion.6), channel_id=1, source_target_pairs={{8,0},{16,24},{9,1},{17,25},{10,2},{18,26},{11,3},{19,27},{12,4},{... | collective-permute-start | bytes 1179656 | tf_op jit(solution)/shard_map/ppermute | solution.py:285
  81.2 5.7 %collective-permute-done.15.refs_3_ = bf16[2,128,768]{2,1,0:T(8,128)(2,1)} collective-permute-done((bf16[2,128,768]{2,1,0:T(8,128)(2,1)}, bf16[2,128,768]{2,1,0:T(8,128)(2,1)}, u32[]{:S(2)}, u32[]{:S(2)}) %collective-permute-start.15) | collective-permute-done | bytes 393248 | tf_op jit(solution)/shard_map/ppermute | solution.py:285
  86.9 7.0 %chunk.4 = (f32[64,2048]{1,0:T(8,128)S(1)}, f32[64,2048]{1,0:T(8,128)S(1)}, bf16[2048,4096]{1,0:T(8,128)(2,1)}, bf16[4096,2048]{1,0:T(8,128)(2,1)}) custom-call(f32[2,128,768]{2,1,0:T(8,128)S(1)} %copy-done.7, bf16[2,128,768]{2,1,0:T(8,128)(2,1)S(1)} %copy-done.19, bf16[2,128,768]{2,1,0:T(8,128)(2,1)S(1)} %copy-done.21, ...), custom_call_target="tpu_custom_call" | custom-call | flops 1207959552 | bytes 11534336 | tf_op jit(solution)/shard_map/chunk/pallas_call | solution.py:188
  93.9 7.0 %collective-permute-done.12.refs_3_ = bf16[2,128,1280]{2,1,0:T(8,128)(2,1)} collective-permute-done((bf16[2,128,1280]{2,1,0:T(8,128)(2,1)}, bf16[2,128,1280]{2,1,0:T(8,128)(2,1)}, u32[]{:S(2)}, u32[]{:S(2)}) %collective-permute-start.12) | collective-permute-done | bytes 655392 | tf_op jit(solution)/shard_map/ppermute | solution.py:285
  101.0 10.3 %chunk.5 = (f32[64,2048]{1,0:T(8,128)S(1)}, f32[64,2048]{1,0:T(8,128)S(1)}, bf16[2048,4096]{1,0:T(8,128)(2,1)}, bf16[4096,2048]{1,0:T(8,128)(2,1)}) custom-call(f32[2,128,1280]{2,1,0:T(8,128)S(1)} %copy-done.3, bf16[2,128,1280]{2,1,0:T(8,128)(2,1)S(1)} %copy-done.11, ...), custom_call_target="tpu_custom_call", output_to_operand_aliasing={{2}: (11, {}), {3}: (12, {})} | custom-call | flops 2013265920 | bytes 17825792 | tf_op jit(solution)/shard_map/chunk/pallas_call | solution.py:188
  111.3 3.7 %collective-permute-done.9.refs_3_ = bf16[2,128,1280]{2,1,0:T(8,128)(2,1)} collective-permute-done((bf16[2,128,1280]{2,1,0:T(8,128)(2,1)}, bf16[2,128,1280]{2,1,0:T(8,128)(2,1)}, u32[]{:S(2)}, u32[]{:S(2)}) %collective-permute-start.9) | collective-permute-done | bytes 655392 | tf_op jit(solution)/shard_map/ppermute | solution.py:285
  115.0 10.3 %chunk.6 = (f32[64,2048]{1,0:T(8,128)S(1)}, f32[64,2048]{1,0:T(8,128)S(1)}, bf16[2048,4096]{1,0:T(8,128)(2,1)}, bf16[4096,2048]{1,0:T(8,128)(2,1)}) custom-call(f32[2,128,1280]{2,1,0:T(8,128)S(1)} %get-tuple-element.37.refs_0_, bf16[2,128,1280]{2,1,0:T(8,128)(2,1)S(1)} %copy-done.9, ...), custom_call_target="tpu_custom_call", output_to_operand_aliasing={{2}: (11, {}), {3}: (12, {})} | custom-call | flops 2013265920 | bytes 17825792 | tf_op jit(solution)/shard_map/chunk/pallas_call | solution.py:188
  125.4 3.9 %chunk.7 = (f32[64,2048]{1,0:T(8,128)S(1)}, f32[64,2048]{1,0:T(8,128)S(1)}, bf16[128,768]{1,0:T(8,128)(2,1)S(1)}, bf16[128,768]{1,0:T(8,128)(2,1)S(1)}) custom-call(f32[2,128,768]{2,1,0:T(8,128)S(1)} %copy-done.5, bf16[2,128,768]{2,1,0:T(8,128)(2,1)S(1)} %copy-done.17, bf16[2,128,768]{2,1,0:T(8,128)(2,1)} %collective-permute-done.5.refs_2_, ...), custom_call_target="tpu_custom_call" | custom-call | flops 402653184 | bytes 5242880 | tf_op jit(solution)/shard_map/chunk/pallas_call | solution.py:188
  129.4 1.9 %collective-permute-done.16 = f32[64,2048]{1,0:T(8,128)S(1)} collective-permute-done((f32[64,2048]{1,0:T(8,128)S(1)}, f32[64,2048]{1,0:T(8,128)S(1)}, u32[]{:S(2)}, u32[]{:S(2)}) %collective-permute-start.16) | collective-permute-done | bytes 524320 | tf_op jit(solution)/shard_map/ppermute | solution.py:274
  131.4 1.3 collective-permute-start.17
  133.5 1.4 %collective-permute-start.19 = (bf16[16,2048]{1,0:T(8,128)(2,1)S(1)}, bf16[16,2048]{1,0:T(8,128)(2,1)S(1)}, u32[]{:S(2)}, u32[]{:S(2)}) collective-permute-start(bf16[16,2048]{1,0:T(8,128)(2,1)S(1)} %get-tuple-element.64), channel_id=1, source_target_pairs={{0,6},{1,7},{2,4},{3,5},{4,2},{5,3},{6,0},{7,1},{8,14},{9,15},{10,... | collective-permute-start | bytes 196616 | tf_op jit(solution)/shard_map/ppermute | solution.py:279
  134.9 4.0 %weight_grads.1 = (bf16[2048,4096]{1,0:T(8,128)(2,1)}, bf16[4096,2048]{1,0:T(8,128)(2,1)}) custom-call(bf16[2048,128]{1,0:T(8,128)(2,1)S(1)} %copy.20.refs_6_.refs_8_.tokt_ref, bf16[2,128,2048]{2,1,0:T(8,128)(2,1)S(1)} %constant_dynamic-update-slice_fusion.pair_ref.refs_7_.refs_9_.cot_ref, ...), custom_call_target="tpu_custom_call", output_to_operand_aliasing={{0}: (6, {}), {1}: (7, {})} | custom-call | flops 805306368 | bytes 7340032 | tf_op jit(solution)/shard_map/weight_grads/pallas_call | solution.py:237
  (91 shorter events, 13.8 us)
Async XLA Ops:
  0.6 11.8 %copy-start.23 = (bf16[16,2048]{1,0:T(8,128)(2,1)S(1)}, bf16[16,2048]{1,0:T(8,128)(2,1)}, u32[]{:S(2)}) copy-start(bf16[16,2048]{1,0:T(8,128)(2,1)} %param.5) | copy-start | bytes 196612
  0.7 11.8 %copy-start.22 = (bf16[16,2048]{1,0:T(8,128)(2,1)S(1)}, bf16[16,2048]{1,0:T(8,128)(2,1)}, u32[]{:S(2)}) copy-start(bf16[16,2048]{1,0:T(8,128)(2,1)} %param.6) | copy-start | bytes 196612
  1.6 6.9 %collective-permute-start = (bf16[2,16,2048]{2,1,0:T(8,128)(2,1)S(1)}, bf16[2,16,2048]{2,1,0:T(8,128)(2,1)S(1)}, u32[]{:S(2)}, u32[]{:S(2)}) collective-permute-start(bf16[2,16,2048]{2,1,0:T(8,128)(2,1)S(1)} %pad_maximum_fusion.1), channel_id=1, source_target_pairs={{0,2},{1,3},{2,0},{3,1},{4,6},{5,7},{6,4},{7,5},{8,10},{9,11},{10,... | collective-permute-start | bytes 393224 | tf_op jit(solution)/shard_map/ppermute | solution.py:267
  4.6 7.8 %collective-permute-start.1 = (bf16[2,16,2048]{2,1,0:T(8,128)(2,1)S(1)}, bf16[2,16,2048]{2,1,0:T(8,128)(2,1)S(1)}, u32[]{:S(2)}, u32[]{:S(2)}) collective-permute-start(bf16[2,16,2048]{2,1,0:T(8,128)(2,1)S(1)} %pad_maximum_fusion.1), channel_id=1, source_target_pairs={{0,4},{1,5},{2,6},{3,7},{4,0},{5,1},{6,2},{7,3},{8,12},{9,13},{10,... | collective-permute-start | bytes 393224 | tf_op jit(solution)/shard_map/ppermute | solution.py:267
  6.1 6.3 %collective-permute-start.2 = (bf16[2,16,2048]{2,1,0:T(8,128)(2,1)S(1)}, bf16[2,16,2048]{2,1,0:T(8,128)(2,1)S(1)}, u32[]{:S(2)}, u32[]{:S(2)}) collective-permute-start(bf16[2,16,2048]{2,1,0:T(8,128)(2,1)S(1)} %pad_maximum_fusion.1), channel_id=1, source_target_pairs={{0,6},{1,7},{2,4},{3,5},{4,2},{5,3},{6,0},{7,1},{8,14},{9,15},{10,... | collective-permute-start | bytes 393224 | tf_op jit(solution)/shard_map/ppermute | solution.py:267
  12.5 2.0 %collective-permute-start.3 = (bf16[2,64,2048]{2,1,0:T(8,128)(2,1)S(1)}, bf16[2,64,2048]{2,1,0:T(8,128)(2,1)S(1)}, u32[]{:S(2)}, u32[]{:S(2)}) collective-permute-start(bf16[2,64,2048]{2,1,0:T(8,128)(2,1)S(1)} %pad_maximum_fusion), channel_id=1, source_target_pairs={{0,1},{1,0},{2,3},{3,2},{4,5},{5,4},{6,7},{7,6},{8,9},{9,8},{10,11... | collective-permute-start | bytes 1572872 | tf_op jit(solution)/shard_map/ppermute | solution.py:270
  19.0 50.2 %copy-start.6 = (f32[2,128,768]{2,1,0:T(8,128)}, f32[2,128,768]{2,1,0:T(8,128)S(1)}, u32[]{:S(2)}) copy-start(f32[2,128,768]{2,1,0:T(8,128)S(1)} %get-tuple-element.41.refs_0_) | copy-start | bytes 2359300
  19.0 25.5 %collective-permute-start.13 = (bf16[2,128,768]{2,1,0:T(8,128)(2,1)S(1)}, bf16[2,128,768]{2,1,0:T(8,128)(2,1)S(1)}, u32[]{:S(2)}, u32[]{:S(2)}) collective-permute-start(bf16[2,128,768]{2,1,0:T(8,128)(2,1)S(1)} %get-tuple-element.42), channel_id=1, source_target_pairs={{0,8},{24,16},{1,9},{25,17},{2,10},{26,18},{3,11},{27,19},{4,12},{... | collective-permute-start | bytes 1179656 | tf_op jit(solution)/shard_map/ppermute | solution.py:285
  27.0 18.4 %copy-start.4 = (f32[2,128,768]{2,1,0:T(8,128)}, f32[2,128,768]{2,1,0:T(8,128)S(1)}, u32[]{:S(2)}) copy-start(f32[2,128,768]{2,1,0:T(8,128)S(1)} %get-tuple-element.35.refs_0_) | copy-start | bytes 2359300
  27.0 18.3 %collective-permute-start.4 = (bf16[2,128,768]{2,1,0:T(8,128)(2,1)S(1)}, bf16[2,128,768]{2,1,0:T(8,128)(2,1)S(1)}, u32[]{:S(2)}, u32[]{:S(2)}) collective-permute-start(bf16[2,128,768]{2,1,0:T(8,128)(2,1)S(1)} %get-tuple-element.36), channel_id=1, source_target_pairs={{0,8},{24,16},{1,9},{25,17},{2,10},{26,18},{3,11},{27,19},{4,12},{... | collective-permute-start | bytes 1179656 | tf_op jit(solution)/shard_map/ppermute | solution.py:285
  35.1 36.3 %copy-start.2 = (f32[2,128,1280]{2,1,0:T(8,128)}, f32[2,128,1280]{2,1,0:T(8,128)S(1)}, u32[]{:S(2)}) copy-start(f32[2,128,1280]{2,1,0:T(8,128)S(1)} %get-tuple-element.39.refs_0_) | copy-start | bytes 3932164
  35.1 19.3 %collective-permute-start.10 = (bf16[2,128,1280]{2,1,0:T(8,128)(2,1)S(1)}, bf16[2,128,1280]{2,1,0:T(8,128)(2,1)S(1)}, u32[]{:S(2)}, u32[]{:S(2)}) collective-permute-start(bf16[2,128,1280]{2,1,0:T(8,128)(2,1)S(1)} %get-tuple-element.40), channel_id=1, source_target_pairs={{0,8},{24,16},{1,9},{25,17},{2,10},{26,18},{3,11},{27,19},{4,12},{... | collective-permute-start | bytes 1966088 | tf_op jit(solution)/shard_map/ppermute | solution.py:285
  43.2 24.5 %collective-permute-start.7 = (bf16[2,128,1280]{2,1,0:T(8,128)(2,1)S(1)}, bf16[2,128,1280]{2,1,0:T(8,128)(2,1)S(1)}, u32[]{:S(2)}, u32[]{:S(2)}) collective-permute-start(bf16[2,128,1280]{2,1,0:T(8,128)(2,1)S(1)} %get-tuple-element.38), channel_id=1, source_target_pairs={{0,8},{24,16},{1,9},{25,17},{2,10},{26,18},{3,11},{27,19},{4,12},{... | collective-permute-start | bytes 1966088 | tf_op jit(solution)/shard_map/ppermute | solution.py:285
  44.6 24.6 %collective-permute-start.14 = (bf16[2,128,768]{2,1,0:T(8,128)(2,1)S(1)}, bf16[2,128,768]{2,1,0:T(8,128)(2,1)S(1)}, u32[]{:S(2)}, u32[]{:S(2)}) collective-permute-start(bf16[2,128,768]{2,1,0:T(8,128)(2,1)S(1)} %add_convert_fusion.5), channel_id=1, source_target_pairs={{8,16},{16,8},{9,17},{17,9},{10,18},{18,10},{11,19},{19,11},{12,20... | collective-permute-start | bytes 1179656 | tf_op jit(solution)/shard_map/ppermute | solution.py:285
  46.2 32.1 %collective-permute-start.5 = (bf16[2,128,768]{2,1,0:T(8,128)(2,1)}, bf16[2,128,768]{2,1,0:T(8,128)(2,1)}, u32[]{:S(2)}, u32[]{:S(2)}) collective-permute-start(bf16[2,128,768]{2,1,0:T(8,128)(2,1)} %add_convert_fusion.7), channel_id=1, source_target_pairs={{8,16},{16,8},{9,17},{17,9},{10,18},{18,10},{11,19},{19,11},{12,20... | collective-permute-start | bytes 1179656 | tf_op jit(solution)/shard_map/ppermute | solution.py:285
  55.3 16.1 %collective-permute-start.11 = (bf16[2,128,1280]{2,1,0:T(8,128)(2,1)S(1)}, bf16[2,128,1280]{2,1,0:T(8,128)(2,1)S(1)}, u32[]{:S(2)}, u32[]{:S(2)}) collective-permute-start(bf16[2,128,1280]{2,1,0:T(8,128)(2,1)S(1)} %add_convert_fusion.1), channel_id=1, source_target_pairs={{8,16},{16,8},{9,17},{17,9},{10,18},{18,10},{11,19},{19,11},{12,20... | collective-permute-start | bytes 1966088 | tf_op jit(solution)/shard_map/ppermute | solution.py:285
  68.5 5.3 %collective-permute-start.8 = (bf16[2,128,1280]{2,1,0:T(8,128)(2,1)S(1)}, bf16[2,128,1280]{2,1,0:T(8,128)(2,1)S(1)}, u32[]{:S(2)}, u32[]{:S(2)}) collective-permute-start(bf16[2,128,1280]{2,1,0:T(8,128)(2,1)S(1)} %add_convert_fusion.3), channel_id=1, source_target_pairs={{8,16},{16,8},{9,17},{17,9},{10,18},{18,10},{11,19},{19,11},{12,20... | collective-permute-start | bytes 1966088 | tf_op jit(solution)/shard_map/ppermute | solution.py:285
  70.1 16.8 %collective-permute-start.15 = (bf16[2,128,768]{2,1,0:T(8,128)(2,1)}, bf16[2,128,768]{2,1,0:T(8,128)(2,1)}, u32[]{:S(2)}, u32[]{:S(2)}) collective-permute-start(bf16[2,128,768]{2,1,0:T(8,128)(2,1)} %add_convert_fusion.4), channel_id=1, source_target_pairs={{8,0},{16,24},{9,1},{17,25},{10,2},{18,26},{11,3},{19,27},{12,4},{... | collective-permute-start | bytes 1179656 | tf_op jit(solution)/shard_map/ppermute | solution.py:285
  72.5 28.5 %collective-permute-start.12 = (bf16[2,128,1280]{2,1,0:T(8,128)(2,1)}, bf16[2,128,1280]{2,1,0:T(8,128)(2,1)}, u32[]{:S(2)}, u32[]{:S(2)}) collective-permute-start(bf16[2,128,1280]{2,1,0:T(8,128)(2,1)} %add_convert_fusion), channel_id=1, source_target_pairs={{8,0},{16,24},{9,1},{17,25},{10,2},{18,26},{11,3},{19,27},{12,4},{... | collective-permute-start | bytes 1966088 | tf_op jit(solution)/shard_map/ppermute | solution.py:285
  74.9 40.1 %collective-permute-start.9 = (bf16[2,128,1280]{2,1,0:T(8,128)(2,1)}, bf16[2,128,1280]{2,1,0:T(8,128)(2,1)}, u32[]{:S(2)}, u32[]{:S(2)}) collective-permute-start(bf16[2,128,1280]{2,1,0:T(8,128)(2,1)} %add_convert_fusion.2), channel_id=1, source_target_pairs={{8,0},{16,24},{9,1},{17,25},{10,2},{18,26},{11,3},{19,27},{12,4},{... | collective-permute-start | bytes 1966088 | tf_op jit(solution)/shard_map/ppermute | solution.py:285
  79.8 21.2 %copy-start.3 = (f32[2,128,1280]{2,1,0:T(8,128)S(1)}, f32[2,128,1280]{2,1,0:T(8,128)}, u32[]{:S(2)}) copy-start(f32[2,128,1280]{2,1,0:T(8,128)} %copy-done.2) | copy-start | bytes 3932164
  79.8 21.2 %copy-start.11 = (bf16[2,128,1280]{2,1,0:T(8,128)(2,1)S(1)}, bf16[2,128,1280]{2,1,0:T(8,128)(2,1)}, u32[]{:S(2)}) copy-start(bf16[2,128,1280]{2,1,0:T(8,128)(2,1)} %copy-done.10) | copy-start | bytes 1966084
  79.8 21.2 %copy-start.15 = (bf16[2,128,1280]{2,1,0:T(8,128)(2,1)S(1)}, bf16[2,128,1280]{2,1,0:T(8,128)(2,1)}, u32[]{:S(2)}) copy-start(bf16[2,128,1280]{2,1,0:T(8,128)(2,1)} %copy-done.14) | copy-start | bytes 1966084
  79.8 45.6 %collective-permute-start.6 = (bf16[2,128,768]{2,1,0:T(8,128)(2,1)S(1)}, bf16[2,128,768]{2,1,0:T(8,128)(2,1)S(1)}, u32[]{:S(2)}, u32[]{:S(2)}) collective-permute-start(bf16[2,128,768]{2,1,0:T(8,128)(2,1)S(1)} %add_convert_fusion.6), channel_id=1, source_target_pairs={{8,0},{16,24},{9,1},{17,25},{10,2},{18,26},{11,3},{19,27},{12,4},{... | collective-permute-start | bytes 1179656 | tf_op jit(solution)/shard_map/ppermute | solution.py:285
  101.0 14.0 %copy-start.9 = (bf16[2,128,1280]{2,1,0:T(8,128)(2,1)S(1)}, bf16[2,128,1280]{2,1,0:T(8,128)(2,1)}, u32[]{:S(2)}) copy-start(bf16[2,128,1280]{2,1,0:T(8,128)(2,1)} %copy-done.8) | copy-start | bytes 1966084
  101.0 14.0 %copy-start.13 = (bf16[2,128,1280]{2,1,0:T(8,128)(2,1)S(1)}, bf16[2,128,1280]{2,1,0:T(8,128)(2,1)}, u32[]{:S(2)}) copy-start(bf16[2,128,1280]{2,1,0:T(8,128)(2,1)} %copy-done.12) | copy-start | bytes 1966084
  115.0 10.3 %copy-start.5 = (f32[2,128,768]{2,1,0:T(8,128)S(1)}, f32[2,128,768]{2,1,0:T(8,128)}, u32[]{:S(2)}) copy-start(f32[2,128,768]{2,1,0:T(8,128)} %copy-done.4) | copy-start | bytes 2359300
  115.0 10.3 %copy-start.17 = (bf16[2,128,768]{2,1,0:T(8,128)(2,1)S(1)}, bf16[2,128,768]{2,1,0:T(8,128)(2,1)}, u32[]{:S(2)}) copy-start(bf16[2,128,768]{2,1,0:T(8,128)(2,1)} %copy-done.16) | copy-start | bytes 1179652
  129.3 2.0 %collective-permute-start.16 = (f32[64,2048]{1,0:T(8,128)S(1)}, f32[64,2048]{1,0:T(8,128)S(1)}, u32[]{:S(2)}, u32[]{:S(2)}) collective-permute-start(f32[64,2048]{1,0:T(8,128)S(1)} %get-tuple-element.54), channel_id=1, source_target_pairs={{0,1},{1,0},{2,3},{3,2},{4,5},{5,4},{6,7},{7,6},{8,9},{9,8},{10,11... | collective-permute-start | bytes 1572872 | tf_op jit(solution)/shard_map/ppermute | solution.py:274
  131.4 7.6 %collective-permute-start.17 = (bf16[16,2048]{1,0:T(8,128)(2,1)S(1)}, bf16[16,2048]{1,0:T(8,128)(2,1)S(1)}, u32[]{:S(2)}, u32[]{:S(2)}) collective-permute-start(bf16[16,2048]{1,0:T(8,128)(2,1)S(1)} %get-tuple-element.63), channel_id=1, source_target_pairs={{0,2},{1,3},{2,0},{3,1},{4,6},{5,7},{6,4},{7,5},{8,10},{9,11},{10,... | collective-permute-start | bytes 196616 | tf_op jit(solution)/shard_map/ppermute | solution.py:279
  132.6 6.3 %collective-permute-start.18 = (bf16[16,2048]{1,0:T(8,128)(2,1)S(1)}, bf16[16,2048]{1,0:T(8,128)(2,1)S(1)}, u32[]{:S(2)}, u32[]{:S(2)}) collective-permute-start(bf16[16,2048]{1,0:T(8,128)(2,1)S(1)} %get-tuple-element.65), channel_id=1, source_target_pairs={{0,4},{1,5},{2,6},{3,7},{4,0},{5,1},{6,2},{7,3},{8,12},{9,13},{10,... | collective-permute-start | bytes 196616 | tf_op jit(solution)/shard_map/ppermute | solution.py:279
  133.5 5.5 %collective-permute-start.19 = (bf16[16,2048]{1,0:T(8,128)(2,1)S(1)}, bf16[16,2048]{1,0:T(8,128)(2,1)S(1)}, u32[]{:S(2)}, u32[]{:S(2)}) collective-permute-start(bf16[16,2048]{1,0:T(8,128)(2,1)S(1)} %get-tuple-element.64), channel_id=1, source_target_pairs={{0,6},{1,7},{2,4},{3,5},{4,2},{5,3},{6,0},{7,1},{8,14},{9,15},{10,... | collective-permute-start | bytes 196616 | tf_op jit(solution)/shard_map/ppermute | solution.py:279
  (12 other events, 54.1 us)

commit v3 on v2

--- a/solution.py
+++ b/solution.py
@@ -11,10 +11,10 @@
 BLOCK = 128
 SUB = 16
 PAIR = 2
-VMEM_LIMIT = 24 * 1024 * 1024
+VMEM_LIMIT = 20 * 1024 * 1024
 PARAMS = pltpu.CompilerParams(vmem_limit_bytes=VMEM_LIMIT)
-SHARES = (3, 5, 5, 3)
-GROUPS = (1, 1, 1, 1)
+SHARES = (3, 4, 4, 4, 1)
+GROUPS = (1, 1, 1, 1, 1)
 LATE = 1
 BAND = 4
 ROOT = 0.7978845608028654
@@ -202,6 +202,24 @@
     )(*operands)
 
 
+def transposed(pair):
+    _, tokens, feats = pair.shape
+
+    def body(pair_ref, out_ref):
+        out_ref[...] = pair_ref[0].astype(jnp.float32).T.astype(out_ref.dtype)
+
+    return pl.pallas_call(
+        body,
+        grid=(1,),
+        in_specs=[pl.BlockSpec((1, tokens, feats), lambda j: (0, 0, 0))],
+        out_specs=pl.BlockSpec((feats, tokens), lambda j: (0, 0)),
+        out_shape=jax.ShapeDtypeStruct((feats, tokens), pair.dtype),
+        compiler_params=PARAMS,
+        cost_estimate=pl.CostEstimate(flops=0, bytes_accessed=4 * tokens * feats, transcendentals=0),
+        name="transposed",
+    )(pair)
+
+
 def weight_in_specs(tokens, feats, blocks, first):
     return [
         pl.BlockSpec((feats, tokens), lambda j: (0, 0)),
@@ -295,7 +313,8 @@
     md = jnp.repeat(hits.T, BLOCK, axis=1).reshape(units // width, PAIR, feats)
     pair, (mu, md) = gather_tokens(jnp.stack([tokens, cotangent]), cols, (mu, md))
     up_weight, down_weight = (pltpu.with_memory_space_constraint(w, pltpu.HBM) for w in (up_weight, down_weight))
-    weights = [pair[0].T, pair, md]
+    tokt = transposed(pair)
+    weights = [tokt, pair, md]
     plan = chunk_steps(units // width)
     owns = []
     while len(owns) < len(plan):

time: 142 us -> 147 us (1.035); the launches traced: 140 us -> 146 us
  waiting for transfers between devices: 43.8 us -> 57 us
  other arithmetic: 7.77 us -> 4.01 us
  local copies, waits for them, and re-layouts: 4.38 us -> 0.73 us
  starting transfers between devices: 24.5 us -> 27.1 us
  Pallas kernels: 58.1 us -> 56.4 us
    ppermute x12 -> x15, waiting for transfers between devices: 34.9 us -> 46.4 us  [shift(): return lax.ppermute(x, 'row', pairs)]
    convert_element_type x4 -> x5, other arithmetic: 4.44 us -> 0.53 us  [local(): out.astype(jnp.bfloat16)]
    ppermute x12 -> x15, starting transfers between devices: 16.2 us -> 18.8 us  [shift(): return lax.ppermute(x, 'row', pairs)]
    transpose x2 -> x0, local copies, waits for them, and re-layouts: 2.15 us -> none  [local(): weights = [pair[0].T, pair, md]]
    pallas_call x1, Pallas kernels: 4.03 us -> 2 us  [weight_grads(): pl.pallas_call(body, grid=(count,), in_specs=[*weight_in_specs(tokens, fe...]
    ppermute x3, waiting for transfers between devices: 0.01 us -> 1.72 us  [scatter_tokens(): came = lax.ppermute(send[k * rows:(k + 1) * rows], 'col', xor_pairs(n, s))]
    unnamed x50 -> x6, local copies, waits for them, and re-layouts: 1.71 us -> 0.22 us
    pallas_call x4 -> x5, Pallas kernels: 22.5 us -> 22.6 us  [forward(): pl.pallas_call(body, grid=(steps,), in_specs=[pl.BlockSpec((2, tokens, fe...]
  transfers between devices with their start and end apart: 20 -> 23, of which waited for: 9 -> 13; matrix products, arithmetic and copies ran while one was open for 6% -> 1% of each run, Pallas kernels for 36% -> 29%
where the time goes in v3:
time: 147 us; the launch traced here: 146 us
  waiting for transfers between devices  57 us (39%)
  Pallas kernels  56.4 us (38%)
  starting transfers between devices  27.1 us (18%)
  other arithmetic  4.01 us (3%)
    ppermute x15, waiting for transfers between devices, shift(): return lax.ppermute(x, 'row', pairs)  46.4 us
    pallas_call x5, Pallas kernels, chunk_kernel(): pl.pallas_call(body, grid=(count,), in_specs=in_specs, out_specs=[half_sp...  31.6 us
    pallas_call x5, Pallas kernels, forward(): pl.pallas_call(body, grid=(steps,), in_specs=[pl.BlockSpec((2, tokens, fe...  22.6 us
    ppermute x15, starting transfers between devices, shift(): return lax.ppermute(x, 'row', pairs)  18.8 us
    ppermute x3, waiting for transfers between devices, gather_tokens(): lax.ppermute(x, 'col', xor_pairs(n, s))  5.14 us
    ppermute x3, starting transfers between devices, gather_tokens(): lax.ppermute(x, 'col', xor_pairs(n, s))  4.57 us
    ppermute x3, starting transfers between devices, scatter_tokens(): came = lax.ppermute(send[k * rows:(k + 1) * rows], 'col', xor_pairs(n, s))  3.55 us
  transfers between devices with their start and end apart: 23, of which 13 were waited for; matrix products, arithmetic and copies ran while one was open for 1% of the time, Pallas kernels for 29%

profile of v3, /device:TPU:0, one launch (start us, length us, event | category | flops | bytes accessed | tf_op | source)
XLA Modules:
  0.0 146.3 jit_solution(5281737338794161579)
XLA Ops:
  1.5 3.0 %collective-permute-start = (bf16[2,16,2048]{2,1,0:T(8,128)(2,1)S(1)}, bf16[2,16,2048]{2,1,0:T(8,128)(2,1)S(1)}, u32[]{:S(2)}, u32[]{:S(2)}) collective-permute-start(bf16[2,16,2048]{2,1,0:T(8,128)(2,1)S(1)} %pad_maximum_fusion.1), channel_id=1, source_target_pairs={{0,2},{1,3},{2,0},{3,1},{4,6},{5,7},{6,4},{7,5},{8,10},{9,11},{10,... | collective-permute-start | bytes 393224 | tf_op jit(solution)/shard_map/ppermute | solution.py:285
  4.6 1.5 %collective-permute-start.1 = (bf16[2,16,2048]{2,1,0:T(8,128)(2,1)S(1)}, bf16[2,16,2048]{2,1,0:T(8,128)(2,1)S(1)}, u32[]{:S(2)}, u32[]{:S(2)}) collective-permute-start(bf16[2,16,2048]{2,1,0:T(8,128)(2,1)S(1)} %pad_maximum_fusion.1), channel_id=1, source_target_pairs={{0,4},{1,5},{2,6},{3,7},{4,0},{5,1},{6,2},{7,3},{8,12},{9,13},{10,... | collective-permute-start | bytes 393224 | tf_op jit(solution)/shard_map/ppermute | solution.py:285
  8.5 3.9 %collective-permute-done.1 = bf16[2,16,2048]{2,1,0:T(8,128)(2,1)S(1)} collective-permute-done((bf16[2,16,2048]{2,1,0:T(8,128)(2,1)S(1)}, bf16[2,16,2048]{2,1,0:T(8,128)(2,1)S(1)}, u32[]{:S(2)}, u32[]{:S(2)}) %collective-permute-start.1) | collective-permute-done | bytes 131104 | tf_op jit(solution)/shard_map/ppermute | solution.py:285
  13.4 1.8 %collective-permute-done.3 = bf16[2,64,2048]{2,1,0:T(8,128)(2,1)S(1)} collective-permute-done((bf16[2,64,2048]{2,1,0:T(8,128)(2,1)S(1)}, bf16[2,64,2048]{2,1,0:T(8,128)(2,1)S(1)}, u32[]{:S(2)}, u32[]{:S(2)}) %collective-permute-start.3) | collective-permute-done | bytes 524320 | tf_op jit(solution)/shard_map/ppermute | solution.py:288
  15.3 4.5 %forward.9 = (f32[2,128,768]{2,1,0:T(8,128)S(1)}, bf16[2,128,768]{2,1,0:T(8,128)(2,1)S(1)}) custom-call(bf16[2,128,2048]{2,1,0:T(8,128)(2,1)S(1)} %constant_dynamic-update-slice_fusion.pair_ref.refs_7_.refs_9_.cot_ref, bf16[2048,4096]{1,0:T(8,128)(2,1)} %refs_4_.9, bf16[4096,2048]{1,0:T(8,128)(2,1)} %down_ref.9, f32[16,4096]{1,0:T(8,128)S(1)} %bitcast.8, ...), custom_call_target="tpu_custom_call" | custom-call | flops 805306368 | bytes 7340032 | tf_op jit(solution)/shard_map/forward/pallas_call | solution.py:89
  19.8 5.3 %forward.8 = (f32[2,128,1024]{2,1,0:T(8,128)S(1)}, bf16[2,128,1024]{2,1,0:T(8,128)(2,1)S(1)}) custom-call(bf16[2,128,2048]{2,1,0:T(8,128)(2,1)S(1)} %constant_dynamic-update-slice_fusion.pair_ref.refs_7_.refs_9_.cot_ref, bf16[2048,4096]{1,0:T(8,128)(2,1)} %refs_4_.9, bf16[4096,2048]{1,0:T(8,128)(2,1)} %down_ref.9, f32[16,4096]{1,0:T(8,128)S(1)} %bitcast.9, ...), custom_call_target="tpu_custom_call" | custom-call | flops 1073741824 | bytes 9437184 | tf_op jit(solution)/shard_map/forward/pallas_call | solution.py:89
  25.1 2.2 %forward.5 = (f32[2,128,256]{2,1,0:T(8,128)S(1)}, bf16[2,128,256]{2,1,0:T(8,128)(2,1)S(1)}) custom-call(bf16[2,128,2048]{2,1,0:T(8,128)(2,1)S(1)} %constant_dynamic-update-slice_fusion.pair_ref.refs_7_.refs_9_.cot_ref, bf16[2048,4096]{1,0:T(8,128)(2,1)} %refs_4_.9, bf16[4096,2048]{1,0:T(8,128)(2,1)} %down_ref.9, f32[16,4096]{1,0:T(8,128)S(1)} %bitcast.10, ...), custom_call_target="tpu_custom_call" | custom-call | flops 268435456 | bytes 3145728 | tf_op jit(solution)/shard_map/forward/pallas_call | solution.py:89
  27.3 3.5 %collective-permute-start.16 = (bf16[2,128,768]{2,1,0:T(8,128)(2,1)S(1)}, bf16[2,128,768]{2,1,0:T(8,128)(2,1)S(1)}, u32[]{:S(2)}, u32[]{:S(2)}) collective-permute-start(bf16[2,128,768]{2,1,0:T(8,128)(2,1)S(1)} %get-tuple-element.50), channel_id=1, source_target_pairs={{0,8},{24,16},{1,9},{25,17},{2,10},{26,18},{3,11},{27,19},{4,12},{... | collective-permute-start | bytes 1179656 | tf_op jit(solution)/shard_map/ppermute | solution.py:303
  30.8 1.3 collective-permute-start.4
  32.1 5.3 %forward.7 = (f32[2,128,1024]{2,1,0:T(8,128)S(1)}, bf16[2,128,1024]{2,1,0:T(8,128)(2,1)S(1)}) custom-call(bf16[2,128,2048]{2,1,0:T(8,128)(2,1)S(1)} %constant_dynamic-update-slice_fusion.pair_ref.refs_7_.refs_9_.cot_ref, bf16[2048,4096]{1,0:T(8,128)(2,1)} %refs_4_.9, bf16[4096,2048]{1,0:T(8,128)(2,1)} %down_ref.9, f32[16,4096]{1,0:T(8,128)S(1)} %bitcast.11, ...), custom_call_target="tpu_custom_call" | custom-call | flops 1073741824 | bytes 9437184 | tf_op jit(solution)/shard_map/forward/pallas_call | solution.py:89
  37.4 1.3 collective-permute-start.13
  38.8 5.3 %forward.6 = (f32[2,128,1024]{2,1,0:T(8,128)S(1)}, bf16[2,128,1024]{2,1,0:T(8,128)(2,1)S(1)}) custom-call(bf16[2,128,2048]{2,1,0:T(8,128)(2,1)S(1)} %constant_dynamic-update-slice_fusion.pair_ref.refs_7_.refs_9_.cot_ref, bf16[2048,4096]{1,0:T(8,128)(2,1)} %refs_4_.9, bf16[4096,2048]{1,0:T(8,128)(2,1)} %down_ref.9, f32[16,4096]{1,0:T(8,128)S(1)} %bitcast.12, ...), custom_call_target="tpu_custom_call" | custom-call | flops 1073741824 | bytes 9437184 | tf_op jit(solution)/shard_map/forward/pallas_call | solution.py:89
  44.3 1.3 collective-permute-start.10
  45.6 1.3 collective-permute-start.7
  48.5 5.8 %collective-permute-done.13.refs_1_ = bf16[2,128,1024]{2,1,0:T(8,128)(2,1)S(1)} collective-permute-done((bf16[2,128,1024]{2,1,0:T(8,128)(2,1)S(1)}, bf16[2,128,1024]{2,1,0:T(8,128)(2,1)S(1)}, u32[]{:S(2)}, u32[]{:S(2)}) %collective-permute-start.13) | collective-permute-done | bytes 524320 | tf_op jit(solution)/shard_map/ppermute | solution.py:303
  55.2 10.4 %collective-permute-done.10.refs_1_ = bf16[2,128,1024]{2,1,0:T(8,128)(2,1)S(1)} collective-permute-done((bf16[2,128,1024]{2,1,0:T(8,128)(2,1)S(1)}, bf16[2,128,1024]{2,1,0:T(8,128)(2,1)S(1)}, u32[]{:S(2)}, u32[]{:S(2)}) %collective-permute-start.10) | collective-permute-done | bytes 524320 | tf_op jit(solution)/shard_map/ppermute | solution.py:303
  66.4 9.5 %collective-permute-done.7.refs_1_ = bf16[2,128,1024]{2,1,0:T(8,128)(2,1)S(1)} collective-permute-done((bf16[2,128,1024]{2,1,0:T(8,128)(2,1)S(1)}, bf16[2,128,1024]{2,1,0:T(8,128)(2,1)S(1)}, u32[]{:S(2)}, u32[]{:S(2)}) %collective-permute-start.7) | collective-permute-done | bytes 524320 | tf_op jit(solution)/shard_map/ppermute | solution.py:303
  76.9 1.3 collective-permute-start.18
  78.3 1.3 collective-permute-start.15
  82.6 1.5 %collective-permute-start.6 = (bf16[2,128,256]{2,1,0:T(8,128)(2,1)S(1)}, bf16[2,128,256]{2,1,0:T(8,128)(2,1)S(1)}, u32[]{:S(2)}, u32[]{:S(2)}) collective-permute-start(bf16[2,128,256]{2,1,0:T(8,128)(2,1)S(1)} %add_convert_fusion.8), channel_id=1, source_target_pairs={{8,0},{16,24},{9,1},{17,25},{10,2},{18,26},{11,3},{19,27},{12,4},{... | collective-permute-start | bytes 393224 | tf_op jit(solution)/shard_map/ppermute | solution.py:303
  84.1 9.3 %collective-permute-done.18.refs_3_ = bf16[2,128,768]{2,1,0:T(8,128)(2,1)S(1)} collective-permute-done((bf16[2,128,768]{2,1,0:T(8,128)(2,1)S(1)}, bf16[2,128,768]{2,1,0:T(8,128)(2,1)S(1)}, u32[]{:S(2)}, u32[]{:S(2)}) %collective-permute-start.18) | collective-permute-done | bytes 393248 | tf_op jit(solution)/shard_map/ppermute | solution.py:303
  93.4 6.6 %chunk.5 = (f32[64,2048]{1,0:T(8,128)S(1)}, f32[64,2048]{1,0:T(8,128)S(1)}, bf16[2048,4096]{1,0:T(8,128)(2,1)}, bf16[4096,2048]{1,0:T(8,128)(2,1)}) custom-call(f32[2,128,768]{2,1,0:T(8,128)S(1)} %get-tuple-element.49.refs_0_, bf16[2,128,768]{2,1,0:T(8,128)(2,1)S(1)} %collective-permute-done.16.refs_1_, ...), custom_call_target="tpu_custom_call" | custom-call | flops 1207959552 | bytes 11534336 | tf_op jit(solution)/shard_map/chunk/pallas_call | solution.py:188
  100.0 4.6 %collective-permute-done.15.refs_3_ = bf16[2,128,1024]{2,1,0:T(8,128)(2,1)S(1)} collective-permute-done((bf16[2,128,1024]{2,1,0:T(8,128)(2,1)S(1)}, bf16[2,128,1024]{2,1,0:T(8,128)(2,1)S(1)}, u32[]{:S(2)}, u32[]{:S(2)}) %collective-permute-start.15) | collective-permute-done | bytes 524320 | tf_op jit(solution)/shard_map/ppermute | solution.py:303
  104.6 7.7 %chunk.6 = (f32[64,2048]{1,0:T(8,128)S(1)}, f32[64,2048]{1,0:T(8,128)S(1)}, bf16[2048,4096]{1,0:T(8,128)(2,1)}, bf16[4096,2048]{1,0:T(8,128)(2,1)}) custom-call(f32[2,128,1024]{2,1,0:T(8,128)S(1)} %get-tuple-element.47.refs_0_, bf16[2,128,1024]{2,1,0:T(8,128)(2,1)S(1)} %collective-permute-done.13.refs_1_, ...), custom_call_target="tpu_custom_call", output_to_operand_aliasing={{2}: (11, {}), {3}: (12, {})} | custom-call | flops 1610612736 | bytes 14680064 | tf_op jit(solution)/shard_map/chunk/pallas_call | solution.py:188
  112.4 3.5 %collective-permute-done.12.refs_3_ = bf16[2,128,1024]{2,1,0:T(8,128)(2,1)S(1)} collective-permute-done((bf16[2,128,1024]{2,1,0:T(8,128)(2,1)S(1)}, bf16[2,128,1024]{2,1,0:T(8,128)(2,1)S(1)}, u32[]{:S(2)}, u32[]{:S(2)}) %collective-permute-start.12) | collective-permute-done | bytes 524320 | tf_op jit(solution)/shard_map/ppermute | solution.py:303
  115.9 7.7 %chunk.7 = (f32[64,2048]{1,0:T(8,128)S(1)}, f32[64,2048]{1,0:T(8,128)S(1)}, bf16[2048,4096]{1,0:T(8,128)(2,1)}, bf16[4096,2048]{1,0:T(8,128)(2,1)}) custom-call(f32[2,128,1024]{2,1,0:T(8,128)S(1)} %get-tuple-element.45.refs_0_, bf16[2,128,1024]{2,1,0:T(8,128)(2,1)S(1)} %collective-permute-done.10.refs_1_, ...), custom_call_target="tpu_custom_call", output_to_operand_aliasing={{2}: (11, {}), {3}: (12, {})} | custom-call | flops 1610612736 | bytes 14680064 | tf_op jit(solution)/shard_map/chunk/pallas_call | solution.py:188
  123.6 3.2 %collective-permute-done.9.refs_3_ = bf16[2,128,1024]{2,1,0:T(8,128)(2,1)S(1)} collective-permute-done((bf16[2,128,1024]{2,1,0:T(8,128)(2,1)S(1)}, bf16[2,128,1024]{2,1,0:T(8,128)(2,1)S(1)}, u32[]{:S(2)}, u32[]{:S(2)}) %collective-permute-start.9) | collective-permute-done | bytes 524320 | tf_op jit(solution)/shard_map/ppermute | solution.py:303
  126.8 7.7 %chunk.8 = (f32[64,2048]{1,0:T(8,128)S(1)}, f32[64,2048]{1,0:T(8,128)S(1)}, bf16[2048,4096]{1,0:T(8,128)(2,1)}, bf16[4096,2048]{1,0:T(8,128)(2,1)}) custom-call(f32[2,128,1024]{2,1,0:T(8,128)S(1)} %get-tuple-element.43.refs_0_, bf16[2,128,1024]{2,1,0:T(8,128)(2,1)S(1)} %collective-permute-done.7.refs_1_, ...), custom_call_target="tpu_custom_call", output_to_operand_aliasing={{2}: (11, {}), {3}: (12, {})} | custom-call | flops 1610612736 | bytes 14680064 | tf_op jit(solution)/shard_map/chunk/pallas_call | solution.py:188
  134.6 1.7 %chunk.9 = (f32[64,2048]{1,0:T(8,128)S(1)}, f32[64,2048]{1,0:T(8,128)S(1)}, bf16[128,256]{1,0:T(8,128)(2,1)S(1)}, bf16[128,256]{1,0:T(8,128)(2,1)S(1)}) custom-call(f32[2,128,256]{2,1,0:T(8,128)S(1)} %get-tuple-element.41.refs_0_, bf16[2,128,256]{2,1,0:T(8,128)(2,1)S(1)} %collective-permute-done.4.refs_1_, ...), custom_call_target="tpu_custom_call" | custom-call | flops 134217728 | bytes 3145728 | tf_op jit(solution)/shard_map/chunk/pallas_call | solution.py:188
  136.4 1.9 %collective-permute-done.19 = f32[64,2048]{1,0:T(8,128)S(1)} collective-permute-done((f32[64,2048]{1,0:T(8,128)S(1)}, f32[64,2048]{1,0:T(8,128)S(1)}, u32[]{:S(2)}, u32[]{:S(2)}) %collective-permute-start.19) | collective-permute-done | bytes 524320 | tf_op jit(solution)/shard_map/ppermute | solution.py:292
  140.5 1.4 collective-permute-start.22
  141.9 2.0 %weight_grads.1 = (bf16[2048,4096]{1,0:T(8,128)(2,1)}, bf16[4096,2048]{1,0:T(8,128)(2,1)}) custom-call(bf16[2048,128]{1,0:T(8,128)(2,1)S(1)} %transposed.1.refs_6_.refs_8_.tokt_ref, bf16[2,128,2048]{2,1,0:T(8,128)(2,1)S(1)} %constant_dynamic-update-slice_fusion.pair_ref.refs_7_.refs_9_.cot_ref, ...), custom_call_target="tpu_custom_call", output_to_operand_aliasing={{0}: (6, {}), {1}: (7, {})} | custom-call | flops 268435456 | bytes 3145728 | tf_op jit(solution)/shard_map/weight_grads/pallas_call | solution.py:255
  (56 shorter events, 16.2 us)
Async XLA Ops:
  0.6 5.5 %copy-start = (s32[64,96]{1,0:T(8,128)S(1)}, s32[64,96]{1,0:T(8,128)}, u32[]{:S(2)}) copy-start(s32[64,96]{1,0:T(8,128)} %param.9) | copy-start | bytes 73732
  1.5 6.9 %collective-permute-start = (bf16[2,16,2048]{2,1,0:T(8,128)(2,1)S(1)}, bf16[2,16,2048]{2,1,0:T(8,128)(2,1)S(1)}, u32[]{:S(2)}, u32[]{:S(2)}) collective-permute-start(bf16[2,16,2048]{2,1,0:T(8,128)(2,1)S(1)} %pad_maximum_fusion.1), channel_id=1, source_target_pairs={{0,2},{1,3},{2,0},{3,1},{4,6},{5,7},{6,4},{7,5},{8,10},{9,11},{10,... | collective-permute-start | bytes 393224 | tf_op jit(solution)/shard_map/ppermute | solution.py:285
  4.6 7.8 %collective-permute-start.1 = (bf16[2,16,2048]{2,1,0:T(8,128)(2,1)S(1)}, bf16[2,16,2048]{2,1,0:T(8,128)(2,1)S(1)}, u32[]{:S(2)}, u32[]{:S(2)}) collective-permute-start(bf16[2,16,2048]{2,1,0:T(8,128)(2,1)S(1)} %pad_maximum_fusion.1), channel_id=1, source_target_pairs={{0,4},{1,5},{2,6},{3,7},{4,0},{5,1},{6,2},{7,3},{8,12},{9,13},{10,... | collective-permute-start | bytes 393224 | tf_op jit(solution)/shard_map/ppermute | solution.py:285
  6.1 6.3 %collective-permute-start.2 = (bf16[2,16,2048]{2,1,0:T(8,128)(2,1)S(1)}, bf16[2,16,2048]{2,1,0:T(8,128)(2,1)S(1)}, u32[]{:S(2)}, u32[]{:S(2)}) collective-permute-start(bf16[2,16,2048]{2,1,0:T(8,128)(2,1)S(1)} %pad_maximum_fusion.1), channel_id=1, source_target_pairs={{0,6},{1,7},{2,4},{3,5},{4,2},{5,3},{6,0},{7,1},{8,14},{9,15},{10,... | collective-permute-start | bytes 393224 | tf_op jit(solution)/shard_map/ppermute | solution.py:285
  13.3 2.0 %collective-permute-start.3 = (bf16[2,64,2048]{2,1,0:T(8,128)(2,1)S(1)}, bf16[2,64,2048]{2,1,0:T(8,128)(2,1)S(1)}, u32[]{:S(2)}, u32[]{:S(2)}) collective-permute-start(bf16[2,64,2048]{2,1,0:T(8,128)(2,1)S(1)} %pad_maximum_fusion), channel_id=1, source_target_pairs={{0,1},{1,0},{2,3},{3,2},{4,5},{5,4},{6,7},{7,6},{8,9},{9,8},{10,11... | collective-permute-start | bytes 1572872 | tf_op jit(solution)/shard_map/ppermute | solution.py:288
  27.3 20.4 %collective-permute-start.16 = (bf16[2,128,768]{2,1,0:T(8,128)(2,1)S(1)}, bf16[2,128,768]{2,1,0:T(8,128)(2,1)S(1)}, u32[]{:S(2)}, u32[]{:S(2)}) collective-permute-start(bf16[2,128,768]{2,1,0:T(8,128)(2,1)S(1)} %get-tuple-element.50), channel_id=1, source_target_pairs={{0,8},{24,16},{1,9},{25,17},{2,10},{26,18},{3,11},{27,19},{4,12},{... | collective-permute-start | bytes 1179656 | tf_op jit(solution)/shard_map/ppermute | solution.py:303
  30.8 16.2 %collective-permute-start.4 = (bf16[2,128,256]{2,1,0:T(8,128)(2,1)S(1)}, bf16[2,128,256]{2,1,0:T(8,128)(2,1)S(1)}, u32[]{:S(2)}, u32[]{:S(2)}) collective-permute-start(bf16[2,128,256]{2,1,0:T(8,128)(2,1)S(1)} %get-tuple-element.42), channel_id=1, source_target_pairs={{0,8},{24,16},{1,9},{25,17},{2,10},{26,18},{3,11},{27,19},{4,12},{... | collective-permute-start | bytes 393224 | tf_op jit(solution)/shard_map/ppermute | solution.py:303
  37.4 16.9 %collective-permute-start.13 = (bf16[2,128,1024]{2,1,0:T(8,128)(2,1)S(1)}, bf16[2,128,1024]{2,1,0:T(8,128)(2,1)S(1)}, u32[]{:S(2)}, u32[]{:S(2)}) collective-permute-start(bf16[2,128,1024]{2,1,0:T(8,128)(2,1)S(1)} %get-tuple-element.48), channel_id=1, source_target_pairs={{0,8},{24,16},{1,9},{25,17},{2,10},{26,18},{3,11},{27,19},{4,12},{... | collective-permute-start | bytes 1572872 | tf_op jit(solution)/shard_map/ppermute | solution.py:303
  44.3 21.2 %collective-permute-start.10 = (bf16[2,128,1024]{2,1,0:T(8,128)(2,1)S(1)}, bf16[2,128,1024]{2,1,0:T(8,128)(2,1)S(1)}, u32[]{:S(2)}, u32[]{:S(2)}) collective-permute-start(bf16[2,128,1024]{2,1,0:T(8,128)(2,1)S(1)} %get-tuple-element.46), channel_id=1, source_target_pairs={{0,8},{24,16},{1,9},{25,17},{2,10},{26,18},{3,11},{27,19},{4,12},{... | collective-permute-start | bytes 1572872 | tf_op jit(solution)/shard_map/ppermute | solution.py:303
  45.6 30.3 %collective-permute-start.7 = (bf16[2,128,1024]{2,1,0:T(8,128)(2,1)S(1)}, bf16[2,128,1024]{2,1,0:T(8,128)(2,1)S(1)}, u32[]{:S(2)}, u32[]{:S(2)}) collective-permute-start(bf16[2,128,1024]{2,1,0:T(8,128)(2,1)S(1)} %get-tuple-element.44), channel_id=1, source_target_pairs={{0,8},{24,16},{1,9},{25,17},{2,10},{26,18},{3,11},{27,19},{4,12},{... | collective-permute-start | bytes 1572872 | tf_op jit(solution)/shard_map/ppermute | solution.py:303
  47.0 35.6 %collective-permute-start.5 = (bf16[2,128,256]{2,1,0:T(8,128)(2,1)S(1)}, bf16[2,128,256]{2,1,0:T(8,128)(2,1)S(1)}, u32[]{:S(2)}, u32[]{:S(2)}) collective-permute-start(bf16[2,128,256]{2,1,0:T(8,128)(2,1)S(1)} %add_convert_fusion.9), channel_id=1, source_target_pairs={{8,16},{16,8},{9,17},{17,9},{10,18},{18,10},{11,19},{19,11},{12,20... | collective-permute-start | bytes 393224 | tf_op jit(solution)/shard_map/ppermute | solution.py:303
  47.8 29.0 %collective-permute-start.17 = (bf16[2,128,768]{2,1,0:T(8,128)(2,1)S(1)}, bf16[2,128,768]{2,1,0:T(8,128)(2,1)S(1)}, u32[]{:S(2)}, u32[]{:S(2)}) collective-permute-start(bf16[2,128,768]{2,1,0:T(8,128)(2,1)S(1)} %add_convert_fusion.7), channel_id=1, source_target_pairs={{8,16},{16,8},{9,17},{17,9},{10,18},{18,10},{11,19},{19,11},{12,20... | collective-permute-start | bytes 1179656 | tf_op jit(solution)/shard_map/ppermute | solution.py:303
  54.5 23.7 %collective-permute-start.14 = (bf16[2,128,1024]{2,1,0:T(8,128)(2,1)S(1)}, bf16[2,128,1024]{2,1,0:T(8,128)(2,1)S(1)}, u32[]{:S(2)}, u32[]{:S(2)}) collective-permute-start(bf16[2,128,1024]{2,1,0:T(8,128)(2,1)S(1)} %add_convert_fusion.1), channel_id=1, source_target_pairs={{8,16},{16,8},{9,17},{17,9},{10,18},{18,10},{11,19},{19,11},{12,20... | collective-permute-start | bytes 1572872 | tf_op jit(solution)/shard_map/ppermute | solution.py:303
  65.7 14.0 %collective-permute-start.11 = (bf16[2,128,1024]{2,1,0:T(8,128)(2,1)S(1)}, bf16[2,128,1024]{2,1,0:T(8,128)(2,1)S(1)}, u32[]{:S(2)}, u32[]{:S(2)}) collective-permute-start(bf16[2,128,1024]{2,1,0:T(8,128)(2,1)S(1)} %add_convert_fusion.3), channel_id=1, source_target_pairs={{8,16},{16,8},{9,17},{17,9},{10,18},{18,10},{11,19},{19,11},{12,20... | collective-permute-start | bytes 1572872 | tf_op jit(solution)/shard_map/ppermute | solution.py:303
  76.1 5.0 %collective-permute-start.8 = (bf16[2,128,1024]{2,1,0:T(8,128)(2,1)S(1)}, bf16[2,128,1024]{2,1,0:T(8,128)(2,1)S(1)}, u32[]{:S(2)}, u32[]{:S(2)}) collective-permute-start(bf16[2,128,1024]{2,1,0:T(8,128)(2,1)S(1)} %add_convert_fusion.5), channel_id=1, source_target_pairs={{8,16},{16,8},{9,17},{17,9},{10,18},{18,10},{11,19},{19,11},{12,20... | collective-permute-start | bytes 1572872 | tf_op jit(solution)/shard_map/ppermute | solution.py:303
  76.9 16.5 %collective-permute-start.18 = (bf16[2,128,768]{2,1,0:T(8,128)(2,1)S(1)}, bf16[2,128,768]{2,1,0:T(8,128)(2,1)S(1)}, u32[]{:S(2)}, u32[]{:S(2)}) collective-permute-start(bf16[2,128,768]{2,1,0:T(8,128)(2,1)S(1)} %add_convert_fusion.6), channel_id=1, source_target_pairs={{8,0},{16,24},{9,1},{17,25},{10,2},{18,26},{11,3},{19,27},{12,4},{... | collective-permute-start | bytes 1179656 | tf_op jit(solution)/shard_map/ppermute | solution.py:303
  78.3 26.3 %collective-permute-start.15 = (bf16[2,128,1024]{2,1,0:T(8,128)(2,1)S(1)}, bf16[2,128,1024]{2,1,0:T(8,128)(2,1)S(1)}, u32[]{:S(2)}, u32[]{:S(2)}) collective-permute-start(bf16[2,128,1024]{2,1,0:T(8,128)(2,1)S(1)} %add_convert_fusion), channel_id=1, source_target_pairs={{8,0},{16,24},{9,1},{17,25},{10,2},{18,26},{11,3},{19,27},{12,4},{... | collective-permute-start | bytes 1572872 | tf_op jit(solution)/shard_map/ppermute | solution.py:303
  79.8 36.1 %collective-permute-start.12 = (bf16[2,128,1024]{2,1,0:T(8,128)(2,1)S(1)}, bf16[2,128,1024]{2,1,0:T(8,128)(2,1)S(1)}, u32[]{:S(2)}, u32[]{:S(2)}) collective-permute-start(bf16[2,128,1024]{2,1,0:T(8,128)(2,1)S(1)} %add_convert_fusion.2), channel_id=1, source_target_pairs={{8,0},{16,24},{9,1},{17,25},{10,2},{18,26},{11,3},{19,27},{12,4},{... | collective-permute-start | bytes 1572872 | tf_op jit(solution)/shard_map/ppermute | solution.py:303
  81.3 45.6 %collective-permute-start.9 = (bf16[2,128,1024]{2,1,0:T(8,128)(2,1)S(1)}, bf16[2,128,1024]{2,1,0:T(8,128)(2,1)S(1)}, u32[]{:S(2)}, u32[]{:S(2)}) collective-permute-start(bf16[2,128,1024]{2,1,0:T(8,128)(2,1)S(1)} %add_convert_fusion.4), channel_id=1, source_target_pairs={{8,0},{16,24},{9,1},{17,25},{10,2},{18,26},{11,3},{19,27},{12,4},{... | collective-permute-start | bytes 1572872 | tf_op jit(solution)/shard_map/ppermute | solution.py:303
  82.6 51.9 %collective-permute-start.6 = (bf16[2,128,256]{2,1,0:T(8,128)(2,1)S(1)}, bf16[2,128,256]{2,1,0:T(8,128)(2,1)S(1)}, u32[]{:S(2)}, u32[]{:S(2)}) collective-permute-start(bf16[2,128,256]{2,1,0:T(8,128)(2,1)S(1)} %add_convert_fusion.8), channel_id=1, source_target_pairs={{8,0},{16,24},{9,1},{17,25},{10,2},{18,26},{11,3},{19,27},{12,4},{... | collective-permute-start | bytes 393224 | tf_op jit(solution)/shard_map/ppermute | solution.py:303
  136.3 2.0 %collective-permute-start.19 = (f32[64,2048]{1,0:T(8,128)S(1)}, f32[64,2048]{1,0:T(8,128)S(1)}, u32[]{:S(2)}, u32[]{:S(2)}) collective-permute-start(f32[64,2048]{1,0:T(8,128)S(1)} %get-tuple-element.66), channel_id=1, source_target_pairs={{0,1},{1,0},{2,3},{3,2},{4,5},{5,4},{6,7},{7,6},{8,9},{9,8},{10,11... | collective-permute-start | bytes 1572872 | tf_op jit(solution)/shard_map/ppermute | solution.py:292
  138.4 5.6 %collective-permute-start.20 = (bf16[16,2048]{1,0:T(8,128)(2,1)S(1)}, bf16[16,2048]{1,0:T(8,128)(2,1)S(1)}, u32[]{:S(2)}, u32[]{:S(2)}) collective-permute-start(bf16[16,2048]{1,0:T(8,128)(2,1)S(1)} %get-tuple-element.75), channel_id=1, source_target_pairs={{0,2},{1,3},{2,0},{3,1},{4,6},{5,7},{6,4},{7,5},{8,10},{9,11},{10,... | collective-permute-start | bytes 196616 | tf_op jit(solution)/shard_map/ppermute | solution.py:297
  139.7 5.0 %collective-permute-start.21 = (bf16[16,2048]{1,0:T(8,128)(2,1)S(1)}, bf16[16,2048]{1,0:T(8,128)(2,1)S(1)}, u32[]{:S(2)}, u32[]{:S(2)}) collective-permute-start(bf16[16,2048]{1,0:T(8,128)(2,1)S(1)} %get-tuple-element.77), channel_id=1, source_target_pairs={{0,4},{1,5},{2,6},{3,7},{4,0},{5,1},{6,2},{7,3},{8,12},{9,13},{10,... | collective-permute-start | bytes 196616 | tf_op jit(solution)/shard_map/ppermute | solution.py:297
  140.5 5.2 %collective-permute-start.22 = (bf16[16,2048]{1,0:T(8,128)(2,1)S(1)}, bf16[16,2048]{1,0:T(8,128)(2,1)S(1)}, u32[]{:S(2)}, u32[]{:S(2)}) collective-permute-start(bf16[16,2048]{1,0:T(8,128)(2,1)S(1)} %get-tuple-element.76), channel_id=1, source_target_pairs={{0,6},{1,7},{2,4},{3,5},{4,2},{5,3},{6,0},{7,1},{8,14},{9,15},{10,... | collective-permute-start | bytes 196616 | tf_op jit(solution)/shard_map/ppermute | solution.py:297
  141.9 4.4 %copy-start.1 = (s32[64,96]{1,0:T(8,128)S(1)}, s32[64,96]{1,0:T(8,128)}, u32[]{:S(2)}) copy-start(s32[64,96]{1,0:T(8,128)} %param.9) | copy-start | bytes 73732

commit v4 on v3

--- a/solution.py
+++ b/solution.py
@@ -13,10 +13,11 @@
 PAIR = 2
 VMEM_LIMIT = 20 * 1024 * 1024
 PARAMS = pltpu.CompilerParams(vmem_limit_bytes=VMEM_LIMIT)
-SHARES = (3, 4, 4, 4, 1)
+SHARES = (2, 4, 4, 4, 2)
 GROUPS = (1, 1, 1, 1, 1)
 LATE = 1
 BAND = 4
+MERGED = ()
 ROOT = 0.7978845608028654
 CUBE = 0.044715
 
@@ -116,7 +117,7 @@
     return v * half, g * slope
 
 
-def chunk_kernel(own, came, up, mu, state, grads, weights, first, count, width):
+def chunk_kernel(own, came, flags, up, mu, state, grads, weights, first, count, width):
     _, tokens, chunk = own.shape
     feats, units = up.shape
     blocks = width // BLOCK
@@ -125,7 +126,7 @@
 
     def body(*refs):
         refs = list(refs)
-        own_ref = refs.pop(0)
+        flag_ref, own_ref = refs.pop(0), refs.pop(0)
         came_refs = [refs.pop(0) for _ in range(n_came)]
         up_ref, mu_ref = refs.pop(0), refs.pop(0)
         lo_in, hi_in = (refs.pop(0), refs.pop(0)) if state else (None, None)
@@ -140,8 +141,9 @@
 
         def total(k):
             value = own_ref[k]
-            for ref in came_refs:
-                value += ref[k].astype(jnp.float32)
+            for ref, (_, flag) in zip(came_refs, came):
+                part = ref[k].astype(jnp.float32)
+                value += part if flag is None else part * flag_ref[flag]
             return value
 
         act, grad = finish(total(0), total(1))
@@ -166,12 +168,13 @@
     half_spec = pl.BlockSpec((rows, feats), lambda j: (0, 0))
     half_shape = jax.ShapeDtypeStruct((rows, feats), jnp.float32)
     in_specs = [
+        pl.BlockSpec(memory_space=pltpu.SMEM),
         *([part] * (1 + n_came)),
         pl.BlockSpec((feats, width), lambda j: (0, first + j)),
         pl.BlockSpec((feats // BLOCK, width), lambda j: (0, first + j)),
         *([half_spec] * (2 if state else 0)),
     ]
-    operands = [own, *came, up, mu, *(state or ())]
+    operands = [flags, own, *(x for x, _ in came), up, mu, *(state or ())]
     aliases = {}
     if weights:
         in_specs += weight_in_specs(tokens, feats, blocks, first)
@@ -322,25 +325,43 @@
         outs = forward(pair, up_weight, down_weight, mu, md, group[0][0], [n for _, n in group], width)
         owns += list(zip(outs[::2], outs[1::2]))
     right = rows // 2
-    sums = []
-    for own, near in owns:
-        came = []
-        for k in range(right - 1):
-            came.append(shift(near, [(k, k + 1), (rows - 1 - k, rows - 2 - k)]))
-            near = (own + sum(x.astype(jnp.float32) for x in came)).astype(jnp.bfloat16)
-        came.append(shift(near, [(right - 1, right), (right, right - 1)]))
-        out = own + came[-1].astype(jnp.float32)
+    place = lax.axis_index("row")
+    is_outer = (place == 0) | (place == rows - 1)
+    flags = jnp.stack([~is_outer, is_outer]).astype(jnp.float32)
+    joined = dict(MERGED) if right == 2 else {}
+    joined = {f: k for f, k in joined.items() if f < len(plan) and plan[f][1] == plan[k][1]}
+    came = [[] for _ in plan]
+    outs = []
+    for c, (own, near) in enumerate(owns):
+        if c in joined:
+            other = joined[c]
+            send = jnp.where(is_outer, near, outs[other].astype(jnp.bfloat16))
+            x = shift(send, [(0, 1), (1, 0), (2, 3), (3, 2)])
+            came[c].append((x, 0))
+            came[other].append((x, 1))
+            near = (own + jnp.where(is_outer, 0.0, x.astype(jnp.float32))).astype(jnp.bfloat16)
+        else:
+            for k in range(right - 1):
+                came[c].append((shift(near, [(k, k + 1), (rows - 1 - k, rows - 2 - k)]), None))
+                near = (own + sum(x.astype(jnp.float32) for x, _ in came[c])).astype(jnp.bfloat16)
+        mid = shift(near, [(right - 1, right), (right, right - 1)])
+        came[c].append((mid, None))
+        outs.append(own + mid.astype(jnp.float32))
+    for c, out in enumerate(outs):
+        if c in joined.values():
+            continue
         for k in reversed(range(right - 1)):
-            far = shift(out.astype(jnp.bfloat16), [(k + 1, k), (rows - 2 - k, rows - 1 - k)])
-            came.append(far)
+            send = out.astype(jnp.bfloat16)
+            far = shift(send, [(k + 1, k), (rows - 2 - k, rows - 1 - k)])
+            came[c].append((far, None))
             out = out + far.astype(jnp.float32)
-        sums.append((own, came))
+    sums = [(own, part) for (own, _), part in zip(owns, came)]
     state = grads = None
     late = []
     for c, (first, count) in enumerate(plan):
         whole_chunk = c + LATE < len(plan)
         *state, one, two = chunk_kernel(
-            *sums[c], up_weight, mu, state, grads, weights if whole_chunk else None, first, count, width
+            *sums[c], flags, up_weight, mu, state, grads, weights if whole_chunk else None, first, count, width
         )
         if whole_chunk:
             grads = [one, two]

time: 147 us -> 138 us (0.939)
  waiting for transfers between devices: 57 us -> 48 us
    ppermute x15, waiting for transfers between devices: 46.4 us -> 38.3 us  [shift(): return lax.ppermute(x, 'row', pairs)]
  transfers between devices with their start and end apart: 23 -> 23, of which waited for: 13 -> 11; matrix products, arithmetic and copies ran while one was open for 1% -> 2% of each run, Pallas kernels for 29% -> 37%
where the time goes in v4:
time: 138 us; the launch traced here: 137 us
  Pallas kernels  55.5 us (40%)
  waiting for transfers between devices  48 us (35%)
  starting transfers between devices  27.1 us (20%)
  other arithmetic  4.25 us (3%)
    ppermute x15, waiting for transfers between devices, shift(): return lax.ppermute(x, 'row', pairs)  38.3 us
    pallas_call x5, Pallas kernels, chunk_kernel(): pl.pallas_call(body, grid=(count,), in_specs=in_specs, out_specs=[half_sp...  30.4 us
    pallas_call x5, Pallas kernels, forward(): pl.pallas_call(body, grid=(steps,), in_specs=[pl.BlockSpec((2, tokens, fe...  22 us
    ppermute x15, starting transfers between devices, shift(): return lax.ppermute(x, 'row', pairs)  18.8 us
    ppermute x3, waiting for transfers between devices, gather_tokens(): lax.ppermute(x, 'col', xor_pairs(n, s))  5.14 us
    ppermute x3, starting transfers between devices, gather_tokens(): lax.ppermute(x, 'col', xor_pairs(n, s))  4.57 us
    ppermute x3, starting transfers between devices, scatter_tokens(): came = lax.ppermute(send[k * rows:(k + 1) * rows], 'col', xor_pairs(n, s))  3.55 us
    pallas_call x1, Pallas kernels, weight_grads(): pl.pallas_call(body, grid=(count,), in_specs=[*weight_in_specs(tokens, fe...  2.82 us
  transfers between devices with their start and end apart: 23, of which 11 were waited for; matrix products, arithmetic and copies ran while one was open for 2% of the time, Pallas kernels for 37%

profile of v4, /device:TPU:0, one launch (start us, length us, event | category | flops | bytes accessed | tf_op | source)
XLA Modules:
  0.0 136.7 jit_solution(5737488148932654387)
XLA Ops:
  1.5 3.0 %collective-permute-start = (bf16[2,16,2048]{2,1,0:T(8,128)(2,1)S(1)}, bf16[2,16,2048]{2,1,0:T(8,128)(2,1)S(1)}, u32[]{:S(2)}, u32[]{:S(2)}) collective-permute-start(bf16[2,16,2048]{2,1,0:T(8,128)(2,1)S(1)} %pad_maximum_fusion.1), channel_id=1, source_target_pairs={{0,2},{1,3},{2,0},{3,1},{4,6},{5,7},{6,4},{7,5},{8,10},{9,11},{10,... | collective-permute-start | bytes 393224 | tf_op jit(solution)/shard_map/ppermute | solution.py:288
  4.6 1.5 %collective-permute-start.1 = (bf16[2,16,2048]{2,1,0:T(8,128)(2,1)S(1)}, bf16[2,16,2048]{2,1,0:T(8,128)(2,1)S(1)}, u32[]{:S(2)}, u32[]{:S(2)}) collective-permute-start(bf16[2,16,2048]{2,1,0:T(8,128)(2,1)S(1)} %pad_maximum_fusion.1), channel_id=1, source_target_pairs={{0,4},{1,5},{2,6},{3,7},{4,0},{5,1},{6,2},{7,3},{8,12},{9,13},{10,... | collective-permute-start | bytes 393224 | tf_op jit(solution)/shard_map/ppermute | solution.py:288
  8.5 3.9 %collective-permute-done.1 = bf16[2,16,2048]{2,1,0:T(8,128)(2,1)S(1)} collective-permute-done((bf16[2,16,2048]{2,1,0:T(8,128)(2,1)S(1)}, bf16[2,16,2048]{2,1,0:T(8,128)(2,1)S(1)}, u32[]{:S(2)}, u32[]{:S(2)}) %collective-permute-start.1) | collective-permute-done | bytes 131104 | tf_op jit(solution)/shard_map/ppermute | solution.py:288
  13.5 1.8 %collective-permute-done.3 = bf16[2,64,2048]{2,1,0:T(8,128)(2,1)S(1)} collective-permute-done((bf16[2,64,2048]{2,1,0:T(8,128)(2,1)S(1)}, bf16[2,64,2048]{2,1,0:T(8,128)(2,1)S(1)}, u32[]{:S(2)}, u32[]{:S(2)}) %collective-permute-start.3) | collective-permute-done | bytes 524320 | tf_op jit(solution)/shard_map/ppermute | solution.py:291
  15.3 3.0 %forward.9 = (f32[2,128,512]{2,1,0:T(8,128)S(1)}, bf16[2,128,512]{2,1,0:T(8,128)(2,1)S(1)}) custom-call(bf16[2,128,2048]{2,1,0:T(8,128)(2,1)S(1)} %constant_dynamic-update-slice_fusion.pair_ref.refs_8_.refs_10_.cot_ref, bf16[2048,4096]{1,0:T(8,128)(2,1)} %refs_5_.9, bf16[4096,2048]{1,0:T(8,128)(2,1)} %down_ref.9, f32[16,4096]{1,0:T(8,128)S(1)} %bitcast.10, ...), custom_call_target="tpu_custom_call" | custom-call | flops 536870912 | bytes 5242880 | tf_op jit(solution)/shard_map/forward/pallas_call | solution.py:90
  18.3 3.5 %collective-permute-start.16 = (bf16[2,128,512]{2,1,0:T(8,128)(2,1)S(1)}, bf16[2,128,512]{2,1,0:T(8,128)(2,1)S(1)}, u32[]{:S(2)}, u32[]{:S(2)}) collective-permute-start(bf16[2,128,512]{2,1,0:T(8,128)(2,1)S(1)} %get-tuple-element.50), channel_id=1, source_target_pairs={{0,8},{24,16},{1,9},{25,17},{2,10},{26,18},{3,11},{27,19},{4,12},{... | collective-permute-start | bytes 786440 | tf_op jit(solution)/shard_map/ppermute | solution.py:306
  21.8 5.4 %forward.8 = (f32[2,128,1024]{2,1,0:T(8,128)S(1)}, bf16[2,128,1024]{2,1,0:T(8,128)(2,1)S(1)}) custom-call(bf16[2,128,2048]{2,1,0:T(8,128)(2,1)S(1)} %constant_dynamic-update-slice_fusion.pair_ref.refs_8_.refs_10_.cot_ref, bf16[2048,4096]{1,0:T(8,128)(2,1)} %refs_5_.9, bf16[4096,2048]{1,0:T(8,128)(2,1)} %down_ref.9, f32[16,4096]{1,0:T(8,128)S(1)} %bitcast.11, ...), custom_call_target="tpu_custom_call" | custom-call | flops 1073741824 | bytes 9437184 | tf_op jit(solution)/shard_map/forward/pallas_call | solution.py:90
  27.1 1.3 collective-permute-start.13
  28.5 3.0 %forward.5 = (f32[2,128,512]{2,1,0:T(8,128)S(1)}, bf16[2,128,512]{2,1,0:T(8,128)(2,1)S(1)}) custom-call(bf16[2,128,2048]{2,1,0:T(8,128)(2,1)S(1)} %constant_dynamic-update-slice_fusion.pair_ref.refs_8_.refs_10_.cot_ref, bf16[2048,4096]{1,0:T(8,128)(2,1)} %refs_5_.9, bf16[4096,2048]{1,0:T(8,128)(2,1)} %down_ref.9, f32[16,4096]{1,0:T(8,128)S(1)} %bitcast.12, ...), custom_call_target="tpu_custom_call" | custom-call | flops 536870912 | bytes 5242880 | tf_op jit(solution)/shard_map/forward/pallas_call | solution.py:90
  31.4 1.3 collective-permute-start.4
  32.8 5.4 %forward.7 = (f32[2,128,1024]{2,1,0:T(8,128)S(1)}, bf16[2,128,1024]{2,1,0:T(8,128)(2,1)S(1)}) custom-call(bf16[2,128,2048]{2,1,0:T(8,128)(2,1)S(1)} %constant_dynamic-update-slice_fusion.pair_ref.refs_8_.refs_10_.cot_ref, bf16[2048,4096]{1,0:T(8,128)(2,1)} %refs_5_.9, bf16[4096,2048]{1,0:T(8,128)(2,1)} %down_ref.9, f32[16,4096]{1,0:T(8,128)S(1)} %bitcast.13, ...), custom_call_target="tpu_custom_call" | custom-call | flops 1073741824 | bytes 9437184 | tf_op jit(solution)/shard_map/forward/pallas_call | solution.py:90
  38.1 5.4 %forward.6 = (f32[2,128,1024]{2,1,0:T(8,128)S(1)}, bf16[2,128,1024]{2,1,0:T(8,128)(2,1)S(1)}) custom-call(bf16[2,128,2048]{2,1,0:T(8,128)(2,1)S(1)} %constant_dynamic-update-slice_fusion.pair_ref.refs_8_.refs_10_.cot_ref, bf16[2048,4096]{1,0:T(8,128)(2,1)} %refs_5_.9, bf16[4096,2048]{1,0:T(8,128)(2,1)} %down_ref.9, f32[16,4096]{1,0:T(8,128)S(1)} %bitcast.14, ...), custom_call_target="tpu_custom_call" | custom-call | flops 1073741824 | bytes 9437184 | tf_op jit(solution)/shard_map/forward/pallas_call | solution.py:90
  43.7 1.3 collective-permute-start.10
  45.0 1.3 collective-permute-start.7
  48.8 8.5 %collective-permute-done.10.refs_2_ = bf16[2,128,1024]{2,1,0:T(8,128)(2,1)S(1)} collective-permute-done((bf16[2,128,1024]{2,1,0:T(8,128)(2,1)S(1)}, bf16[2,128,1024]{2,1,0:T(8,128)(2,1)S(1)}, u32[]{:S(2)}, u32[]{:S(2)}) %collective-permute-start.10) | collective-permute-done | bytes 524320 | tf_op jit(solution)/shard_map/ppermute | solution.py:306
  58.2 9.8 %collective-permute-done.7.refs_2_ = bf16[2,128,1024]{2,1,0:T(8,128)(2,1)S(1)} collective-permute-done((bf16[2,128,1024]{2,1,0:T(8,128)(2,1)S(1)}, bf16[2,128,1024]{2,1,0:T(8,128)(2,1)S(1)}, u32[]{:S(2)}, u32[]{:S(2)}) %collective-permute-start.7) | collective-permute-done | bytes 524320 | tf_op jit(solution)/shard_map/ppermute | solution.py:306
  68.9 1.3 collective-permute-start.18
  70.4 1.3 collective-permute-start.15
  73.4 1.3 collective-permute-start.9
  74.7 1.5 %collective-permute-start.6 = (bf16[2,128,512]{2,1,0:T(8,128)(2,1)S(1)}, bf16[2,128,512]{2,1,0:T(8,128)(2,1)S(1)}, u32[]{:S(2)}, u32[]{:S(2)}) collective-permute-start(bf16[2,128,512]{2,1,0:T(8,128)(2,1)S(1)} %add_convert_fusion.8), channel_id=1, source_target_pairs={{8,0},{16,24},{9,1},{17,25},{10,2},{18,26},{11,3},{19,27},{12,4},{... | collective-permute-start | bytes 786440 | tf_op jit(solution)/shard_map/ppermute | solution.py:306
  76.2 6.4 %collective-permute-done.18.refs_4_ = bf16[2,128,512]{2,1,0:T(8,128)(2,1)S(1)} collective-permute-done((bf16[2,128,512]{2,1,0:T(8,128)(2,1)S(1)}, bf16[2,128,512]{2,1,0:T(8,128)(2,1)S(1)}, u32[]{:S(2)}, u32[]{:S(2)}) %collective-permute-start.18) | collective-permute-done | bytes 262176 | tf_op jit(solution)/shard_map/ppermute | solution.py:306
  82.6 4.6 %chunk.5 = (f32[64,2048]{1,0:T(8,128)S(1)}, f32[64,2048]{1,0:T(8,128)S(1)}, bf16[2048,4096]{1,0:T(8,128)(2,1)}, bf16[4096,2048]{1,0:T(8,128)(2,1)}) custom-call(f32[2]{0:T(128)S(1)} %add_convert_fusion.10.refs_0_, f32[2,128,512]{2,1,0:T(8,128)S(1)} %get-tuple-element.49.refs_1_, bf16[2,128,512]{2,1,0:T(8,128)(2,1)S(1)} %collective-permute-done.16.refs_2_, ...), custom_call_target="tpu_custom_call" | custom-call | flops 805306368 | bytes 8388608 | tf_op jit(solution)/shard_map/chunk/pallas_call | solution.py:191
  87.3 6.6 %collective-permute-done.15.refs_4_ = bf16[2,128,1024]{2,1,0:T(8,128)(2,1)S(1)} collective-permute-done((bf16[2,128,1024]{2,1,0:T(8,128)(2,1)S(1)}, bf16[2,128,1024]{2,1,0:T(8,128)(2,1)S(1)}, u32[]{:S(2)}, u32[]{:S(2)}) %collective-permute-start.15) | collective-permute-done | bytes 524320 | tf_op jit(solution)/shard_map/ppermute | solution.py:306
  93.9 7.8 %chunk.6 = (f32[64,2048]{1,0:T(8,128)S(1)}, f32[64,2048]{1,0:T(8,128)S(1)}, bf16[2048,4096]{1,0:T(8,128)(2,1)}, bf16[4096,2048]{1,0:T(8,128)(2,1)}) custom-call(f32[2]{0:T(128)S(1)} %add_convert_fusion.10.refs_0_, f32[2,128,1024]{2,1,0:T(8,128)S(1)} %get-tuple-element.47.refs_1_, ...), custom_call_target="tpu_custom_call", output_to_operand_aliasing={{2}: (12, {}), {3}: (13, {})} | custom-call | flops 1610612736 | bytes 14680064 | tf_op jit(solution)/shard_map/chunk/pallas_call | solution.py:191
  101.7 3.5 %collective-permute-done.12.refs_4_ = bf16[2,128,1024]{2,1,0:T(8,128)(2,1)S(1)} collective-permute-done((bf16[2,128,1024]{2,1,0:T(8,128)(2,1)S(1)}, bf16[2,128,1024]{2,1,0:T(8,128)(2,1)S(1)}, u32[]{:S(2)}, u32[]{:S(2)}) %collective-permute-start.12) | collective-permute-done | bytes 524320 | tf_op jit(solution)/shard_map/ppermute | solution.py:306
  105.1 7.8 %chunk.7 = (f32[64,2048]{1,0:T(8,128)S(1)}, f32[64,2048]{1,0:T(8,128)S(1)}, bf16[2048,4096]{1,0:T(8,128)(2,1)}, bf16[4096,2048]{1,0:T(8,128)(2,1)}) custom-call(f32[2]{0:T(128)S(1)} %add_convert_fusion.10.refs_0_, f32[2,128,1024]{2,1,0:T(8,128)S(1)} %get-tuple-element.45.refs_1_, ...), custom_call_target="tpu_custom_call", output_to_operand_aliasing={{2}: (12, {}), {3}: (13, {})} | custom-call | flops 1610612736 | bytes 14680064 | tf_op jit(solution)/shard_map/chunk/pallas_call | solution.py:191
  112.9 3.5 %collective-permute-done.9.refs_4_ = bf16[2,128,1024]{2,1,0:T(8,128)(2,1)S(1)} collective-permute-done((bf16[2,128,1024]{2,1,0:T(8,128)(2,1)S(1)}, bf16[2,128,1024]{2,1,0:T(8,128)(2,1)S(1)}, u32[]{:S(2)}, u32[]{:S(2)}) %collective-permute-start.9) | collective-permute-done | bytes 524320 | tf_op jit(solution)/shard_map/ppermute | solution.py:306
  116.4 7.8 %chunk.8 = (f32[64,2048]{1,0:T(8,128)S(1)}, f32[64,2048]{1,0:T(8,128)S(1)}, bf16[2048,4096]{1,0:T(8,128)(2,1)}, bf16[4096,2048]{1,0:T(8,128)(2,1)}) custom-call(f32[2]{0:T(128)S(1)} %add_convert_fusion.10.refs_0_, f32[2,128,1024]{2,1,0:T(8,128)S(1)} %get-tuple-element.43.refs_1_, ...), custom_call_target="tpu_custom_call", output_to_operand_aliasing={{2}: (12, {}), {3}: (13, {})} | custom-call | flops 1610612736 | bytes 14680064 | tf_op jit(solution)/shard_map/chunk/pallas_call | solution.py:191
  124.1 2.5 %chunk.9 = (f32[64,2048]{1,0:T(8,128)S(1)}, f32[64,2048]{1,0:T(8,128)S(1)}, bf16[128,512]{1,0:T(8,128)(2,1)S(1)}, bf16[128,512]{1,0:T(8,128)(2,1)S(1)}) custom-call(f32[2]{0:T(128)S(1)} %add_convert_fusion.10.refs_0_, f32[2,128,512]{2,1,0:T(8,128)S(1)} %get-tuple-element.41.refs_1_, bf16[2,128,512]{2,1,0:T(8,128)(2,1)S(1)} %collective-permute-done.4.refs_2_, ...), custom_call_target="tpu_custom_call" | custom-call | flops 268435456 | bytes 4194304 | tf_op jit(solution)/shard_map/chunk/pallas_call | solution.py:191
  126.7 1.9 %collective-permute-done.19 = f32[64,2048]{1,0:T(8,128)S(1)} collective-permute-done((f32[64,2048]{1,0:T(8,128)S(1)}, f32[64,2048]{1,0:T(8,128)S(1)}, u32[]{:S(2)}, u32[]{:S(2)}) %collective-permute-start.19) | collective-permute-done | bytes 524320 | tf_op jit(solution)/shard_map/ppermute | solution.py:295
  130.8 1.4 %collective-permute-start.22 = (bf16[16,2048]{1,0:T(8,128)(2,1)S(1)}, bf16[16,2048]{1,0:T(8,128)(2,1)S(1)}, u32[]{:S(2)}, u32[]{:S(2)}) collective-permute-start(bf16[16,2048]{1,0:T(8,128)(2,1)S(1)} %get-tuple-element.76), channel_id=1, source_target_pairs={{0,6},{1,7},{2,4},{3,5},{4,2},{5,3},{6,0},{7,1},{8,14},{9,15},{10,... | collective-permute-start | bytes 196616 | tf_op jit(solution)/shard_map/ppermute | solution.py:300
  132.3 2.8 %weight_grads.1 = (bf16[2048,4096]{1,0:T(8,128)(2,1)}, bf16[4096,2048]{1,0:T(8,128)(2,1)}) custom-call(bf16[2048,128]{1,0:T(8,128)(2,1)S(1)} %transposed.1.refs_7_.refs_9_.tokt_ref, bf16[2,128,2048]{2,1,0:T(8,128)(2,1)S(1)} %constant_dynamic-update-slice_fusion.pair_ref.refs_8_.refs_10_.cot_ref, ...), custom_call_target="tpu_custom_call", output_to_operand_aliasing={{0}: (6, {}), {1}: (7, {})} | custom-call | flops 536870912 | bytes 5242880 | tf_op jit(solution)/shard_map/weight_grads/pallas_call | solution.py:258
  (57 shorter events, 14.4 us)
Async XLA Ops:
  0.6 5.5 %copy-start = (s32[64,96]{1,0:T(8,128)S(1)}, s32[64,96]{1,0:T(8,128)}, u32[]{:S(2)}) copy-start(s32[64,96]{1,0:T(8,128)} %param.9) | copy-start | bytes 73732
  1.5 6.9 %collective-permute-start = (bf16[2,16,2048]{2,1,0:T(8,128)(2,1)S(1)}, bf16[2,16,2048]{2,1,0:T(8,128)(2,1)S(1)}, u32[]{:S(2)}, u32[]{:S(2)}) collective-permute-start(bf16[2,16,2048]{2,1,0:T(8,128)(2,1)S(1)} %pad_maximum_fusion.1), channel_id=1, source_target_pairs={{0,2},{1,3},{2,0},{3,1},{4,6},{5,7},{6,4},{7,5},{8,10},{9,11},{10,... | collective-permute-start | bytes 393224 | tf_op jit(solution)/shard_map/ppermute | solution.py:288
  4.6 7.8 %collective-permute-start.1 = (bf16[2,16,2048]{2,1,0:T(8,128)(2,1)S(1)}, bf16[2,16,2048]{2,1,0:T(8,128)(2,1)S(1)}, u32[]{:S(2)}, u32[]{:S(2)}) collective-permute-start(bf16[2,16,2048]{2,1,0:T(8,128)(2,1)S(1)} %pad_maximum_fusion.1), channel_id=1, source_target_pairs={{0,4},{1,5},{2,6},{3,7},{4,0},{5,1},{6,2},{7,3},{8,12},{9,13},{10,... | collective-permute-start | bytes 393224 | tf_op jit(solution)/shard_map/ppermute | solution.py:288
  6.1 6.3 %collective-permute-start.2 = (bf16[2,16,2048]{2,1,0:T(8,128)(2,1)S(1)}, bf16[2,16,2048]{2,1,0:T(8,128)(2,1)S(1)}, u32[]{:S(2)}, u32[]{:S(2)}) collective-permute-start(bf16[2,16,2048]{2,1,0:T(8,128)(2,1)S(1)} %pad_maximum_fusion.1), channel_id=1, source_target_pairs={{0,6},{1,7},{2,4},{3,5},{4,2},{5,3},{6,0},{7,1},{8,14},{9,15},{10,... | collective-permute-start | bytes 393224 | tf_op jit(solution)/shard_map/ppermute | solution.py:288
  13.3 2.0 %collective-permute-start.3 = (bf16[2,64,2048]{2,1,0:T(8,128)(2,1)S(1)}, bf16[2,64,2048]{2,1,0:T(8,128)(2,1)S(1)}, u32[]{:S(2)}, u32[]{:S(2)}) collective-permute-start(bf16[2,64,2048]{2,1,0:T(8,128)(2,1)S(1)} %pad_maximum_fusion), channel_id=1, source_target_pairs={{0,1},{1,0},{2,3},{3,2},{4,5},{5,4},{6,7},{7,6},{8,9},{9,8},{10,11... | collective-permute-start | bytes 1572872 | tf_op jit(solution)/shard_map/ppermute | solution.py:291
  18.3 28.1 %collective-permute-start.16 = (bf16[2,128,512]{2,1,0:T(8,128)(2,1)S(1)}, bf16[2,128,512]{2,1,0:T(8,128)(2,1)S(1)}, u32[]{:S(2)}, u32[]{:S(2)}) collective-permute-start(bf16[2,128,512]{2,1,0:T(8,128)(2,1)S(1)} %get-tuple-element.50), channel_id=1, source_target_pairs={{0,8},{24,16},{1,9},{25,17},{2,10},{26,18},{3,11},{27,19},{4,12},{... | collective-permute-start | bytes 786440 | tf_op jit(solution)/shard_map/ppermute | solution.py:306
  27.1 20.8 %collective-permute-start.13 = (bf16[2,128,1024]{2,1,0:T(8,128)(2,1)S(1)}, bf16[2,128,1024]{2,1,0:T(8,128)(2,1)S(1)}, u32[]{:S(2)}, u32[]{:S(2)}) collective-permute-start(bf16[2,128,1024]{2,1,0:T(8,128)(2,1)S(1)} %get-tuple-element.48), channel_id=1, source_target_pairs={{0,8},{24,16},{1,9},{25,17},{2,10},{26,18},{3,11},{27,19},{4,12},{... | collective-permute-start | bytes 1572872 | tf_op jit(solution)/shard_map/ppermute | solution.py:306
  31.4 15.7 %collective-permute-start.4 = (bf16[2,128,512]{2,1,0:T(8,128)(2,1)S(1)}, bf16[2,128,512]{2,1,0:T(8,128)(2,1)S(1)}, u32[]{:S(2)}, u32[]{:S(2)}) collective-permute-start(bf16[2,128,512]{2,1,0:T(8,128)(2,1)S(1)} %get-tuple-element.42), channel_id=1, source_target_pairs={{0,8},{24,16},{1,9},{25,17},{2,10},{26,18},{3,11},{27,19},{4,12},{... | collective-permute-start | bytes 786440 | tf_op jit(solution)/shard_map/ppermute | solution.py:306
  43.7 13.6 %collective-permute-start.10 = (bf16[2,128,1024]{2,1,0:T(8,128)(2,1)S(1)}, bf16[2,128,1024]{2,1,0:T(8,128)(2,1)S(1)}, u32[]{:S(2)}, u32[]{:S(2)}) collective-permute-start(bf16[2,128,1024]{2,1,0:T(8,128)(2,1)S(1)} %get-tuple-element.46), channel_id=1, source_target_pairs={{0,8},{24,16},{1,9},{25,17},{2,10},{26,18},{3,11},{27,19},{4,12},{... | collective-permute-start | bytes 1572872 | tf_op jit(solution)/shard_map/ppermute | solution.py:306
  45.0 23.0 %collective-permute-start.7 = (bf16[2,128,1024]{2,1,0:T(8,128)(2,1)S(1)}, bf16[2,128,1024]{2,1,0:T(8,128)(2,1)S(1)}, u32[]{:S(2)}, u32[]{:S(2)}) collective-permute-start(bf16[2,128,1024]{2,1,0:T(8,128)(2,1)S(1)} %get-tuple-element.44), channel_id=1, source_target_pairs={{0,8},{24,16},{1,9},{25,17},{2,10},{26,18},{3,11},{27,19},{4,12},{... | collective-permute-start | bytes 1572872 | tf_op jit(solution)/shard_map/ppermute | solution.py:306
  46.5 22.4 %collective-permute-start.17 = (bf16[2,128,512]{2,1,0:T(8,128)(2,1)S(1)}, bf16[2,128,512]{2,1,0:T(8,128)(2,1)S(1)}, u32[]{:S(2)}, u32[]{:S(2)}) collective-permute-start(bf16[2,128,512]{2,1,0:T(8,128)(2,1)S(1)} %add_convert_fusion.7), channel_id=1, source_target_pairs={{8,16},{16,8},{9,17},{17,9},{10,18},{18,10},{11,19},{19,11},{12,20... | collective-permute-start | bytes 786440 | tf_op jit(solution)/shard_map/ppermute | solution.py:306
  47.2 27.4 %collective-permute-start.5 = (bf16[2,128,512]{2,1,0:T(8,128)(2,1)S(1)}, bf16[2,128,512]{2,1,0:T(8,128)(2,1)S(1)}, u32[]{:S(2)}, u32[]{:S(2)}) collective-permute-start(bf16[2,128,512]{2,1,0:T(8,128)(2,1)S(1)} %add_convert_fusion.9), channel_id=1, source_target_pairs={{8,16},{16,8},{9,17},{17,9},{10,18},{18,10},{11,19},{19,11},{12,20... | collective-permute-start | bytes 786440 | tf_op jit(solution)/shard_map/ppermute | solution.py:306
  48.1 22.2 %collective-permute-start.14 = (bf16[2,128,1024]{2,1,0:T(8,128)(2,1)S(1)}, bf16[2,128,1024]{2,1,0:T(8,128)(2,1)S(1)}, u32[]{:S(2)}, u32[]{:S(2)}) collective-permute-start(bf16[2,128,1024]{2,1,0:T(8,128)(2,1)S(1)} %add_convert_fusion.1), channel_id=1, source_target_pairs={{8,16},{16,8},{9,17},{17,9},{10,18},{18,10},{11,19},{19,11},{12,20... | collective-permute-start | bytes 1572872 | tf_op jit(solution)/shard_map/ppermute | solution.py:306
  57.5 14.2 %collective-permute-start.11 = (bf16[2,128,1024]{2,1,0:T(8,128)(2,1)S(1)}, bf16[2,128,1024]{2,1,0:T(8,128)(2,1)S(1)}, u32[]{:S(2)}, u32[]{:S(2)}) collective-permute-start(bf16[2,128,1024]{2,1,0:T(8,128)(2,1)S(1)} %add_convert_fusion.3), channel_id=1, source_target_pairs={{8,16},{16,8},{9,17},{17,9},{10,18},{18,10},{11,19},{19,11},{12,20... | collective-permute-start | bytes 1572872 | tf_op jit(solution)/shard_map/ppermute | solution.py:306
  68.2 5.0 %collective-permute-start.8 = (bf16[2,128,1024]{2,1,0:T(8,128)(2,1)S(1)}, bf16[2,128,1024]{2,1,0:T(8,128)(2,1)S(1)}, u32[]{:S(2)}, u32[]{:S(2)}) collective-permute-start(bf16[2,128,1024]{2,1,0:T(8,128)(2,1)S(1)} %add_convert_fusion.5), channel_id=1, source_target_pairs={{8,16},{16,8},{9,17},{17,9},{10,18},{18,10},{11,19},{19,11},{12,20... | collective-permute-start | bytes 1572872 | tf_op jit(solution)/shard_map/ppermute | solution.py:306
  68.9 13.7 %collective-permute-start.18 = (bf16[2,128,512]{2,1,0:T(8,128)(2,1)S(1)}, bf16[2,128,512]{2,1,0:T(8,128)(2,1)S(1)}, u32[]{:S(2)}, u32[]{:S(2)}) collective-permute-start(bf16[2,128,512]{2,1,0:T(8,128)(2,1)S(1)} %add_convert_fusion.6), channel_id=1, source_target_pairs={{8,0},{16,24},{9,1},{17,25},{10,2},{18,26},{11,3},{19,27},{12,4},{... | collective-permute-start | bytes 786440 | tf_op jit(solution)/shard_map/ppermute | solution.py:306
  70.4 23.5 %collective-permute-start.15 = (bf16[2,128,1024]{2,1,0:T(8,128)(2,1)S(1)}, bf16[2,128,1024]{2,1,0:T(8,128)(2,1)S(1)}, u32[]{:S(2)}, u32[]{:S(2)}) collective-permute-start(bf16[2,128,1024]{2,1,0:T(8,128)(2,1)S(1)} %add_convert_fusion), channel_id=1, source_target_pairs={{8,0},{16,24},{9,1},{17,25},{10,2},{18,26},{11,3},{19,27},{12,4},{... | collective-permute-start | bytes 1572872 | tf_op jit(solution)/shard_map/ppermute | solution.py:306
  71.9 33.2 %collective-permute-start.12 = (bf16[2,128,1024]{2,1,0:T(8,128)(2,1)S(1)}, bf16[2,128,1024]{2,1,0:T(8,128)(2,1)S(1)}, u32[]{:S(2)}, u32[]{:S(2)}) collective-permute-start(bf16[2,128,1024]{2,1,0:T(8,128)(2,1)S(1)} %add_convert_fusion.2), channel_id=1, source_target_pairs={{8,0},{16,24},{9,1},{17,25},{10,2},{18,26},{11,3},{19,27},{12,4},{... | collective-permute-start | bytes 1572872 | tf_op jit(solution)/shard_map/ppermute | solution.py:306
  73.4 43.0 %collective-permute-start.9 = (bf16[2,128,1024]{2,1,0:T(8,128)(2,1)S(1)}, bf16[2,128,1024]{2,1,0:T(8,128)(2,1)S(1)}, u32[]{:S(2)}, u32[]{:S(2)}) collective-permute-start(bf16[2,128,1024]{2,1,0:T(8,128)(2,1)S(1)} %add_convert_fusion.4), channel_id=1, source_target_pairs={{8,0},{16,24},{9,1},{17,25},{10,2},{18,26},{11,3},{19,27},{12,4},{... | collective-permute-start | bytes 1572872 | tf_op jit(solution)/shard_map/ppermute | solution.py:306
  74.7 49.4 %collective-permute-start.6 = (bf16[2,128,512]{2,1,0:T(8,128)(2,1)S(1)}, bf16[2,128,512]{2,1,0:T(8,128)(2,1)S(1)}, u32[]{:S(2)}, u32[]{:S(2)}) collective-permute-start(bf16[2,128,512]{2,1,0:T(8,128)(2,1)S(1)} %add_convert_fusion.8), channel_id=1, source_target_pairs={{8,0},{16,24},{9,1},{17,25},{10,2},{18,26},{11,3},{19,27},{12,4},{... | collective-permute-start | bytes 786440 | tf_op jit(solution)/shard_map/ppermute | solution.py:306
  126.6 2.0 %collective-permute-start.19 = (f32[64,2048]{1,0:T(8,128)S(1)}, f32[64,2048]{1,0:T(8,128)S(1)}, u32[]{:S(2)}, u32[]{:S(2)}) collective-permute-start(f32[64,2048]{1,0:T(8,128)S(1)} %get-tuple-element.66), channel_id=1, source_target_pairs={{0,1},{1,0},{2,3},{3,2},{4,5},{5,4},{6,7},{7,6},{8,9},{9,8},{10,11... | collective-permute-start | bytes 1572872 | tf_op jit(solution)/shard_map/ppermute | solution.py:295
  128.7 6.4 %collective-permute-start.20 = (bf16[16,2048]{1,0:T(8,128)(2,1)S(1)}, bf16[16,2048]{1,0:T(8,128)(2,1)S(1)}, u32[]{:S(2)}, u32[]{:S(2)}) collective-permute-start(bf16[16,2048]{1,0:T(8,128)(2,1)S(1)} %get-tuple-element.75), channel_id=1, source_target_pairs={{0,2},{1,3},{2,0},{3,1},{4,6},{5,7},{6,4},{7,5},{8,10},{9,11},{10,... | collective-permute-start | bytes 196616 | tf_op jit(solution)/shard_map/ppermute | solution.py:300
  130.0 5.1 %collective-permute-start.21 = (bf16[16,2048]{1,0:T(8,128)(2,1)S(1)}, bf16[16,2048]{1,0:T(8,128)(2,1)S(1)}, u32[]{:S(2)}, u32[]{:S(2)}) collective-permute-start(bf16[16,2048]{1,0:T(8,128)(2,1)S(1)} %get-tuple-element.77), channel_id=1, source_target_pairs={{0,4},{1,5},{2,6},{3,7},{4,0},{5,1},{6,2},{7,3},{8,12},{9,13},{10,... | collective-permute-start | bytes 196616 | tf_op jit(solution)/shard_map/ppermute | solution.py:300
  130.8 5.2 %collective-permute-start.22 = (bf16[16,2048]{1,0:T(8,128)(2,1)S(1)}, bf16[16,2048]{1,0:T(8,128)(2,1)S(1)}, u32[]{:S(2)}, u32[]{:S(2)}) collective-permute-start(bf16[16,2048]{1,0:T(8,128)(2,1)S(1)} %get-tuple-element.76), channel_id=1, source_target_pairs={{0,6},{1,7},{2,4},{3,5},{4,2},{5,3},{6,0},{7,1},{8,14},{9,15},{10,... | collective-permute-start | bytes 196616 | tf_op jit(solution)/shard_map/ppermute | solution.py:300
  132.3 4.4 %copy-start.1 = (s32[64,96]{1,0:T(8,128)S(1)}, s32[64,96]{1,0:T(8,128)}, u32[]{:S(2)}) copy-start(s32[64,96]{1,0:T(8,128)} %param.9) | copy-start | bytes 73732

commit v5 on v4

--- a/solution.py
+++ b/solution.py
@@ -282,11 +282,21 @@
     return [(i, i ^ bits) for i in range(n)]
 
 
+def join(parts, axis):
+    shape = list(parts[0].shape)
+    step = shape[axis]
+    shape[axis] = step * len(parts)
+    out = jnp.zeros(shape, parts[0].dtype)
+    for k, part in enumerate(parts):
+        out = lax.dynamic_update_slice_in_dim(out, part, k * step, axis)
+    return out
+
+
 def gather_tokens(x, n, masks):
     if n == 1:
         return x, masks
     parts = [x] + [lax.ppermute(x, "col", xor_pairs(n, s)) for s in range(2, n, 2)]
-    half = jnp.concatenate(parts, axis=1)
+    half = join(parts, 1)
     half, masks = lax.optimization_barrier((half, masks))
     return jnp.concatenate([half, lax.ppermute(half, "col", xor_pairs(n, 1))], axis=1), masks
 

time: 138 us -> 137 us (level)
  no operation moved by 1% of the time
where the time goes in v5:
time: 137 us; the launch traced here: 136 us
  Pallas kernels  55.5 us (41%)
  waiting for transfers between devices  47.9 us (35%)
  starting transfers between devices  27.1 us (20%)
  other arithmetic  3.34 us (2%)
    ppermute x15, waiting for transfers between devices, shift(): return lax.ppermute(x, 'row', pairs)  38.3 us
    pallas_call x5, Pallas kernels, chunk_kernel(): pl.pallas_call(body, grid=(count,), in_specs=in_specs, out_specs=[half_sp...  30.4 us
    pallas_call x5, Pallas kernels, forward(): pl.pallas_call(body, grid=(steps,), in_specs=[pl.BlockSpec((2, tokens, fe...  22 us
    ppermute x15, starting transfers between devices, shift(): return lax.ppermute(x, 'row', pairs)  18.8 us
    ppermute x3, waiting for transfers between devices, gather_tokens(): lax.ppermute(x, 'col', xor_pairs(n, s))  5.08 us
    ppermute x3, starting transfers between devices, gather_tokens(): lax.ppermute(x, 'col', xor_pairs(n, s))  4.57 us
    ppermute x3, starting transfers between devices, scatter_tokens(): came = lax.ppermute(send[k * rows:(k + 1) * rows], 'col', xor_pairs(n, s))  3.55 us
    pallas_call x1, Pallas kernels, weight_grads(): pl.pallas_call(body, grid=(count,), in_specs=[*weight_in_specs(tokens, fe...  2.82 us
  transfers between devices with their start and end apart: 23, of which 11 were waited for; matrix products, arithmetic and copies ran while one was open for 2% of the time, Pallas kernels for 37%

profile of v5, /device:TPU:0, one launch (start us, length us, event | category | flops | bytes accessed | tf_op | source)
XLA Modules:
  0.0 135.8 jit_solution(18304812028831215236)
XLA Ops:
  1.5 3.0 %collective-permute-start = (bf16[2,16,2048]{2,1,0:T(8,128)(2,1)S(1)}, bf16[2,16,2048]{2,1,0:T(8,128)(2,1)S(1)}, u32[]{:S(2)}, u32[]{:S(2)}) collective-permute-start(bf16[2,16,2048]{2,1,0:T(8,128)(2,1)S(1)} %pad_maximum_fusion), channel_id=1, source_target_pairs={{0,2},{1,3},{2,0},{3,1},{4,6},{5,7},{6,4},{7,5},{8,10},{9,11},{10,... | collective-permute-start | bytes 393224 | tf_op jit(solution)/shard_map/ppermute | solution.py:298
  4.6 1.5 %collective-permute-start.1 = (bf16[2,16,2048]{2,1,0:T(8,128)(2,1)S(1)}, bf16[2,16,2048]{2,1,0:T(8,128)(2,1)S(1)}, u32[]{:S(2)}, u32[]{:S(2)}) collective-permute-start(bf16[2,16,2048]{2,1,0:T(8,128)(2,1)S(1)} %pad_maximum_fusion), channel_id=1, source_target_pairs={{0,4},{1,5},{2,6},{3,7},{4,0},{5,1},{6,2},{7,3},{8,12},{9,13},{10,... | collective-permute-start | bytes 393224 | tf_op jit(solution)/shard_map/ppermute | solution.py:298
  8.5 3.9 %collective-permute-done.1 = bf16[2,16,2048]{2,1,0:T(8,128)(2,1)S(1)} collective-permute-done((bf16[2,16,2048]{2,1,0:T(8,128)(2,1)S(1)}, bf16[2,16,2048]{2,1,0:T(8,128)(2,1)S(1)}, u32[]{:S(2)}, u32[]{:S(2)}) %collective-permute-start.1) | collective-permute-done | bytes 131104 | tf_op jit(solution)/shard_map/ppermute | solution.py:298
  12.6 1.8 %collective-permute-done.3 = bf16[2,64,2048]{2,1,0:T(8,128)(2,1)S(1)} collective-permute-done((bf16[2,64,2048]{2,1,0:T(8,128)(2,1)S(1)}, bf16[2,64,2048]{2,1,0:T(8,128)(2,1)S(1)}, u32[]{:S(2)}, u32[]{:S(2)}) %collective-permute-start.3) | collective-permute-done | bytes 524320 | tf_op jit(solution)/shard_map/ppermute | solution.py:301
  14.4 3.0 %forward.9 = (f32[2,128,512]{2,1,0:T(8,128)S(1)}, bf16[2,128,512]{2,1,0:T(8,128)(2,1)S(1)}) custom-call(bf16[2,128,2048]{2,1,0:T(8,128)(2,1)S(1)} %constant_dynamic-update-slice_fusion.pair_ref.refs_8_.refs_10_.cot_ref, bf16[2048,4096]{1,0:T(8,128)(2,1)} %refs_5_.9, bf16[4096,2048]{1,0:T(8,128)(2,1)} %down_ref.9, f32[16,4096]{1,0:T(8,128)S(1)} %bitcast.10, ...), custom_call_target="tpu_custom_call" | custom-call | flops 536870912 | bytes 5242880 | tf_op jit(solution)/shard_map/forward/pallas_call | solution.py:90
  17.4 3.5 %collective-permute-start.16 = (bf16[2,128,512]{2,1,0:T(8,128)(2,1)S(1)}, bf16[2,128,512]{2,1,0:T(8,128)(2,1)S(1)}, u32[]{:S(2)}, u32[]{:S(2)}) collective-permute-start(bf16[2,128,512]{2,1,0:T(8,128)(2,1)S(1)} %get-tuple-element.50), channel_id=1, source_target_pairs={{0,8},{24,16},{1,9},{25,17},{2,10},{26,18},{3,11},{27,19},{4,12},{... | collective-permute-start | bytes 786440 | tf_op jit(solution)/shard_map/ppermute | solution.py:316
  20.9 5.4 %forward.8 = (f32[2,128,1024]{2,1,0:T(8,128)S(1)}, bf16[2,128,1024]{2,1,0:T(8,128)(2,1)S(1)}) custom-call(bf16[2,128,2048]{2,1,0:T(8,128)(2,1)S(1)} %constant_dynamic-update-slice_fusion.pair_ref.refs_8_.refs_10_.cot_ref, bf16[2048,4096]{1,0:T(8,128)(2,1)} %refs_5_.9, bf16[4096,2048]{1,0:T(8,128)(2,1)} %down_ref.9, f32[16,4096]{1,0:T(8,128)S(1)} %bitcast.11, ...), custom_call_target="tpu_custom_call" | custom-call | flops 1073741824 | bytes 9437184 | tf_op jit(solution)/shard_map/forward/pallas_call | solution.py:90
  26.3 1.3 collective-permute-start.13
  27.6 3.0 %forward.5 = (f32[2,128,512]{2,1,0:T(8,128)S(1)}, bf16[2,128,512]{2,1,0:T(8,128)(2,1)S(1)}) custom-call(bf16[2,128,2048]{2,1,0:T(8,128)(2,1)S(1)} %constant_dynamic-update-slice_fusion.pair_ref.refs_8_.refs_10_.cot_ref, bf16[2048,4096]{1,0:T(8,128)(2,1)} %refs_5_.9, bf16[4096,2048]{1,0:T(8,128)(2,1)} %down_ref.9, f32[16,4096]{1,0:T(8,128)S(1)} %bitcast.12, ...), custom_call_target="tpu_custom_call" | custom-call | flops 536870912 | bytes 5242880 | tf_op jit(solution)/shard_map/forward/pallas_call | solution.py:90
  30.6 1.3 collective-permute-start.4
  31.9 5.4 %forward.7 = (f32[2,128,1024]{2,1,0:T(8,128)S(1)}, bf16[2,128,1024]{2,1,0:T(8,128)(2,1)S(1)}) custom-call(bf16[2,128,2048]{2,1,0:T(8,128)(2,1)S(1)} %constant_dynamic-update-slice_fusion.pair_ref.refs_8_.refs_10_.cot_ref, bf16[2048,4096]{1,0:T(8,128)(2,1)} %refs_5_.9, bf16[4096,2048]{1,0:T(8,128)(2,1)} %down_ref.9, f32[16,4096]{1,0:T(8,128)S(1)} %bitcast.13, ...), custom_call_target="tpu_custom_call" | custom-call | flops 1073741824 | bytes 9437184 | tf_op jit(solution)/shard_map/forward/pallas_call | solution.py:90
  37.3 5.4 %forward.6 = (f32[2,128,1024]{2,1,0:T(8,128)S(1)}, bf16[2,128,1024]{2,1,0:T(8,128)(2,1)S(1)}) custom-call(bf16[2,128,2048]{2,1,0:T(8,128)(2,1)S(1)} %constant_dynamic-update-slice_fusion.pair_ref.refs_8_.refs_10_.cot_ref, bf16[2048,4096]{1,0:T(8,128)(2,1)} %refs_5_.9, bf16[4096,2048]{1,0:T(8,128)(2,1)} %down_ref.9, f32[16,4096]{1,0:T(8,128)S(1)} %bitcast.14, ...), custom_call_target="tpu_custom_call" | custom-call | flops 1073741824 | bytes 9437184 | tf_op jit(solution)/shard_map/forward/pallas_call | solution.py:90
  42.8 1.3 collective-permute-start.10
  44.2 1.3 collective-permute-start.7
  47.9 8.5 %collective-permute-done.10.refs_2_ = bf16[2,128,1024]{2,1,0:T(8,128)(2,1)S(1)} collective-permute-done((bf16[2,128,1024]{2,1,0:T(8,128)(2,1)S(1)}, bf16[2,128,1024]{2,1,0:T(8,128)(2,1)S(1)}, u32[]{:S(2)}, u32[]{:S(2)}) %collective-permute-start.10) | collective-permute-done | bytes 524320 | tf_op jit(solution)/shard_map/ppermute | solution.py:316
  57.3 9.8 %collective-permute-done.7.refs_2_ = bf16[2,128,1024]{2,1,0:T(8,128)(2,1)S(1)} collective-permute-done((bf16[2,128,1024]{2,1,0:T(8,128)(2,1)S(1)}, bf16[2,128,1024]{2,1,0:T(8,128)(2,1)S(1)}, u32[]{:S(2)}, u32[]{:S(2)}) %collective-permute-start.7) | collective-permute-done | bytes 524320 | tf_op jit(solution)/shard_map/ppermute | solution.py:316
  68.1 1.3 collective-permute-start.18
  69.5 1.3 collective-permute-start.15
  71.0 1.3 collective-permute-start.12
  73.9 1.5 %collective-permute-start.6 = (bf16[2,128,512]{2,1,0:T(8,128)(2,1)S(1)}, bf16[2,128,512]{2,1,0:T(8,128)(2,1)S(1)}, u32[]{:S(2)}, u32[]{:S(2)}) collective-permute-start(bf16[2,128,512]{2,1,0:T(8,128)(2,1)S(1)} %add_convert_fusion.8), channel_id=1, source_target_pairs={{8,0},{16,24},{9,1},{17,25},{10,2},{18,26},{11,3},{19,27},{12,4},{... | collective-permute-start | bytes 786440 | tf_op jit(solution)/shard_map/ppermute | solution.py:316
  75.3 6.4 %collective-permute-done.18.refs_4_ = bf16[2,128,512]{2,1,0:T(8,128)(2,1)S(1)} collective-permute-done((bf16[2,128,512]{2,1,0:T(8,128)(2,1)S(1)}, bf16[2,128,512]{2,1,0:T(8,128)(2,1)S(1)}, u32[]{:S(2)}, u32[]{:S(2)}) %collective-permute-start.18) | collective-permute-done | bytes 262176 | tf_op jit(solution)/shard_map/ppermute | solution.py:316
  81.8 4.6 %chunk.5 = (f32[64,2048]{1,0:T(8,128)S(1)}, f32[64,2048]{1,0:T(8,128)S(1)}, bf16[2048,4096]{1,0:T(8,128)(2,1)}, bf16[4096,2048]{1,0:T(8,128)(2,1)}) custom-call(f32[2]{0:T(128)S(1)} %add_convert_fusion.10.refs_0_, f32[2,128,512]{2,1,0:T(8,128)S(1)} %get-tuple-element.49.refs_1_, bf16[2,128,512]{2,1,0:T(8,128)(2,1)S(1)} %collective-permute-done.16.refs_2_, ...), custom_call_target="tpu_custom_call" | custom-call | flops 805306368 | bytes 8388608 | tf_op jit(solution)/shard_map/chunk/pallas_call | solution.py:191
  86.4 6.6 %collective-permute-done.15.refs_4_ = bf16[2,128,1024]{2,1,0:T(8,128)(2,1)S(1)} collective-permute-done((bf16[2,128,1024]{2,1,0:T(8,128)(2,1)S(1)}, bf16[2,128,1024]{2,1,0:T(8,128)(2,1)S(1)}, u32[]{:S(2)}, u32[]{:S(2)}) %collective-permute-start.15) | collective-permute-done | bytes 524320 | tf_op jit(solution)/shard_map/ppermute | solution.py:316
  93.0 7.8 %chunk.6 = (f32[64,2048]{1,0:T(8,128)S(1)}, f32[64,2048]{1,0:T(8,128)S(1)}, bf16[2048,4096]{1,0:T(8,128)(2,1)}, bf16[4096,2048]{1,0:T(8,128)(2,1)}) custom-call(f32[2]{0:T(128)S(1)} %add_convert_fusion.10.refs_0_, f32[2,128,1024]{2,1,0:T(8,128)S(1)} %get-tuple-element.47.refs_1_, ...), custom_call_target="tpu_custom_call", output_to_operand_aliasing={{2}: (12, {}), {3}: (13, {})} | custom-call | flops 1610612736 | bytes 14680064 | tf_op jit(solution)/shard_map/chunk/pallas_call | solution.py:191
  100.8 3.5 %collective-permute-done.12.refs_4_ = bf16[2,128,1024]{2,1,0:T(8,128)(2,1)S(1)} collective-permute-done((bf16[2,128,1024]{2,1,0:T(8,128)(2,1)S(1)}, bf16[2,128,1024]{2,1,0:T(8,128)(2,1)S(1)}, u32[]{:S(2)}, u32[]{:S(2)}) %collective-permute-start.12) | collective-permute-done | bytes 524320 | tf_op jit(solution)/shard_map/ppermute | solution.py:316
  104.2 7.8 %chunk.7 = (f32[64,2048]{1,0:T(8,128)S(1)}, f32[64,2048]{1,0:T(8,128)S(1)}, bf16[2048,4096]{1,0:T(8,128)(2,1)}, bf16[4096,2048]{1,0:T(8,128)(2,1)}) custom-call(f32[2]{0:T(128)S(1)} %add_convert_fusion.10.refs_0_, f32[2,128,1024]{2,1,0:T(8,128)S(1)} %get-tuple-element.45.refs_1_, ...), custom_call_target="tpu_custom_call", output_to_operand_aliasing={{2}: (12, {}), {3}: (13, {})} | custom-call | flops 1610612736 | bytes 14680064 | tf_op jit(solution)/shard_map/chunk/pallas_call | solution.py:191
  112.0 3.5 %collective-permute-done.9.refs_4_ = bf16[2,128,1024]{2,1,0:T(8,128)(2,1)S(1)} collective-permute-done((bf16[2,128,1024]{2,1,0:T(8,128)(2,1)S(1)}, bf16[2,128,1024]{2,1,0:T(8,128)(2,1)S(1)}, u32[]{:S(2)}, u32[]{:S(2)}) %collective-permute-start.9) | collective-permute-done | bytes 524320 | tf_op jit(solution)/shard_map/ppermute | solution.py:316
  115.5 7.8 %chunk.8 = (f32[64,2048]{1,0:T(8,128)S(1)}, f32[64,2048]{1,0:T(8,128)S(1)}, bf16[2048,4096]{1,0:T(8,128)(2,1)}, bf16[4096,2048]{1,0:T(8,128)(2,1)}) custom-call(f32[2]{0:T(128)S(1)} %add_convert_fusion.10.refs_0_, f32[2,128,1024]{2,1,0:T(8,128)S(1)} %get-tuple-element.43.refs_1_, ...), custom_call_target="tpu_custom_call", output_to_operand_aliasing={{2}: (12, {}), {3}: (13, {})} | custom-call | flops 1610612736 | bytes 14680064 | tf_op jit(solution)/shard_map/chunk/pallas_call | solution.py:191
  123.3 2.5 %chunk.9 = (f32[64,2048]{1,0:T(8,128)S(1)}, f32[64,2048]{1,0:T(8,128)S(1)}, bf16[128,512]{1,0:T(8,128)(2,1)S(1)}, bf16[128,512]{1,0:T(8,128)(2,1)S(1)}) custom-call(f32[2]{0:T(128)S(1)} %add_convert_fusion.10.refs_0_, f32[2,128,512]{2,1,0:T(8,128)S(1)} %get-tuple-element.41.refs_1_, bf16[2,128,512]{2,1,0:T(8,128)(2,1)S(1)} %collective-permute-done.4.refs_2_, ...), custom_call_target="tpu_custom_call" | custom-call | flops 268435456 | bytes 4194304 | tf_op jit(solution)/shard_map/chunk/pallas_call | solution.py:191
  125.8 1.9 %collective-permute-done.19 = f32[64,2048]{1,0:T(8,128)S(1)} collective-permute-done((f32[64,2048]{1,0:T(8,128)S(1)}, f32[64,2048]{1,0:T(8,128)S(1)}, u32[]{:S(2)}, u32[]{:S(2)}) %collective-permute-start.19) | collective-permute-done | bytes 524320 | tf_op jit(solution)/shard_map/ppermute | solution.py:305
  129.9 1.4 %collective-permute-start.22 = (bf16[16,2048]{1,0:T(8,128)(2,1)S(1)}, bf16[16,2048]{1,0:T(8,128)(2,1)S(1)}, u32[]{:S(2)}, u32[]{:S(2)}) collective-permute-start(bf16[16,2048]{1,0:T(8,128)(2,1)S(1)} %get-tuple-element.76), channel_id=1, source_target_pairs={{0,6},{1,7},{2,4},{3,5},{4,2},{5,3},{6,0},{7,1},{8,14},{9,15},{10,... | collective-permute-start | bytes 196616 | tf_op jit(solution)/shard_map/ppermute | solution.py:310
  131.4 2.8 %weight_grads.1 = (bf16[2048,4096]{1,0:T(8,128)(2,1)}, bf16[4096,2048]{1,0:T(8,128)(2,1)}) custom-call(bf16[2048,128]{1,0:T(8,128)(2,1)S(1)} %transposed.1.refs_7_.refs_9_.tokt_ref, bf16[2,128,2048]{2,1,0:T(8,128)(2,1)S(1)} %constant_dynamic-update-slice_fusion.pair_ref.refs_8_.refs_10_.cot_ref, ...), custom_call_target="tpu_custom_call", output_to_operand_aliasing={{0}: (6, {}), {1}: (7, {})} | custom-call | flops 536870912 | bytes 5242880 | tf_op jit(solution)/shard_map/weight_grads/pallas_call | solution.py:258
  (60 shorter events, 13.5 us)
Async XLA Ops:
  0.6 5.5 %copy-start = (s32[64,96]{1,0:T(8,128)S(1)}, s32[64,96]{1,0:T(8,128)}, u32[]{:S(2)}) copy-start(s32[64,96]{1,0:T(8,128)} %param.9) | copy-start | bytes 73732
  1.5 6.9 %collective-permute-start = (bf16[2,16,2048]{2,1,0:T(8,128)(2,1)S(1)}, bf16[2,16,2048]{2,1,0:T(8,128)(2,1)S(1)}, u32[]{:S(2)}, u32[]{:S(2)}) collective-permute-start(bf16[2,16,2048]{2,1,0:T(8,128)(2,1)S(1)} %pad_maximum_fusion), channel_id=1, source_target_pairs={{0,2},{1,3},{2,0},{3,1},{4,6},{5,7},{6,4},{7,5},{8,10},{9,11},{10,... | collective-permute-start | bytes 393224 | tf_op jit(solution)/shard_map/ppermute | solution.py:298
  4.6 7.8 %collective-permute-start.1 = (bf16[2,16,2048]{2,1,0:T(8,128)(2,1)S(1)}, bf16[2,16,2048]{2,1,0:T(8,128)(2,1)S(1)}, u32[]{:S(2)}, u32[]{:S(2)}) collective-permute-start(bf16[2,16,2048]{2,1,0:T(8,128)(2,1)S(1)} %pad_maximum_fusion), channel_id=1, source_target_pairs={{0,4},{1,5},{2,6},{3,7},{4,0},{5,1},{6,2},{7,3},{8,12},{9,13},{10,... | collective-permute-start | bytes 393224 | tf_op jit(solution)/shard_map/ppermute | solution.py:298
  6.1 6.3 %collective-permute-start.2 = (bf16[2,16,2048]{2,1,0:T(8,128)(2,1)S(1)}, bf16[2,16,2048]{2,1,0:T(8,128)(2,1)S(1)}, u32[]{:S(2)}, u32[]{:S(2)}) collective-permute-start(bf16[2,16,2048]{2,1,0:T(8,128)(2,1)S(1)} %pad_maximum_fusion), channel_id=1, source_target_pairs={{0,6},{1,7},{2,4},{3,5},{4,2},{5,3},{6,0},{7,1},{8,14},{9,15},{10,... | collective-permute-start | bytes 393224 | tf_op jit(solution)/shard_map/ppermute | solution.py:298
  12.4 2.0 %collective-permute-start.3 = (bf16[2,64,2048]{2,1,0:T(8,128)(2,1)S(1)}, bf16[2,64,2048]{2,1,0:T(8,128)(2,1)S(1)}, u32[]{:S(2)}, u32[]{:S(2)}) collective-permute-start(bf16[2,64,2048]{2,1,0:T(8,128)(2,1)S(1)} %constant_dynamic-update-slice_fusion.2), channel_id=1, source_target_pairs={{0,1},{1,0},{2,3},{3,2},{4,5},{5,4},{6,7},{7,6},{8,9},{9,8},{10,11... | collective-permute-start | bytes 1572872 | tf_op jit(solution)/shard_map/ppermute | solution.py:301
  17.4 28.1 %collective-permute-start.16 = (bf16[2,128,512]{2,1,0:T(8,128)(2,1)S(1)}, bf16[2,128,512]{2,1,0:T(8,128)(2,1)S(1)}, u32[]{:S(2)}, u32[]{:S(2)}) collective-permute-start(bf16[2,128,512]{2,1,0:T(8,128)(2,1)S(1)} %get-tuple-element.50), channel_id=1, source_target_pairs={{0,8},{24,16},{1,9},{25,17},{2,10},{26,18},{3,11},{27,19},{4,12},{... | collective-permute-start | bytes 786440 | tf_op jit(solution)/shard_map/ppermute | solution.py:316
  26.3 20.8 %collective-permute-start.13 = (bf16[2,128,1024]{2,1,0:T(8,128)(2,1)S(1)}, bf16[2,128,1024]{2,1,0:T(8,128)(2,1)S(1)}, u32[]{:S(2)}, u32[]{:S(2)}) collective-permute-start(bf16[2,128,1024]{2,1,0:T(8,128)(2,1)S(1)} %get-tuple-element.48), channel_id=1, source_target_pairs={{0,8},{24,16},{1,9},{25,17},{2,10},{26,18},{3,11},{27,19},{4,12},{... | collective-permute-start | bytes 1572872 | tf_op jit(solution)/shard_map/ppermute | solution.py:316
  30.6 15.7 %collective-permute-start.4 = (bf16[2,128,512]{2,1,0:T(8,128)(2,1)S(1)}, bf16[2,128,512]{2,1,0:T(8,128)(2,1)S(1)}, u32[]{:S(2)}, u32[]{:S(2)}) collective-permute-start(bf16[2,128,512]{2,1,0:T(8,128)(2,1)S(1)} %get-tuple-element.42), channel_id=1, source_target_pairs={{0,8},{24,16},{1,9},{25,17},{2,10},{26,18},{3,11},{27,19},{4,12},{... | collective-permute-start | bytes 786440 | tf_op jit(solution)/shard_map/ppermute | solution.py:316
  42.8 13.6 %collective-permute-start.10 = (bf16[2,128,1024]{2,1,0:T(8,128)(2,1)S(1)}, bf16[2,128,1024]{2,1,0:T(8,128)(2,1)S(1)}, u32[]{:S(2)}, u32[]{:S(2)}) collective-permute-start(bf16[2,128,1024]{2,1,0:T(8,128)(2,1)S(1)} %get-tuple-element.46), channel_id=1, source_target_pairs={{0,8},{24,16},{1,9},{25,17},{2,10},{26,18},{3,11},{27,19},{4,12},{... | collective-permute-start | bytes 1572872 | tf_op jit(solution)/shard_map/ppermute | solution.py:316
  44.2 22.9 %collective-permute-start.7 = (bf16[2,128,1024]{2,1,0:T(8,128)(2,1)S(1)}, bf16[2,128,1024]{2,1,0:T(8,128)(2,1)S(1)}, u32[]{:S(2)}, u32[]{:S(2)}) collective-permute-start(bf16[2,128,1024]{2,1,0:T(8,128)(2,1)S(1)} %get-tuple-element.44), channel_id=1, source_target_pairs={{0,8},{24,16},{1,9},{25,17},{2,10},{26,18},{3,11},{27,19},{4,12},{... | collective-permute-start | bytes 1572872 | tf_op jit(solution)/shard_map/ppermute | solution.py:316
  45.6 22.4 %collective-permute-start.17 = (bf16[2,128,512]{2,1,0:T(8,128)(2,1)S(1)}, bf16[2,128,512]{2,1,0:T(8,128)(2,1)S(1)}, u32[]{:S(2)}, u32[]{:S(2)}) collective-permute-start(bf16[2,128,512]{2,1,0:T(8,128)(2,1)S(1)} %add_convert_fusion.7), channel_id=1, source_target_pairs={{8,16},{16,8},{9,17},{17,9},{10,18},{18,10},{11,19},{19,11},{12,20... | collective-permute-start | bytes 786440 | tf_op jit(solution)/shard_map/ppermute | solution.py:316
  46.4 27.4 %collective-permute-start.5 = (bf16[2,128,512]{2,1,0:T(8,128)(2,1)S(1)}, bf16[2,128,512]{2,1,0:T(8,128)(2,1)S(1)}, u32[]{:S(2)}, u32[]{:S(2)}) collective-permute-start(bf16[2,128,512]{2,1,0:T(8,128)(2,1)S(1)} %add_convert_fusion.9), channel_id=1, source_target_pairs={{8,16},{16,8},{9,17},{17,9},{10,18},{18,10},{11,19},{19,11},{12,20... | collective-permute-start | bytes 786440 | tf_op jit(solution)/shard_map/ppermute | solution.py:316
  47.2 22.1 %collective-permute-start.14 = (bf16[2,128,1024]{2,1,0:T(8,128)(2,1)S(1)}, bf16[2,128,1024]{2,1,0:T(8,128)(2,1)S(1)}, u32[]{:S(2)}, u32[]{:S(2)}) collective-permute-start(bf16[2,128,1024]{2,1,0:T(8,128)(2,1)S(1)} %add_convert_fusion.1), channel_id=1, source_target_pairs={{8,16},{16,8},{9,17},{17,9},{10,18},{18,10},{11,19},{19,11},{12,20... | collective-permute-start | bytes 1572872 | tf_op jit(solution)/shard_map/ppermute | solution.py:316
  56.6 14.2 %collective-permute-start.11 = (bf16[2,128,1024]{2,1,0:T(8,128)(2,1)S(1)}, bf16[2,128,1024]{2,1,0:T(8,128)(2,1)S(1)}, u32[]{:S(2)}, u32[]{:S(2)}) collective-permute-start(bf16[2,128,1024]{2,1,0:T(8,128)(2,1)S(1)} %add_convert_fusion.3), channel_id=1, source_target_pairs={{8,16},{16,8},{9,17},{17,9},{10,18},{18,10},{11,19},{19,11},{12,20... | collective-permute-start | bytes 1572872 | tf_op jit(solution)/shard_map/ppermute | solution.py:316
  67.3 5.0 %collective-permute-start.8 = (bf16[2,128,1024]{2,1,0:T(8,128)(2,1)S(1)}, bf16[2,128,1024]{2,1,0:T(8,128)(2,1)S(1)}, u32[]{:S(2)}, u32[]{:S(2)}) collective-permute-start(bf16[2,128,1024]{2,1,0:T(8,128)(2,1)S(1)} %add_convert_fusion.5), channel_id=1, source_target_pairs={{8,16},{16,8},{9,17},{17,9},{10,18},{18,10},{11,19},{19,11},{12,20... | collective-permute-start | bytes 1572872 | tf_op jit(solution)/shard_map/ppermute | solution.py:316
  68.1 13.7 %collective-permute-start.18 = (bf16[2,128,512]{2,1,0:T(8,128)(2,1)S(1)}, bf16[2,128,512]{2,1,0:T(8,128)(2,1)S(1)}, u32[]{:S(2)}, u32[]{:S(2)}) collective-permute-start(bf16[2,128,512]{2,1,0:T(8,128)(2,1)S(1)} %add_convert_fusion.6), channel_id=1, source_target_pairs={{8,0},{16,24},{9,1},{17,25},{10,2},{18,26},{11,3},{19,27},{12,4},{... | collective-permute-start | bytes 786440 | tf_op jit(solution)/shard_map/ppermute | solution.py:316
  69.5 23.5 %collective-permute-start.15 = (bf16[2,128,1024]{2,1,0:T(8,128)(2,1)S(1)}, bf16[2,128,1024]{2,1,0:T(8,128)(2,1)S(1)}, u32[]{:S(2)}, u32[]{:S(2)}) collective-permute-start(bf16[2,128,1024]{2,1,0:T(8,128)(2,1)S(1)} %add_convert_fusion), channel_id=1, source_target_pairs={{8,0},{16,24},{9,1},{17,25},{10,2},{18,26},{11,3},{19,27},{12,4},{... | collective-permute-start | bytes 1572872 | tf_op jit(solution)/shard_map/ppermute | solution.py:316
  71.0 33.2 %collective-permute-start.12 = (bf16[2,128,1024]{2,1,0:T(8,128)(2,1)S(1)}, bf16[2,128,1024]{2,1,0:T(8,128)(2,1)S(1)}, u32[]{:S(2)}, u32[]{:S(2)}) collective-permute-start(bf16[2,128,1024]{2,1,0:T(8,128)(2,1)S(1)} %add_convert_fusion.2), channel_id=1, source_target_pairs={{8,0},{16,24},{9,1},{17,25},{10,2},{18,26},{11,3},{19,27},{12,4},{... | collective-permute-start | bytes 1572872 | tf_op jit(solution)/shard_map/ppermute | solution.py:316
  72.5 43.0 %collective-permute-start.9 = (bf16[2,128,1024]{2,1,0:T(8,128)(2,1)S(1)}, bf16[2,128,1024]{2,1,0:T(8,128)(2,1)S(1)}, u32[]{:S(2)}, u32[]{:S(2)}) collective-permute-start(bf16[2,128,1024]{2,1,0:T(8,128)(2,1)S(1)} %add_convert_fusion.4), channel_id=1, source_target_pairs={{8,0},{16,24},{9,1},{17,25},{10,2},{18,26},{11,3},{19,27},{12,4},{... | collective-permute-start | bytes 1572872 | tf_op jit(solution)/shard_map/ppermute | solution.py:316
  73.9 49.4 %collective-permute-start.6 = (bf16[2,128,512]{2,1,0:T(8,128)(2,1)S(1)}, bf16[2,128,512]{2,1,0:T(8,128)(2,1)S(1)}, u32[]{:S(2)}, u32[]{:S(2)}) collective-permute-start(bf16[2,128,512]{2,1,0:T(8,128)(2,1)S(1)} %add_convert_fusion.8), channel_id=1, source_target_pairs={{8,0},{16,24},{9,1},{17,25},{10,2},{18,26},{11,3},{19,27},{12,4},{... | collective-permute-start | bytes 786440 | tf_op jit(solution)/shard_map/ppermute | solution.py:316
  125.8 2.0 %collective-permute-start.19 = (f32[64,2048]{1,0:T(8,128)S(1)}, f32[64,2048]{1,0:T(8,128)S(1)}, u32[]{:S(2)}, u32[]{:S(2)}) collective-permute-start(f32[64,2048]{1,0:T(8,128)S(1)} %get-tuple-element.66), channel_id=1, source_target_pairs={{0,1},{1,0},{2,3},{3,2},{4,5},{5,4},{6,7},{7,6},{8,9},{9,8},{10,11... | collective-permute-start | bytes 1572872 | tf_op jit(solution)/shard_map/ppermute | solution.py:305
  127.8 6.4 %collective-permute-start.20 = (bf16[16,2048]{1,0:T(8,128)(2,1)S(1)}, bf16[16,2048]{1,0:T(8,128)(2,1)S(1)}, u32[]{:S(2)}, u32[]{:S(2)}) collective-permute-start(bf16[16,2048]{1,0:T(8,128)(2,1)S(1)} %get-tuple-element.75), channel_id=1, source_target_pairs={{0,2},{1,3},{2,0},{3,1},{4,6},{5,7},{6,4},{7,5},{8,10},{9,11},{10,... | collective-permute-start | bytes 196616 | tf_op jit(solution)/shard_map/ppermute | solution.py:310
  129.1 5.1 %collective-permute-start.21 = (bf16[16,2048]{1,0:T(8,128)(2,1)S(1)}, bf16[16,2048]{1,0:T(8,128)(2,1)S(1)}, u32[]{:S(2)}, u32[]{:S(2)}) collective-permute-start(bf16[16,2048]{1,0:T(8,128)(2,1)S(1)} %get-tuple-element.77), channel_id=1, source_target_pairs={{0,4},{1,5},{2,6},{3,7},{4,0},{5,1},{6,2},{7,3},{8,12},{9,13},{10,... | collective-permute-start | bytes 196616 | tf_op jit(solution)/shard_map/ppermute | solution.py:310
  129.9 5.2 %collective-permute-start.22 = (bf16[16,2048]{1,0:T(8,128)(2,1)S(1)}, bf16[16,2048]{1,0:T(8,128)(2,1)S(1)}, u32[]{:S(2)}, u32[]{:S(2)}) collective-permute-start(bf16[16,2048]{1,0:T(8,128)(2,1)S(1)} %get-tuple-element.76), channel_id=1, source_target_pairs={{0,6},{1,7},{2,4},{3,5},{4,2},{5,3},{6,0},{7,1},{8,14},{9,15},{10,... | collective-permute-start | bytes 196616 | tf_op jit(solution)/shard_map/ppermute | solution.py:310
  131.4 4.4 %copy-start.1 = (s32[64,96]{1,0:T(8,128)S(1)}, s32[64,96]{1,0:T(8,128)}, u32[]{:S(2)}) copy-start(s32[64,96]{1,0:T(8,128)} %param.9) | copy-start | bytes 73732
